TPU v7x, 32 devices: a whole 2x2x4 slice. The times are simulated.
32 devices in a mesh: gx: 16 (over z, y, x), gy: 2 (over core).
Axes of the slice: x: 2, y: 2, z: 4, core: 2. Of those that a mesh axis runs over, the one named last changes fastest.
Arguments:
- scalars: bfloat16 [16, 2, 256, 2048], P('gx', 'gy'), may hold values from -6 to 6
- tensors: bfloat16 [16, 2, 9, 64, 2048], P('gx', 'gy'), may hold values from -6 to 6
- vectors: float32 [16, 2, 3, 2048], P('gx', 'gy'), may hold values from -1 to 1
- species: int32 [16, 2, 2048], P('gx', 'gy'), may hold values from 0 to 3
- species_table: float32 [256, 4], replicated, may hold values from -3 to 3
- reverse: int32 [16, 2, 2048], P('gx', 'gy'), may hold values from 0 to 2559, as said below
- send_index: int32 [16, 2, 8, 64], P('gx', 'gy'), may hold values from 0 to 2047, as said below
- counts: int32 [16, 2, 8], P('gx', 'gy'), may hold values from 32 to 64, as said below
- w_query: bfloat16 [256, 256], replicated, may hold values from -0.375 to 0.375
- w_key: bfloat16 [256, 256], replicated, may hold values from -0.375 to 0.375
- w_value: bfloat16 [256, 256], replicated, may hold values from -0.375 to 0.375
- w_output: bfloat16 [256, 256], replicated, may hold values from -0.375 to 0.375
- w_invariant: bfloat16 [256, 192], replicated, may hold values from -0.4375 to 0.4375
- w_message: bfloat16 [256, 256], replicated, may hold values from -0.375 to 0.375
- w_gate: bfloat16 [192, 256], replicated, may hold values from -0.375 to 0.375
- w_radial: bfloat16 [192, 256], replicated, may hold values from -0.375 to 0.375
- w_mixing: bfloat16 [64, 64], replicated, may hold values from -0.75 to 0.75
- w_expand: bfloat16 [512, 256], replicated, may hold values from -0.375 to 0.375
- w_reverse: bfloat16 [512, 256], replicated, may hold values from -0.375 to 0.375
- w_contract: bfloat16 [256, 512], replicated, may hold values from -0.25 to 0.25
Outputs:
- new_scalars: bfloat16 [16, 2, 256, 2048], P('gx', 'gy')
- new_tensors: bfloat16 [16, 2, 9, 64, 2048], P('gx', 'gy')
Inputs may be any that keep to these rules, and one draw needn't show every extreme that they name: counts[p] of a domain equals the count of its partner in direction p toward it (the opposite direction); some domain has 64 live slots toward some partner in every direction. `send_index`: live slots of a domain name distinct edges; slots at or above the count hold 0. The edge in live slot s of block p has as reverse slot s of the block received in the opposite direction; every live received slot is named by exactly one edge, no empty slot is named, and the other edges are paired among themselves (at most one edge of a domain is its own reverse).
All inputs are finite; a program needn't handle non-finite values.
Results may differ from a plain program's by a relative error of at most 0.01.
Values may be sent and summed in bfloat16 or wider, within the bound.
No kernel may reach another device: no remote copies, remote signals or barrier semaphores. Data moves between devices by JAX's collectives and lax.ppermute only.
A program may use at most 64 MiB of HBM per device.

v0:
```python
import math

import jax
import jax.numpy as jnp
from jax import lax
from jax.sharding import PartitionSpec as P

HEADS = 8


DIRECTIONS = ((1, 0), (-1, 0), (0, 1), (0, -1), (1, 1), (1, -1), (-1, 1), (-1, -1))


def passed_along(x, axis, by):
    devices = lax.axis_size(axis)
    return lax.ppermute(x, axis, [(i, (i + by) % devices) for i in range(devices)])


def solid_harmonics(vectors):
    xcoord, ycoord, zcoord = (vectors[0], vectors[1], vectors[2])
    radius_sq = xcoord * xcoord + ycoord * ycoord + zcoord * zcoord
    root_three = math.sqrt(3.0)
    return jnp.stack(
        [
            jnp.ones_like(xcoord),
            xcoord,
            ycoord,
            zcoord,
            root_three * xcoord * ycoord,
            root_three * ycoord * zcoord,
            0.5 * (3.0 * zcoord * zcoord - radius_sq),
            root_three * xcoord * zcoord,
            0.5 * root_three * (xcoord * xcoord - ycoord * ycoord),
        ]
    )


def by_degree(rows):
    multiplicity, edge_count = (rows.shape[1], rows.shape[2])
    return jnp.concatenate(
        [
            rows[0:1],
            jnp.broadcast_to(rows[1:2], (3, multiplicity, edge_count)),
            jnp.broadcast_to(rows[2:3], (5, multiplicity, edge_count)),
        ],
        axis=0,
    )


def send_blocks(scalars, tensors, send_index, counts):
    edge_count = scalars.shape[1]
    flatten = send_index.reshape(-1)
    picked = jnp.concatenate(
        [
            jnp.take(scalars, flatten, axis=1),
            jnp.take(tensors.reshape(-1, edge_count), flatten, axis=1),
        ],
        axis=0,
    )
    live_slots = (lax.broadcasted_iota(jnp.int32, send_index.shape, 1) < counts[:, None]).reshape(
        -1
    )
    return jnp.where(live_slots[None, :], picked, jnp.zeros_like(picked))


def deliver(pieces, heading):
    block_width = pieces[0].shape[1]
    arrived = list(pieces)
    for along_x in (1, -1):
        members = [
            position for position, (step_x, step_y) in enumerate(DIRECTIONS) if step_x == along_x
        ]
        shifted = passed_along(
            jnp.concatenate([arrived[position] for position in members], axis=1),
            "gx",
            heading * along_x,
        )
        for number, position in enumerate(members):
            arrived[position] = shifted[:, number * block_width : (number + 1) * block_width]
    for along_y in (1, -1):
        members = [
            position for position, (step_x, step_y) in enumerate(DIRECTIONS) if step_y == along_y
        ]
        shifted = passed_along(
            jnp.concatenate([arrived[position] for position in members], axis=1),
            "gy",
            heading * along_y,
        )
        for number, position in enumerate(members):
            arrived[position] = shifted[:, number * block_width : (number + 1) * block_width]
    return arrived


def edge_update(scalars, tensors, vectors, species, reverse, received, species_table, weights):
    w_query, w_key, w_value, w_output, w_invariant, w_message, w_gate, w_radial, w_mixing = weights
    channels, edge_count = scalars.shape
    multiplicity = tensors.shape[1]
    table_scalar = jnp.concatenate([scalars, received[:channels]], axis=1)
    table_tensor = jnp.concatenate(
        [tensors.reshape(9 * multiplicity, edge_count), received[channels:]], axis=1
    )
    scalar_rev = jnp.take(table_scalar, reverse, axis=1)
    tensor_rev = jnp.take(table_tensor, reverse, axis=1).reshape(9, multiplicity, edge_count)
    species_ids = lax.broadcasted_iota(jnp.int32, (species_table.shape[1], edge_count), 0)
    onehot = (species_ids == species[None, :]).astype(jnp.float32)
    embedding = jnp.sum(species_table[:, :, None] * onehot[None, :, :], axis=1)
    embedded = (scalars.astype(jnp.float32) + embedding).astype(jnp.bfloat16)
    queries = jnp.dot(w_query, embedded, preferred_element_type=jnp.float32)
    key_rows = jnp.dot(w_key, scalar_rev, preferred_element_type=jnp.float32)
    values = jnp.dot(w_value, scalar_rev, preferred_element_type=jnp.float32)
    head_size = channels // HEADS
    scores = jnp.sum(
        (queries * key_rows).reshape(HEADS, head_size, edge_count), axis=1
    ) / math.sqrt(head_size)
    attention = jax.nn.sigmoid(scores)
    attended = (
        (attention[:, None, :] * values.reshape(HEADS, head_size, edge_count))
        .reshape(channels, edge_count)
        .astype(jnp.bfloat16)
    )
    product = tensors.astype(jnp.float32) * tensor_rev.astype(jnp.float32)
    invariant = jnp.concatenate(
        [product[0], jnp.sum(product[1:4], axis=0), jnp.sum(product[4:9], axis=0)], axis=0
    ).astype(jnp.bfloat16)
    middle = (
        embedded.astype(jnp.float32)
        + jnp.dot(w_output, attended, preferred_element_type=jnp.float32)
        + jnp.dot(w_invariant, invariant, preferred_element_type=jnp.float32)
    ).astype(jnp.bfloat16)
    message = jnp.dot(w_message, middle, preferred_element_type=jnp.float32).astype(jnp.bfloat16)
    slot_count = received.shape[1]
    target = jnp.where(reverse >= edge_count, reverse - edge_count, slot_count)
    returned = (
        jnp.zeros((channels, slot_count), jnp.bfloat16).at[:, target].add(message, mode="drop")
    )
    tensor_gate = jax.nn.sigmoid(
        jnp.dot(w_gate, middle, preferred_element_type=jnp.float32)
    ).reshape(3, multiplicity, edge_count)
    radial = jnp.dot(w_radial, middle, preferred_element_type=jnp.float32).reshape(
        3, multiplicity, edge_count
    )
    mixed_rev = jnp.einsum("oi,cie->coe", w_mixing, tensor_rev, preferred_element_type=jnp.float32)
    harmonic = solid_harmonics(vectors)
    new_tensors = (
        tensors.astype(jnp.float32)
        + by_degree(tensor_gate) * mixed_rev
        + by_degree(radial) * harmonic[:, None, :]
    ).astype(jnp.bfloat16)
    return (middle, message, returned, new_tensors)


def finish(middle, message, reverse, send_index, counts, returns, w_expand, w_reverse, w_contract):
    channels, edge_count = middle.shape
    local_part = jnp.take(message, jnp.minimum(reverse, edge_count - 1), axis=1).astype(jnp.float32)
    local_part = jnp.where((reverse < edge_count)[None, :], local_part, jnp.float32(0.0))
    live_slots = (lax.broadcasted_iota(jnp.int32, send_index.shape, 1) < counts[:, None]).reshape(
        -1
    )
    arrived = jnp.where(live_slots[None, :], returns.astype(jnp.float32), jnp.float32(0.0))
    incoming = (
        local_part
        + jnp.zeros((channels, edge_count), jnp.float32).at[:, send_index.reshape(-1)].add(arrived)
    ).astype(jnp.bfloat16)
    hidden = jax.nn.silu(
        jnp.dot(w_expand, middle, preferred_element_type=jnp.float32)
        + jnp.dot(w_reverse, incoming, preferred_element_type=jnp.float32)
    ).astype(jnp.bfloat16)
    return (
        middle.astype(jnp.float32) + jnp.dot(w_contract, hidden, preferred_element_type=jnp.float32)
    ).astype(jnp.bfloat16)


def per_device(
    scalars,
    tensors,
    vectors,
    species,
    species_table,
    reverse,
    send_index,
    counts,
    w_query,
    w_key,
    w_value,
    w_output,
    w_invariant,
    w_message,
    w_gate,
    w_radial,
    w_mixing,
    w_expand,
    w_reverse,
    w_contract,
):
    scalars_here = scalars[0, 0]
    tensors_here = tensors[0, 0]
    reverse_here = reverse[0, 0]
    send_here = send_index[0, 0]
    counts_here = counts[0, 0]
    block_width = send_here.shape[-1]
    outgoing = send_blocks(scalars_here, tensors_here, send_here, counts_here)
    pieces = [
        outgoing[:, position * block_width : (position + 1) * block_width] for position in range(8)
    ]
    received = jnp.concatenate(deliver(pieces, 1), axis=1)
    weights = (
        w_query,
        w_key,
        w_value,
        w_output,
        w_invariant,
        w_message,
        w_gate,
        w_radial,
        w_mixing,
    )
    middle, message, returned, new_tensors = edge_update(
        scalars_here,
        tensors_here,
        vectors[0, 0],
        species[0, 0],
        reverse_here,
        received,
        species_table,
        weights,
    )
    answer_pieces = [
        returned[:, position * block_width : (position + 1) * block_width] for position in range(8)
    ]
    returns = jnp.concatenate(deliver(answer_pieces, -1), axis=1)
    result = finish(
        middle,
        message,
        reverse_here,
        send_here,
        counts_here,
        returns,
        w_expand,
        w_reverse,
        w_contract,
    )
    return (result[None, None], new_tensors[None, None])


def solution(mesh):
    return jax.shard_map(
        per_device,
        mesh=mesh,
        in_specs=(
            P("gx", "gy", None, None),
            P("gx", "gy", None, None, None),
            P("gx", "gy", None, None),
            P("gx", "gy", None),
            P(),
            P("gx", "gy", None),
            P("gx", "gy", None, None),
            P("gx", "gy", None),
            P(),
            P(),
            P(),
            P(),
            P(),
            P(),
            P(),
            P(),
            P(),
            P(),
            P(),
            P(),
        ),
        out_specs=(P("gx", "gy", None, None), P("gx", "gy", None, None, None)),
        check_vma=False,
    )
```

profile of v0, /device:TPU:0, one launch (start us, length us, event | category | flops | bytes accessed | tf_op | source)
XLA Modules:
  0.0 156.0 jit_solution(5250342391085845063)
XLA Ops:
  0.6 0.8 reshape_squeeze.11
  2.2 3.1 %copy.41 = bf16[576,2048]{0,1:T(8,128)(2,1)S(1)} copy(bf16[576,2048]{1,0:T(8,128)(2,1)} %bitcast.156) | data formatting | bytes 4718592 | tf_op jit(solution)/shard_map/reshape;squeeze | solution.py:56
  6.0 2.5 %copy.39 = bf16[1,1,256,2048]{2,3,1,0:T(8,128)(2,1)} copy(bf16[1,1,256,2048]{3,2,1,0:T(8,128)(2,1)} %param.20) | data formatting | bytes 2097152 | tf_op args[0]
  8.5 2.0 %gather_fusion.1 = bf16[512,576]{1,0:T(8,128)(2,1)S(1)} fusion(bf16[576,2048]{0,1:T(8,128)(2,1)S(1)} %copy.41, s32[1024]{0:T(1024)S(1)} %pad_clamp_fusion), kind=kCustom, calls=%fused_computation.1 | custom fusion | bytes 1181696 | tf_op jit(solution)/shard_map/jit(_take)/gather | solution.py:56
  10.5 2.9 %gather_fusion = bf16[512,256]{1,0:T(8,128)(2,1)S(1)} fusion(bf16[256,2048]{0,1:T(8,128)(2,1)} %bitcast.153, s32[1024]{0:T(1024)S(1)} %pad_clamp_fusion), kind=kCustom, calls=%fused_computation | custom fusion | bytes 526336 | tf_op jit(solution)/shard_map/jit(_take)/gather | solution.py:55
  16.3 7.0 %collective-permute-start.1 = (bf16[832,192]{0,1:T(8,128)(2,1)}, bf16[832,192]{0,1:T(8,128)(2,1)}, u32[]{:S(2)}, u32[]{:S(2)}) collective-permute-start(bf16[832,192]{0,1:T(8,128)(2,1)} %pad_maximum_fusion.3), channel_id=1, source_target_pairs={{0,30},{2,0},{4,2},{6,4},{8,6},{10,8},{12,10},{14,12},{16,14},{18,... | collective-permute-start | bytes 958472 | tf_op jit(solution)/shard_map/ppermute | solution.py:16
  23.2 0.8 pad_maximum_fusion.2
  25.9 2.0 %multiply_reduce_fusion = f32[256,2048]{1,0:T(8,128)} fusion(f32[4,2048]{1,0:T(4,128)S(1)} %fusion.36, f32[256,4]{0,1:T(4,128)S(1)} %copy-done.35), kind=kLoop, calls=%fused_computation.7 | loop fusion | flops 3670016 | bytes 2134016 | tf_op jit(solution)/shard_map/reduce_sum | solution.py:106
  27.9 2.0 %copy.40 = f32[256,2048]{0,1:T(8,128)S(1)} copy(f32[256,2048]{1,0:T(8,128)} %multiply_reduce_fusion) | data formatting | bytes 4194304 | tf_op jit(solution)/shard_map/reduce_sum | solution.py:106
  30.0 3.1 %fusion.46 = f32[2048,256]{0,1:T(8,128)} fusion(bf16[256,256]{1,0:T(8,128)(2,1)} %param.28, f32[256,2048]{0,1:T(8,128)S(1)} %copy.40, bf16[1,1,256,2048]{2,3,1,0:T(8,128)(2,1)S(1)} %copy-done.3), kind=kOutput, calls=%fused_computation.133 | convolution fusion | flops 270008320 | bytes 5373952 | tf_op jit(solution)/shard_map/dot_general | solution.py:108
  33.7 3.8 %collective-permute-done = bf16[832,192]{0,1:T(8,128)(2,1)} collective-permute-done((bf16[832,192]{0,1:T(8,128)(2,1)}, bf16[832,192]{0,1:T(8,128)(2,1)}, u32[]{:S(2)}, u32[]{:S(2)}) %collective-permute-start) | collective-permute-done | bytes 319520 | tf_op jit(solution)/shard_map/ppermute | solution.py:16
  37.4 1.0 fusion.49
  38.5 1.0 fusion.50
  40.3 0.8 pad_maximum_fusion.5
  42.2 2.1 %stack.2 = f32[9,2048]{1,0:T(8,128)} concatenate(f32[1,2048]{1,0:T(1,128)S(1)} %stack_broadcast_in_dim.3, f32[1,2048]{1,0:T(1,128)S(1)} %get-tuple-element.46, f32[1,2048]{1,0:T(1,128)S(1)} %copy-done.25, f32[1,2048]{1,0:T(1,128)S(1)} %get-tuple-element.45, f32[1,2048]{1,0:T(1,128)} %get-tuple-element.41, f32[1,2048]{1,0:T(1,128)} %get-tuple-element.42, ...), dimensions={0} | concatenate | bytes 147456 | tf_op jit(solution)/shard_map/stack | solution.py:23
  44.4 0.9 slice_dynamic-update-slice_fusion.5
  45.3 0.9 slice_dynamic-update-slice_fusion.4
  46.2 0.9 slice_dynamic-update-slice_fusion.3
  47.1 0.9 slice_dynamic-update-slice_fusion.2
  48.0 0.9 slice_dynamic-update-slice_fusion.1
  48.9 0.9 slice_dynamic-update-slice_fusion
  49.9 1.0 copy-done.14
  50.9 2.0 %pad_maximum_fusion = bf16[576,2560]{0,1:T(8,128)(2,1)S(1)} fusion(bf16[576,512]{0,1:T(8,128)(2,1)S(1)} %slice.262, bf16[576,2048]{0,1:T(8,128)(2,1)} %copy-done.2), kind=kLoop, calls=%fused_computation.20 | loop fusion | flops 5898240 | bytes 5898240 | tf_op jit(solution)/shard_map/concatenate | solution.py:99
  52.9 9.3 %gather_fusion.3 = bf16[2048,576]{1,0:T(8,128)(2,1)} fusion(bf16[576,2560]{0,1:T(8,128)(2,1)S(1)} %pad_maximum_fusion, s32[2048]{0:T(1024)S(1)} %get-tuple-element.55), kind=kCustom, calls=%fused_computation.3 | custom fusion | bytes 4726784 | tf_op jit(solution)/shard_map/jit(_take)/gather | solution.py:103
  62.3 4.5 %copy.44 = bf16[576,2048]{1,0:T(8,128)(2,1)} copy(bf16[576,2048]{0,1:T(8,128)(2,1)} %bitcast.155) | data formatting | bytes 4718592 | tf_op jit(solution)/shard_map/jit(_take)/gather | solution.py:103
  66.7 2.6 %convert_multiply_fusion = f32[9,64,2048]{2,1,0:T(8,128)S(1)} fusion(bf16[1,1,9,64,2048]{4,3,2,1,0:T(8,128)(2,1)S(1)} %copy-done.6, bf16[9,64,2048]{2,1,0:T(8,128)(2,1)} %bitcast.157, pred[2048]{0:T(1024)(128)(4,1)S(1)} %copy-done.30), kind=kLoop, calls=%fused_computation.9 | loop fusion | flops 4718592 | bytes 9439232 | tf_op jit(solution)/shard_map/mul | solution.py:121
  69.3 0.9 slice_reduce_fusion
  70.2 0.8 slice_reduce_fusion.1
  71.8 1.0 slice.261
  72.9 9.1 %gather_fusion.2 = bf16[2048,256]{1,0:T(8,128)(2,1)} fusion(bf16[256,2560]{0,1:T(8,128)(2,1)S(1)} %pad_maximum_fusion.1, s32[2048]{0:T(1024)S(1)} %get-tuple-element.55), kind=kCustom, calls=%fused_computation.2 | custom fusion | bytes 2105344 | tf_op jit(solution)/shard_map/jit(_take)/gather | solution.py:102
  81.9 2.6 %bitcast_reduce_fusion = f32[8,2048]{1,0:T(8,128)S(1)} fusion(f32[2048,256]{0,1:T(8,128)} %fusion.46, bf16[256,256]{1,0:T(8,128)(2,1)S(1)} %copy-done.19, bf16[2048,256]{1,0:T(8,128)(2,1)} %gather_fusion.2, pred[2048]{0:T(1024)(128)(4,1)S(1)} %copy-done.30), kind=kOutput, calls=%fused_computation.44 | convolution fusion | flops 269991936 | bytes 3344384 | tf_op jit(solution)/shard_map/dot_general | solution.py:109
  84.8 1.8 %copy.42 = f32[256,2048]{0,1:T(8,128)} copy(f32[256,2048]{1,0:T(8,128)S(1)} %bitcast.159) | data formatting | bytes 4194304 | tf_op jit(solution)/shard_map/mul | solution.py:117
  86.6 3.1 %convolution_bitcast_fusion = f32[256,2048]{0,1:T(8,128)} fusion(bf16[256,192]{0,1:T(8,128)(2,1)} %param.32, bf16[64,2048]{1,0:T(8,128)(2,1)} %slice_reduce_fusion, bf16[64,2048]{1,0:T(8,128)(2,1)} %slice_reduce_fusion.1, bf16[64,2048]{1,0:T(8,128)(2,1)} %fusion.31), kind=kOutput, calls=%fused_computation.22 | convolution fusion | flops 203685888 | bytes 2981888 | tf_op jit(solution)/shard_map/dot_general | solution.py:128
  89.7 3.8 %fusion.15 = bf16[256,2048]{0,1:T(8,128)(2,1)S(1)} fusion(f32[256,2048]{0,1:T(8,128)} %convolution_bitcast_fusion, bf16[256,256]{1,0:T(8,128)(2,1)S(1)} %copy-done.18, f32[256,2048]{0,1:T(8,128)} %copy.42, bf16[256,256]{1,0:T(8,128)(2,1)} %param.30, bf16[2048,256]{1,0:T(8,128)(2,1)S(1)} %copy-done.9, pred[2048]{0:T(1024)(128)(4,1)S(1)} %copy-done.30, ...), kind=kOutput, calls=%fused_computation.38 | convolution fusion | flops 542113792 | bytes 9701376 | tf_op jit(solution)/shard_map/dot_general | solution.py:127
  93.5 1.4 convolution_convert_fusion
  94.8 11.9 %scatter_custom_fusion = bf16[256,512]{0,1:T(8,128)(2,1)S(1)} fusion(s32[2048]{0:T(1024)} %bitcast.166, bf16[2048,256]{1,0:T(8,128)(2,1)S(1)} %convolution_convert_fusion, bf16[]{:T(256)} %constant.59.clone.1), kind=kCustom, calls=%fused_computation.74 | custom fusion | flops 524288 | bytes 262656 | tf_op jit(solution)/shard_map/scatter-add | solution.py:134
  107.4 2.7 %fusion.55 = f32[2048,512]{1,0:T(8,128)} fusion(bf16[256,2048]{0,1:T(8,128)(2,1)S(1)} %fusion.15, bf16[512,256]{1,0:T(8,128)(2,1)S(1)} %copy-done), kind=kOutput, calls=%fused_computation.142 | convolution fusion | flops 536870912 | bytes 5505024 | tf_op jit(solution)/shard_map/dot_general | solution.py:165
  110.1 3.5 %collective-permute-start.4 = (bf16[256,192]{0,1:T(8,128)(2,1)S(1)}, bf16[256,192]{0,1:T(8,128)(2,1)}, u32[]{:S(2)}, u32[]{:S(2)}) collective-permute-start(bf16[256,192]{0,1:T(8,128)(2,1)S(1)} %pad_maximum_fusion.6), channel_id=1, source_target_pairs={{0,30},{2,0},{4,2},{6,4},{8,6},{10,8},{12,10},{14,12},{16,14},{18,... | collective-permute-start | bytes 294920 | tf_op jit(solution)/shard_map/ppermute | solution.py:16
  114.1 1.2 slice_bitcast_fusion
  115.9 1.2 slice_bitcast_fusion.1
  117.2 7.5 %gather_fusion.4 = bf16[2048,256]{1,0:T(8,128)(2,1)S(1)} fusion(bf16[256,2048]{0,1:T(8,128)(2,1)S(1)} %bitcast.152, s32[2048]{0:T(1024)S(1)} %copy-done.29), kind=kCustom, calls=%fused_computation.4 | custom fusion | bytes 2105344 | tf_op jit(solution)/shard_map/jit(_take)/gather | solution.py:154
  124.7 2.7 %select_bitcast_fusion = f32[256,2048]{0,1:T(8,128)} fusion(bf16[2048,256]{1,0:T(8,128)(2,1)S(1)} %gather_fusion.4, pred[2048]{0:T(1024)(128)(4,1)S(1)} %copy-done.32, pred[2048]{0:T(1024)(128)(4,1)S(1)} %copy-done.31), kind=kLoop, calls=%fused_computation.45 | loop fusion | flops 1572864 | bytes 3149824 | tf_op jit(solution)/shard_map/jit(_where)/select_n | solution.py:155
  131.5 2.5 %fusion.6 = bf16[1,1,9,64,2048]{4,3,2,1,0:T(8,128)(2,1)} fusion(f32[5,64,2048]{2,1,0:T(8,128)S(1)} %broadcast_in_dim.145, f32[3,64,2048]{2,1,0:T(8,128)S(1)} %broadcast_in_dim.144, f32[1,64,2048]{2,1,0:T(8,128)S(1)} %copy-done.15, f32[5,64,2048]{2,1,0:T(8,128)S(1)} %broadcast_in_dim.143, f32[3,64,2048]{2,1,0:T(8,128)S(1)} %broadcast_in_dim.142, ...), kind=kOutput, calls=%fused_computation.21 | convolution fusion | flops 163971072 | bytes 16599040 | tf_op jit(solution)/shard_map/oi,cie->coe/dot_general | solution.py:142
  134.1 0.9 fusion.53
  134.9 7.3 %collective-permute-done.5 = bf16[256,192]{0,1:T(8,128)(2,1)S(1)} collective-permute-done((bf16[256,192]{0,1:T(8,128)(2,1)S(1)}, bf16[256,192]{0,1:T(8,128)(2,1)S(1)}, u32[]{:S(2)}, u32[]{:S(2)}) %collective-permute-start.5) | collective-permute-done | bytes 98336 | tf_op jit(solution)/shard_map/ppermute | solution.py:16
  143.9 6.2 %scatter_custom_fusion.1 = f32[256,2048]{0,1:T(8,128)} fusion(f32[256,2048]{0,1:T(8,128)} %select_bitcast_fusion, s32[512]{0:T(512)} %bitcast.165, bf16[256,512]{0,1:T(8,128)(2,1)S(1)} %slice_dynamic-update-slice_fusion.8, f32[]{:T(128)} %constant.45.clone.1, pred[512]{0:T(512)(128)(4,1)S(1)} %copy-done.37), kind=kCustom, calls=%fused_computation.62 | custom fusion | flops 393216 | bytes 2360320 | tf_op jit(solution)/shard_map/scatter-add | solution.py:162
  150.2 4.4 %fusion.18 = bf16[1,1,256,2048]{2,3,1,0:T(8,128)(2,1)S(1)} fusion(bf16[256,512]{1,0:T(8,128)(2,1)S(1)} %copy-done.38, bf16[256,2048]{0,1:T(8,128)(2,1)S(1)} %fusion.15, f32[2048,512]{1,0:T(8,128)} %fusion.55, bf16[512,256]{1,0:T(8,128)(2,1)S(1)} %copy-done.39, f32[256,2048]{0,1:T(8,128)} %scatter_custom_fusion.1), kind=kOutput, calls=%fused_computation.42 | convolution fusion | flops 1082130432 | bytes 8912896 | tf_op jit(solution)/shard_map/dot_general | solution.py:169
  154.6 1.4 copy.45
  (141 shorter events, 17.1 us)
Async XLA Ops:
  0.6 106.7 %copy-start = (bf16[512,256]{1,0:T(8,128)(2,1)S(1)}, bf16[512,256]{1,0:T(8,128)(2,1)}, u32[]{:S(2)}) copy-start(bf16[512,256]{1,0:T(8,128)(2,1)} %param.37) | copy-start | bytes 786436
  5.3 5.2 %copy-start.2 = (bf16[576,2048]{0,1:T(8,128)(2,1)}, bf16[576,2048]{0,1:T(8,128)(2,1)S(1)}, u32[]{:S(2)}) copy-start(bf16[576,2048]{0,1:T(8,128)(2,1)S(1)} %copy.41) | copy-start | bytes 7077892
  10.5 3.3 %copy-start.42 = (s32[1,1,8]{2,1,0:T(1,128)S(1)}, s32[1,1,8]{2,1,0:T(1,128)}, u32[]{:S(2)}) copy-start(s32[1,1,8]{2,1,0:T(1,128)} %param.27) | copy-start | bytes 100
  14.5 9.5 %copy-start.22 = (f32[1,1,3,2048]{3,1,2,0:T(1,128)S(1)}, f32[1,1,3,2048]{3,1,2,0:T(1,128)}, u32[]{:S(2)}) copy-start(f32[1,1,3,2048]{3,1,2,0:T(1,128)} %param.22) | copy-start | bytes 73732
  14.7 10.5 %copy-start.24 = (s32[1,1,2048]{2,1,0:T(1,128)S(1)}, s32[1,1,2048]{2,1,0:T(1,128)}, u32[]{:S(2)}) copy-start(s32[1,1,2048]{2,1,0:T(1,128)} %param.25) | copy-start | bytes 24580
  14.8 11.2 %copy-start.33 = (s32[1,1,2048]{2,1,0:T(1,128)S(1)}, s32[1,1,2048]{2,1,0:T(1,128)}, u32[]{:S(2)}) copy-start(s32[1,1,2048]{2,1,0:T(1,128)} %param.23) | copy-start | bytes 24580
  14.8 11.2 %copy-start.35 = (f32[256,4]{0,1:T(4,128)S(1)}, f32[256,4]{0,1:T(4,128)}, u32[]{:S(2)}) copy-start(f32[256,4]{0,1:T(4,128)} %param.24) | copy-start | bytes 12292
  16.3 22.2 %collective-permute-start.1 = (bf16[832,192]{0,1:T(8,128)(2,1)}, bf16[832,192]{0,1:T(8,128)(2,1)}, u32[]{:S(2)}, u32[]{:S(2)}) collective-permute-start(bf16[832,192]{0,1:T(8,128)(2,1)} %pad_maximum_fusion.3), channel_id=1, source_target_pairs={{0,30},{2,0},{4,2},{6,4},{8,6},{10,8},{12,10},{14,12},{16,14},{18,... | collective-permute-start | bytes 958472 | tf_op jit(solution)/shard_map/ppermute | solution.py:16
  24.0 13.4 %collective-permute-start = (bf16[832,192]{0,1:T(8,128)(2,1)}, bf16[832,192]{0,1:T(8,128)(2,1)}, u32[]{:S(2)}, u32[]{:S(2)}) collective-permute-start(bf16[832,192]{0,1:T(8,128)(2,1)} %pad_maximum_fusion.2), channel_id=1, source_target_pairs={{0,2},{2,4},{4,6},{6,8},{8,10},{10,12},{12,14},{14,16},{16,18},{18... | collective-permute-start | bytes 958472 | tf_op jit(solution)/shard_map/ppermute | solution.py:16
  27.9 2.0 %copy-start.3 = (bf16[1,1,256,2048]{2,3,1,0:T(8,128)(2,1)S(1)}, bf16[1,1,256,2048]{2,3,1,0:T(8,128)(2,1)}, u32[]{:S(2)}) copy-start(bf16[1,1,256,2048]{2,3,1,0:T(8,128)(2,1)} %copy.39) | copy-start | bytes 3145732
  29.9 19.9 %copy-start.5 = (f32[256,2048]{0,1:T(8,128)}, f32[256,2048]{0,1:T(8,128)S(1)}, u32[]{:S(2)}) copy-start(f32[256,2048]{0,1:T(8,128)S(1)} %copy.40) | copy-start | bytes 6291460
  30.0 3.1 %copy-start.27 = (s32[2048,1]{0,1:T(1,128)S(1)}, s32[2048,1]{0,1:T(1,128)}, u32[]{:S(2)}) copy-start(s32[2048,1]{0,1:T(1,128)} %get-tuple-element.49) | copy-start | bytes 24580
  30.0 3.1 %copy-start.28 = (s32[2048,1]{0,1:T(1,128)S(1)}, s32[2048,1]{0,1:T(1,128)}, u32[]{:S(2)}) copy-start(s32[2048,1]{0,1:T(1,128)} %get-tuple-element.50) | copy-start | bytes 24580
  30.0 9.6 %copy-start.17 = (bf16[832,64]{0,1:T(8,128)(2,1)S(1)}, bf16[832,64]{0,1:T(8,128)(2,1)}, u32[]{:S(2)}) copy-start(bf16[832,64]{0,1:T(8,128)(2,1)} %get-tuple-element.17) | copy-start | bytes 319492
  33.0 9.2 %copy-start.25 = (f32[1,2048]{1,0:T(1,128)S(1)}, f32[1,2048]{1,0:T(1,128)}, u32[]{:S(2)}) copy-start(f32[1,2048]{1,0:T(1,128)} %get-tuple-element.47) | copy-start | bytes 24580
  33.0 9.2 %copy-start.26 = (f32[1,2048]{1,0:T(1,128)S(1)}, f32[1,2048]{1,0:T(1,128)}, u32[]{:S(2)}) copy-start(f32[1,2048]{1,0:T(1,128)} %get-tuple-element.40) | copy-start | bytes 24580
  40.3 4.0 %collective-permute-start.2 = (bf16[832,192]{0,1:T(8,128)(2,1)}, bf16[832,192]{0,1:T(8,128)(2,1)}, u32[]{:S(2)}, u32[]{:S(2)}) collective-permute-start(bf16[832,192]{0,1:T(8,128)(2,1)} %pad_maximum_fusion.4), channel_id=1, source_target_pairs={{0,1},{1,0},{2,3},{3,2},{4,5},{5,4},{6,7},{7,6},{8,9},{9,8},{10,11... | collective-permute-start | bytes 958472 | tf_op jit(solution)/shard_map/ppermute | solution.py:16
  41.1 4.2 %collective-permute-start.3 = (bf16[832,192]{0,1:T(8,128)(2,1)}, bf16[832,192]{0,1:T(8,128)(2,1)}, u32[]{:S(2)}, u32[]{:S(2)}) collective-permute-start(bf16[832,192]{0,1:T(8,128)(2,1)} %pad_maximum_fusion.5), channel_id=1, source_target_pairs={{0,1},{1,0},{2,3},{3,2},{4,5},{5,4},{6,7},{7,6},{8,9},{9,8},{10,11... | collective-permute-start | bytes 958472 | tf_op jit(solution)/shard_map/ppermute | solution.py:16
  62.3 4.5 %copy-start.6 = (bf16[1,1,9,64,2048]{4,3,2,1,0:T(8,128)(2,1)S(1)}, bf16[1,1,9,64,2048]{4,3,2,1,0:T(8,128)(2,1)}, u32[]{:S(2)}) copy-start(bf16[1,1,9,64,2048]{4,3,2,1,0:T(8,128)(2,1)} %param.21) | copy-start | bytes 7077892
  62.3 4.5 %copy-start.30 = (pred[2048]{0:T(1024)(128)(4,1)S(1)}, pred[2048]{0:T(1024)(128)(4,1)}, u32[]{:S(2)}) copy-start(pred[2048]{0:T(1024)(128)(4,1)} %get-tuple-element.52) | copy-start | bytes 6148
  70.2 2.5 %copy-start.4 = (bf16[1,1,256,2048]{2,3,1,0:T(8,128)(2,1)S(1)}, bf16[1,1,256,2048]{2,3,1,0:T(8,128)(2,1)}, u32[]{:S(2)}) copy-start(bf16[1,1,256,2048]{2,3,1,0:T(8,128)(2,1)} %copy.39) | copy-start | bytes 3145732
  72.9 9.1 %copy-start.19 = (bf16[256,256]{1,0:T(8,128)(2,1)S(1)}, bf16[256,256]{1,0:T(8,128)(2,1)}, u32[]{:S(2)}) copy-start(bf16[256,256]{1,0:T(8,128)(2,1)} %param.29) | copy-start | bytes 393220
  86.6 3.1 %copy-start.9 = (bf16[2048,256]{1,0:T(8,128)(2,1)S(1)}, bf16[2048,256]{1,0:T(8,128)(2,1)}, u32[]{:S(2)}) copy-start(bf16[2048,256]{1,0:T(8,128)(2,1)} %gather_fusion.2) | copy-start | bytes 3145732
  86.6 3.1 %copy-start.18 = (bf16[256,256]{1,0:T(8,128)(2,1)S(1)}, bf16[256,256]{1,0:T(8,128)(2,1)}, u32[]{:S(2)}) copy-start(bf16[256,256]{1,0:T(8,128)(2,1)} %param.31) | copy-start | bytes 393220
  107.4 6.2 %copy-start.23 = (bf16[192,256]{1,0:T(8,128)(2,1)S(1)}, bf16[192,256]{1,0:T(8,128)(2,1)}, u32[]{:S(2)}) copy-start(bf16[192,256]{1,0:T(8,128)(2,1)} %param.35) | copy-start | bytes 294916
  110.1 24.0 %collective-permute-start.4 = (bf16[256,192]{0,1:T(8,128)(2,1)S(1)}, bf16[256,192]{0,1:T(8,128)(2,1)}, u32[]{:S(2)}, u32[]{:S(2)}) collective-permute-start(bf16[256,192]{0,1:T(8,128)(2,1)S(1)} %pad_maximum_fusion.6), channel_id=1, source_target_pairs={{0,30},{2,0},{4,2},{6,4},{8,6},{10,8},{12,10},{14,12},{16,14},{18,... | collective-permute-start | bytes 294920 | tf_op jit(solution)/shard_map/ppermute | solution.py:16
  114.1 1.2 copy-start.40
  115.9 1.3 copy-start.29
  117.2 7.5 %copy-start.31 = (pred[2048]{0:T(1024)(128)(4,1)S(1)}, pred[2048]{0:T(1024)(128)(4,1)}, u32[]{:S(2)}) copy-start(pred[2048]{0:T(1024)(128)(4,1)} %get-tuple-element.51) | copy-start | bytes 6148
  117.2 7.5 %copy-start.32 = (pred[2048]{0:T(1024)(128)(4,1)S(1)}, pred[2048]{0:T(1024)(128)(4,1)}, u32[]{:S(2)}) copy-start(pred[2048]{0:T(1024)(128)(4,1)} %get-tuple-element.53) | copy-start | bytes 6148
  124.7 2.8 %copy-start.11 = (f32[64,2048]{1,0:T(8,128)S(1)}, f32[64,2048]{1,0:T(8,128)}, u32[]{:S(2)}) copy-start(f32[64,2048]{1,0:T(8,128)} %get-tuple-element.14) | copy-start | bytes 1572868
  127.5 1.0 copy-start.10
  127.5 1.2 copy-start.13
  128.5 1.5 copy-start.15
  128.5 1.5 copy-start.16
  128.5 1.5 copy-start.20
  128.5 1.5 copy-start.41
  128.7 1.1 copy-start.12
  128.7 2.0 %copy-start.7 = (bf16[1,1,9,64,2048]{4,3,2,1,0:T(8,128)(2,1)S(1)}, bf16[1,1,9,64,2048]{4,3,2,1,0:T(8,128)(2,1)}, u32[]{:S(2)}) copy-start(bf16[1,1,9,64,2048]{4,3,2,1,0:T(8,128)(2,1)} %param.21) | copy-start | bytes 7077892
  128.7 2.7 %copy-start.8 = (bf16[576,2048]{1,0:T(8,128)(2,1)S(1)}, bf16[576,2048]{1,0:T(8,128)(2,1)}, u32[]{:S(2)}) copy-start(bf16[576,2048]{1,0:T(8,128)(2,1)} %copy.44) | copy-start | bytes 7077892
  131.5 2.5 %copy-start.21 = (bf16[256,64]{0,1:T(8,128)(2,1)S(1)}, bf16[256,64]{0,1:T(8,128)(2,1)}, u32[]{:S(2)}) copy-start(bf16[256,64]{0,1:T(8,128)(2,1)} %get-tuple-element.30) | copy-start | bytes 98308
  131.5 12.5 %copy-start.37 = (pred[512]{0:T(512)(128)(4,1)S(1)}, pred[512]{0:T(512)(128)(4,1)}, u32[]{:S(2)}) copy-start(pred[512]{0:T(512)(128)(4,1)} %copy-done.36) | copy-start | bytes 1540
  134.0 16.2 %copy-start.38 = (bf16[256,512]{1,0:T(8,128)(2,1)S(1)}, bf16[256,512]{1,0:T(8,128)(2,1)}, u32[]{:S(2)}) copy-start(bf16[256,512]{1,0:T(8,128)(2,1)} %param.39) | copy-start | bytes 786436
  134.0 16.2 %copy-start.39 = (bf16[512,256]{1,0:T(8,128)(2,1)S(1)}, bf16[512,256]{1,0:T(8,128)(2,1)}, u32[]{:S(2)}) copy-start(bf16[512,256]{1,0:T(8,128)(2,1)} %param.38) | copy-start | bytes 786436
  134.0 8.3 %collective-permute-start.5 = (bf16[256,192]{0,1:T(8,128)(2,1)S(1)}, bf16[256,192]{0,1:T(8,128)(2,1)S(1)}, u32[]{:S(2)}, u32[]{:S(2)}) collective-permute-start(bf16[256,192]{0,1:T(8,128)(2,1)S(1)} %pad_maximum_fusion.7), channel_id=1, source_target_pairs={{0,2},{2,4},{4,6},{6,8},{8,10},{10,12},{12,14},{14,16},{16,18},{18... | collective-permute-start | bytes 294920 | tf_op jit(solution)/shard_map/ppermute | solution.py:16
  142.3 1.4 collective-permute-start.6
  142.4 1.5 collective-permute-start.7
  150.2 5.8 %copy-start.1 = (bf16[512,256]{1,0:T(8,128)(2,1)S(1)}, bf16[512,256]{1,0:T(8,128)(2,1)}, u32[]{:S(2)}) copy-start(bf16[512,256]{1,0:T(8,128)(2,1)} %param.37) | copy-start | bytes 786436
  (3 other events, 2.2 us)
where the time goes:
time: 157 us; the launch traced here: 156 us
  local copies, waits for them, and re-layouts  70.9 us (45%)
  other arithmetic  35.5 us (23%)
  matrix products  24.6 us (16%)
  waiting for transfers between devices  12.1 us (8%)
  starting transfers between devices  11.6 us (7%)
    gather x2, local copies, waits for them, and re-layouts, edge_update(): jnp.take(table_tensor, reverse, axis=1).reshape(9, multiplicity, edge_count)  13.8 us
    unnamed x98, local copies, waits for them, and re-layouts  13.7 us
    ppermute x8, waiting for transfers between devices, passed_along(): lax.ppermute(x, axis, [(i, (i + by) % devices) for i in range(devices)])  12.1 us
    scatter-add x1, other arithmetic, edge_update(): jnp.zeros((channels, slot_count), jnp.bfloat16).at[:, target]  11.9 us
    ppermute x8, starting transfers between devices, passed_along(): lax.ppermute(x, axis, [(i, (i + by) % devices) for i in range(devices)])  11.6 us
    gather x1, local copies, waits for them, and re-layouts, edge_update(): scalar_rev = jnp.take(table_scalar, reverse, axis=1)  9.06 us
    gather x1, local copies, waits for them, and re-layouts, finish(): jnp.take(message, jnp.minimum(reverse, edge_count - 1), axis=1)  7.49 us
    scatter-add x1, other arithmetic, finish(): jnp.zeros((channels, edge_count), jnp.float32).at[:, send_index.reshape(-1)]  6.25 us
  transfers between devices with their start and end apart: 8, of which 4 were waited for; matrix products, arithmetic and copies ran while one was open for 22% of the time, Pallas kernels for 0%

commit v1 on v0

v1 whole, which is shorter than its diff:
```python
import functools
import math

import jax
import jax.numpy as jnp
from jax import lax
from jax.experimental import pallas as pl
from jax.experimental.pallas import tpu as pltpu
from jax.sharding import PartitionSpec as P

HEADS = 8
DIRECTIONS = ((1, 0), (-1, 0), (0, 1), (0, -1), (1, 1), (1, -1), (-1, 1), (-1, -1))
OPPOSITE = tuple(DIRECTIONS.index((-dx, -dy)) for dx, dy in DIRECTIONS)
EXTRA = 16
BF16 = jnp.bfloat16
F32 = jnp.float32


def plan_groups(gx, gy):
    groups = {}
    for p in (4, 5, 7, 6, 0, 1, 2, 3):
        dx, dy = DIRECTIONS[p]
        pairs = tuple(
            (a * gy + b, ((a + dx) % gx) * gy + (b + dy) % gy)
            for a in range(gx)
            for b in range(gy)
        )
        groups.setdefault(pairs, []).append(p)
    return [(pairs, tuple(members)) for pairs, members in groups.items()]


def mm(a, b):
    return jnp.dot(a, b, preferred_element_type=F32)


def embed(own, table, species):
    picked = table[:, 3:4]
    for j in (2, 1, 0):
        picked = jnp.where(species == j, table[:, j : j + 1], picked)
    return (own.astype(F32) + picked).astype(BF16)


def attend(queries, keys, values):
    channels, width = queries.shape
    size = channels // HEADS
    product = queries * keys
    parts = []
    for h in range(HEADS):
        rows = slice(h * size, (h + 1) * size)
        score = jnp.sum(product[rows], axis=0, keepdims=True) * (1.0 / math.sqrt(size))
        parts.append(jax.nn.sigmoid(score) * values[rows])
    return jnp.concatenate(parts, axis=0).astype(BF16)


def invariants(own, rev):
    product = own.astype(F32) * rev.astype(F32)
    return jnp.concatenate(
        [
            product[0],
            product[1] + product[2] + product[3],
            product[4] + product[5] + product[6] + product[7] + product[8],
        ],
        axis=0,
    ).astype(BF16)


def harmonics(vectors):
    x, y, z = vectors[0:1], vectors[1:2], vectors[2:3]
    r2 = x * x + y * y + z * z
    root = math.sqrt(3.0)
    return (
        None,
        x,
        y,
        z,
        root * x * y,
        root * y * z,
        0.5 * (3.0 * z * z - r2),
        root * x * z,
        0.5 * root * (x * x - y * y),
    )


def update_tensors(own, rev, gate, radial, mixing, vectors):
    m = own.shape[1]
    harmonic = harmonics(vectors)
    for k in range(9):
        degree = 0 if k == 0 else (1 if k < 4 else 2)
        rows = slice(degree * m, (degree + 1) * m)
        mixed = mm(mixing, rev[k])
        tail = radial[rows] if harmonic[k] is None else radial[rows] * harmonic[k]
        yield k, (own[k].astype(F32) + gate[rows] * mixed + tail).astype(BF16)


def feed_forward(middle, incoming, w_expand, w_reverse, w_contract):
    v = mm(w_expand, middle) + mm(w_reverse, incoming)
    hidden = (v * jax.nn.sigmoid(v)).astype(BF16)
    return (middle.astype(F32) + mm(w_contract, hidden)).astype(BF16)


def prepare_kernel(
    groups, scalars, tensors, vectors, species, send_index, counts, own, where, *rest
):
    sends, (s_buf, t_buf, sem) = rest[: len(groups)], rest[len(groups) :]
    copies = [
        pltpu.make_async_copy(scalars.at[0, 0], s_buf, sem.at[0]),
        pltpu.make_async_copy(tensors.at[0, 0], t_buf, sem.at[1]),
    ]
    for copy in copies:
        copy.start()
    channels, edges = s_buf.shape
    block = send_index.shape[-1]
    features = channels + t_buf.shape[0] * t_buf.shape[1]
    lane = lax.broadcasted_iota(jnp.int32, (1, block), 1)
    order = [p for _, members in groups for p in members]
    index = jnp.concatenate(
        [jnp.where(lane < counts[0, 0, p], send_index[0, 0, p : p + 1, :], -1) for p in order],
        axis=1,
    )
    slots = index.shape[1]
    onehot = (lax.broadcasted_iota(jnp.int32, (edges, slots), 0) == index).astype(BF16)
    vec = vectors[0, 0]
    high = vec.astype(BF16)
    left = vec - high.astype(F32)
    mid = left.astype(BF16)
    low = (left - mid.astype(F32)).astype(BF16)
    extra = jnp.concatenate(
        [
            jnp.broadcast_to(species[0].astype(F32), (7, edges)),
            high.astype(F32),
            mid.astype(F32),
            low.astype(F32),
        ],
        axis=0,
    ).astype(BF16)
    extra = mm(extra, onehot)
    where[0:3, :] = extra[7:10] + extra[10:13] + extra[13:16]
    where[3:8, :] = jnp.zeros((5, slots), F32)
    own[features:, :] = jnp.broadcast_to(extra[0:1], (EXTRA, slots)).astype(BF16)
    copies[0].wait()
    own[:channels, :] = mm(s_buf[...], onehot).astype(BF16)
    copies[1].wait()
    own[channels:features, :] = mm(
        t_buf[...].reshape(features - channels, edges), onehot
    ).astype(BF16)
    at = 0
    for send, (_, members) in zip(sends, groups):
        width = len(members) * block
        if width % 128 == 0:
            send[...] = own[:, at : at + width]
        else:
            half = features // 2
            piece = own[:, at : at + width]
            send[:half, :] = jnp.concatenate([piece[:half], piece[half:features]], axis=1)
            send[half:, :] = jnp.concatenate([piece[features:], piece[features:]], axis=1)
        at += width


def interior_kernel(
    scalars,
    tensors,
    vectors,
    species,
    reverse,
    table,
    w_query,
    w_key,
    w_value,
    w_output,
    w_invariant,
    w_message,
    w_gate,
    w_radial,
    w_mixing,
    middle_out,
    message_out,
    tensors_out,
):
    edges = scalars.shape[-1]
    width = reverse.shape[-1]
    channels = scalars.shape[2]
    here = pl.ds(pl.multiple_of(pl.program_id(0) * width, 128), width)
    comps, m = tensors.shape[2:4]
    onehot = (lax.broadcasted_iota(jnp.int32, (edges, width), 0) == reverse[0]).astype(BF16)
    s_rev = mm(scalars[0, 0], onehot).astype(BF16)
    t_rev = (
        mm(tensors[0, 0].reshape(comps * m, edges), onehot).astype(BF16).reshape(comps, m, width)
    )
    embedded = embed(scalars[0, 0, :, here], table[...], species[0])
    attended = attend(mm(w_query[...], embedded), mm(w_key[...], s_rev), mm(w_value[...], s_rev))
    own_t = tensors[0, 0, :, :, here]
    middle = (
        embedded.astype(F32)
        + mm(w_output[...], attended)
        + mm(w_invariant[...], invariants(own_t, t_rev))
    ).astype(BF16)
    middle_out[...] = middle
    message_out[...] = mm(w_message[...], middle).astype(BF16)
    gate = jax.nn.sigmoid(mm(w_gate[...], middle))
    radial = mm(w_radial[...], middle)
    for k, new in update_tensors(own_t, t_rev, gate, radial, w_mixing[...], vectors[0, 0]):
        tensors_out[k] = new


def incoming_kernel(message, middle, reverse, w_expand, w_reverse, w_contract, scalars_out):
    edges = message.shape[1]
    width = reverse.shape[-1]
    onehot = (lax.broadcasted_iota(jnp.int32, (edges, width), 0) == reverse[0]).astype(BF16)
    incoming = mm(message[...], onehot).astype(BF16)
    scalars_out[...] = feed_forward(
        middle[...], incoming, w_expand[...], w_reverse[...], w_contract[...]
    )


def boundary_kernel(groups, block, edges, *refs):
    count = len(groups)
    received, refs = refs[:count], refs[count:]
    (
        own,
        where,
        reverse,
        scalars_in,
        tensors_in,
        table,
        w_query,
        w_key,
        w_value,
        w_output,
        w_invariant,
        w_message,
        w_gate,
        w_radial,
        w_mixing,
        w_expand,
        w_reverse,
        w_contract,
        scalars_out,
        tensors_out,
        s_new,
        t_new,
        far,
    ) = refs
    order = [p for _, members in groups for p in members]
    comps, m = tensors_in.shape[:2]
    channels = scalars_in.shape[0]
    features = channels + comps * m
    slots = own.shape[1]

    @pl.when(pl.program_id(0) == 0)
    def _():
        place = {}
        for g, (_, members) in enumerate(groups):
            for n, p in enumerate(members):
                place[p] = (g, n, len(members))

        def block_of(p):
            g, n, total = place[p]
            if (total * block) % 128 == 0:
                return received[g][:, n * block : (n + 1) * block]
            half = features // 2
            piece = received[g]
            return jnp.concatenate(
                [piece[:half, :block], piece[:half, block:], piece[half:, :block]], axis=0
            )

        per = 128 // block
        for j in range(0, len(order), per):
            far[:, j * block : (j + per) * block] = jnp.concatenate(
                [block_of(OPPOSITE[p]) for p in order[j : j + per]], axis=1
            )
        s_own, s_far = own[:channels, :], far[:channels, :]
        t_own = own[channels:features, :].reshape(comps, m, slots)
        t_far = far[channels:features, :].reshape(comps, m, slots)
        e_own = embed(s_own, table[...], own[features : features + 1, :].astype(F32))
        e_far = embed(s_far, table[...], far[features : features + 1, :].astype(F32))
        shared = mm(w_invariant[...], invariants(t_own, t_far))
        a_own = attend(mm(w_query[...], e_own), mm(w_key[...], s_far), mm(w_value[...], s_far))
        a_far = attend(mm(w_query[...], e_far), mm(w_key[...], s_own), mm(w_value[...], s_own))
        middle = (e_own.astype(F32) + mm(w_output[...], a_own) + shared).astype(BF16)
        middle_far = (e_far.astype(F32) + mm(w_output[...], a_far) + shared).astype(BF16)
        incoming = mm(w_message[...], middle_far).astype(BF16)
        s_new[...] = feed_forward(middle, incoming, w_expand[...], w_reverse[...], w_contract[...])
        gate = jax.nn.sigmoid(mm(w_gate[...], middle))
        radial = mm(w_radial[...], middle)
        for k, new in update_tensors(t_own, t_far, gate, radial, w_mixing[...], where[...]):
            t_new[k * m : (k + 1) * m, :] = new

    target = reverse[0] - edges
    width = target.shape[1]
    rows = lax.broadcasted_iota(jnp.int32, (block, width), 0)
    onehot = jnp.concatenate(
        [(rows + OPPOSITE[p] * block == target).astype(F32) for p in order], axis=0
    ).astype(BF16)
    crosses = target >= 0
    scalars_out[0, 0] = jnp.where(
        crosses, mm(s_new[...], onehot), scalars_in[...].astype(F32)
    ).astype(BF16)
    merged = mm(t_new[...], onehot)
    for k in range(comps):
        tensors_out[0, 0, k] = jnp.where(
            crosses, merged[k * m : (k + 1) * m], tensors_in[k].astype(F32)
        ).astype(BF16)


def whole(*shape):
    return pl.BlockSpec(shape, lambda *_: (0,) * len(shape))


def per_device(gx, gy, *args):
    (
        scalars,
        tensors,
        vectors,
        species,
        table,
        reverse,
        send_index,
        counts,
        w_query,
        w_key,
        w_value,
        w_output,
        w_invariant,
        w_message,
        w_gate,
        w_radial,
        w_mixing,
        w_expand,
        w_reverse,
        w_contract,
    ) = args
    groups = plan_groups(gx, gy)
    _, _, channels, edges = scalars.shape
    comps, m = tensors.shape[2:4]
    features = channels + comps * m
    block = send_index.shape[-1]
    slots = len(DIRECTIONS) * block
    vmem = pl.BlockSpec(memory_space=pltpu.VMEM)
    limit = pltpu.CompilerParams(vmem_limit_bytes=56 * 2**20)

    def send_shape(members):
        width = len(members) * block
        if width % 128 == 0:
            return (features + EXTRA, width)
        return (features // 2 + EXTRA, 2 * width)

    own, where, *sends = pl.pallas_call(
        functools.partial(prepare_kernel, groups),
        in_specs=[
            pl.BlockSpec(memory_space=pl.ANY),
            pl.BlockSpec(memory_space=pl.ANY),
            vmem,
            vmem,
            vmem,
            pl.BlockSpec(memory_space=pltpu.SMEM),
        ],
        out_specs=[vmem] * (2 + len(groups)),
        out_shape=[
            jax.ShapeDtypeStruct((features + EXTRA, slots), BF16),
            jax.ShapeDtypeStruct((8, slots), F32),
        ]
        + [jax.ShapeDtypeStruct(send_shape(members), BF16) for _, members in groups],
        scratch_shapes=[
            pltpu.VMEM((channels, edges), BF16),
            pltpu.VMEM((comps, m, edges), BF16),
            pltpu.SemaphoreType.DMA((2,)),
        ],
        compiler_params=limit,
        name="prepare",
    )(scalars, tensors, vectors, species, send_index, counts)

    received = [
        lax.ppermute(send, ("gx", "gy"), pairs) for send, (pairs, _) in zip(sends, groups)
    ]

    width = 512
    steps = edges // width
    row = pl.BlockSpec((1, 1, width), lambda i: (0, 0, i))
    flat = pl.BlockSpec((channels, width), lambda i: (0, i))
    stack = pl.BlockSpec((comps, m, width), lambda i: (0, 0, i))
    first_weights = (w_query, w_key, w_value, w_output, w_invariant, w_message, w_gate, w_radial, w_mixing)
    last_weights = (w_expand, w_reverse, w_contract)
    middle, message, t_inside = pl.pallas_call(
        interior_kernel,
        grid=(steps,),
        in_specs=[
            whole(*scalars.shape),
            whole(*tensors.shape),
            pl.BlockSpec((1, 1, 3, width), lambda i: (0, 0, 0, i)),
            row,
            row,
            whole(*table.shape),
        ]
        + [whole(*w.shape) for w in first_weights],
        out_specs=[flat, flat, stack],
        out_shape=[
            jax.ShapeDtypeStruct((channels, edges), BF16),
            jax.ShapeDtypeStruct((channels, edges), BF16),
            jax.ShapeDtypeStruct((comps, m, edges), BF16),
        ],
        compiler_params=limit,
        cost_estimate=pl.CostEstimate(
            flops=2 * edges * edges * features, bytes_accessed=4 * edges * features, transcendentals=0
        ),
        name="interior",
    )(scalars, tensors, vectors, species, reverse, table, *first_weights)
    s_inside = pl.pallas_call(
        incoming_kernel,
        grid=(steps,),
        in_specs=[whole(channels, edges), flat, row] + [whole(*w.shape) for w in last_weights],
        out_specs=flat,
        out_shape=jax.ShapeDtypeStruct((channels, edges), BF16),
        compiler_params=limit,
        cost_estimate=pl.CostEstimate(
            flops=4 * edges * edges * channels, bytes_accessed=8 * edges * channels, transcendentals=0
        ),
        name="incoming",
    )(message, middle, reverse, *last_weights)

    return pl.pallas_call(
        functools.partial(boundary_kernel, groups, block, edges),
        grid=(steps,),
        in_specs=[whole(*r.shape) for r in received]
        + [whole(*own.shape), whole(*where.shape), row, flat, stack, whole(*table.shape)]
        + [whole(*w.shape) for w in first_weights + last_weights],
        out_specs=[
            pl.BlockSpec((1, 1, channels, width), lambda i: (0, 0, 0, i)),
            pl.BlockSpec((1, 1, comps, m, width), lambda i: (0, 0, 0, 0, i)),
        ],
        out_shape=[
            jax.ShapeDtypeStruct(scalars.shape, BF16),
            jax.ShapeDtypeStruct(tensors.shape, BF16),
        ],
        scratch_shapes=[
            pltpu.VMEM((channels, slots), BF16),
            pltpu.VMEM((comps * m, slots), BF16),
            pltpu.VMEM((features + EXTRA, slots), BF16),
        ],
        compiler_params=limit,
        cost_estimate=pl.CostEstimate(
            flops=2 * edges * slots * features, bytes_accessed=8 * edges * features, transcendentals=0
        ),
        name="boundary",
    )(*received, own, where, reverse, s_inside, t_inside, table, *first_weights, *last_weights)


def solution(mesh):
    return jax.shard_map(
        functools.partial(per_device, mesh.shape["gx"], mesh.shape["gy"]),
        mesh=mesh,
        in_specs=(
            P("gx", "gy", None, None),
            P("gx", "gy", None, None, None),
            P("gx", "gy", None, None),
            P("gx", "gy", None),
            P(),
            P("gx", "gy", None),
            P("gx", "gy", None, None),
            P("gx", "gy", None),
        )
        + (P(),) * 12,
        out_specs=(P("gx", "gy", None, None), P("gx", "gy", None, None, None)),
        check_vma=False,
    )
```

time: 157 us -> 56 us (0.36)
  local copies, waits for them, and re-layouts: 70.9 us -> 3.84 us
  Pallas kernels: 0 us -> 38.7 us
  other arithmetic: 35.5 us -> 0 us
  matrix products: 24.6 us -> 0 us
  waiting for transfers between devices: 12.1 us -> 0.01 us
    pallas_call x0 -> x4, Pallas kernels: none -> 38.7 us  [the longest x1 16.2 us: per_device(): pl.pallas_call(interior_kernel, grid=(steps,), in_specs=[whole(*scalars.s...]
    gather x6 -> x0, local copies, waits for them, and re-layouts: 35.3 us -> none  [the longest x2 13.8 us: edge_update(): jnp.take(table_tensor, reverse, axis=1).reshape(9, multiplicity, edge_count)]
    dot_general x10 -> x0, matrix products: 24.6 us -> none  [the longest x1 4.36 us: finish(): jnp.dot(w_contract, hidden, preferred_element_type=jnp.float32)]
    scatter-add x2 -> x0, other arithmetic: 18.1 us -> none  [the longest x1 11.9 us: edge_update(): jnp.zeros((channels, slot_count), jnp.bfloat16).at[:, target]]
    ppermute x8 -> x5, waiting for transfers between devices: 12.1 us -> 0.01 us  [per_device(): lax.ppermute(send, ('gx', 'gy'), pairs)]
    unnamed x98 -> x17, local copies, waits for them, and re-layouts: 13.7 us -> 3.84 us
    slice x13 -> x0, local copies, waits for them, and re-layouts: 8.33 us -> none  [the longest x4 2.94 us: deliver(): shifted[:, number * block_width:(number + 1) * block_width]]
    another operation x5 -> x0, local copies, waits for them, and re-layouts: 6.77 us -> none  [the longest x1 3.08 us: send_blocks(): tensors.reshape(-1, edge_count)]
  transfers between devices with their start and end apart: 8 -> 5, of which waited for: 4 -> 0; matrix products, arithmetic and copies ran while one was open for 22% -> 3% of each run, Pallas kernels for 0% -> 43%
where the time goes in v1:
time: 56 us; the launch traced here: 55.7 us
  Pallas kernels  38.7 us (69%)
  starting transfers between devices  12.4 us (22%)
  local copies, waits for them, and re-layouts  3.84 us (7%)
  between operations  0.73 us (1%)
    pallas_call x1, Pallas kernels, per_device(): pl.pallas_call(interior_kernel, grid=(steps,), in_specs=[whole(*scalars.s...  16.2 us
    ppermute x5, starting transfers between devices, per_device(): lax.ppermute(send, ('gx', 'gy'), pairs)  12.4 us
    pallas_call x1, Pallas kernels, per_device(): pl.pallas_call(functools.partial(boundary_kernel, groups, block, edges),...  9.15 us
    pallas_call x1, Pallas kernels, per_device(): pl.pallas_call(incoming_kernel, grid=(steps,), in_specs=[whole(channels,...  7.81 us
    pallas_call x1, Pallas kernels, per_device(): pl.pallas_call(functools.partial(prepare_kernel, groups), in_specs=[pl.Bl...  5.52 us
    unnamed x17, local copies, waits for them, and re-layouts  3.84 us
  transfers between devices with their start and end apart: 5, of which 0 were waited for; matrix products, arithmetic and copies ran while one was open for 3% of the time, Pallas kernels for 43%

profile of v1, /device:TPU:0, one launch (start us, length us, event | category | flops | bytes accessed | tf_op | source)
XLA Modules:
  0.0 55.7 jit_solution(2350292582612896012)
XLA Ops:
  0.6 0.0 copy-start.6
  0.6 0.0 copy-start.5
  0.7 1.4 %copy.22.vectors = f32[1,1,3,2048]{3,2,1,0:T(4,128)} copy(f32[1,1,3,2048]{3,1,2,0:T(1,128)} %param.22) | data formatting | bytes 49152 | tf_op args[2]
  2.0 5.5 %prepare.1 = (bf16[848,512]{1,0:T(8,128)(2,1)}, f32[8,512]{1,0:T(8,128)}, bf16[848,128]{1,0:T(8,128)(2,1)}, bf16[848,128]{1,0:T(8,128)(2,1)}, bf16[432,128]{1,0:...) custom-call(bf16[1,1,256,2048]{3,2,1,0:T(8,128)(2,1)} %scalars.3, ...), custom_call_target="tpu_custom_call" | custom-call | tf_op jit(solution)/shard_map/prepare/pallas_call | solution.py:347
  7.6 3.0 %collective-permute-start.2 = (bf16[432,128]{1,0:T(8,128)(2,1)}, bf16[432,128]{1,0:T(8,128)(2,1)S(1)}, u32[]{:S(2)}, u32[]{:S(2)}) collective-permute-start(bf16[432,128]{1,0:T(8,128)(2,1)} %get-tuple-element.14), channel_id=1, source_target_pairs={{0,2},{1,3},{2,4},{3,5},{4,6},{5,7},{6,8},{7,9},{8,10},{9,11},{10,... | collective-permute-start | bytes 331784 | tf_op jit(solution)/shard_map/ppermute | solution.py:373
  10.6 4.1 %collective-permute-start.3 = (bf16[432,128]{1,0:T(8,128)(2,1)}, bf16[432,128]{1,0:T(8,128)(2,1)S(1)}, u32[]{:S(2)}, u32[]{:S(2)}) collective-permute-start(bf16[432,128]{1,0:T(8,128)(2,1)} %get-tuple-element.15), channel_id=1, source_target_pairs={{0,30},{1,31},{2,0},{3,1},{4,2},{5,3},{6,4},{7,5},{8,6},{9,7},{10,... | collective-permute-start | bytes 331784 | tf_op jit(solution)/shard_map/ppermute | solution.py:373
  14.6 0.0 collective-permute-start
  14.6 5.3 %collective-permute-start.1 = (bf16[848,128]{1,0:T(8,128)(2,1)}, bf16[848,128]{1,0:T(8,128)(2,1)S(1)}, u32[]{:S(2)}, u32[]{:S(2)}) collective-permute-start(bf16[848,128]{1,0:T(8,128)(2,1)} %get-tuple-element.13), channel_id=1, source_target_pairs={{0,31},{1,30},{2,1},{3,0},{4,3},{5,2},{6,5},{7,4},{8,7},{9,6},{10,... | collective-permute-start | bytes 651272 | tf_op jit(solution)/shard_map/ppermute | solution.py:373
  20.0 0.0 collective-permute-start.4
  20.0 0.0 copy-done.6
  20.0 0.8 %copy.24.table.refs_10_ = f32[256,4]{1,0:T(8,128)} copy(f32[256,4]{0,1:T(4,128)S(1)} %copy-done.6) | data formatting | bytes 8192 | tf_op args[4]
  20.8 0.0 copy-done.5
  20.8 0.8 %copy.25.w_invariant.refs_15_ = bf16[256,192]{1,0:T(8,128)(2,1)} copy(bf16[256,192]{0,1:T(8,128)(2,1)S(1)} %copy-done.5) | data formatting | bytes 196608 | tf_op args[12]
  21.6 16.2 %interior.1 = (bf16[256,2048]{1,0:T(8,128)(2,1)}, bf16[256,2048]{1,0:T(8,128)(2,1)}, bf16[9,64,2048]{2,1,0:T(8,128)(2,1)}) custom-call(bf16[1,1,256,2048]{3,2,1,0:T(8,128)(2,1)} %scalars.3, bf16[1,1,9,64,2048]{4,3,2,1,0:T(8,128)(2,1)} %tensors.3, f32[1,1,3,2048]{3,2,1,0:T(4,128)} %copy.22.vectors, s32[1,1,2048]{2,1,0:T(1,128)} %species.3, ...), custom_call_target="tpu_custom_call" | custom-call | flops 6979321856 | bytes 6815744 | tf_op jit(solution)/shard_map/interior/pallas_call | solution.py:383
  37.8 7.8 %incoming.1.refs_8_ = bf16[256,2048]{1,0:T(8,128)(2,1)} custom-call(bf16[256,2048]{1,0:T(8,128)(2,1)} %get-tuple-element.19.message, bf16[256,2048]{1,0:T(8,128)(2,1)} %get-tuple-element.20.middle, s32[1,1,2048]{2,1,0:T(1,128)} %refs_7_.1, bf16[512,256]{1,0:T(8,128)(2,1)} %refs_20_.1, bf16[512,256]{1,0:T(8,128)(2,1)} %refs_21_.1, bf16[256,512]{1,0:T(8,128)(2,1)} %refs_22_.1), custom_call_target="tpu_custom_call" | custom-call | flops 4294967296 | bytes 4194304 | tf_op jit(solution)/shard_map/incoming/pallas_call | solution.py:407
  45.6 0.0 collective-permute-done.2.refs_2_
  45.6 0.0 copy-start.3
  45.6 0.0 collective-permute-done.3.refs_3_
  45.6 0.0 copy-start.4
  45.6 0.0 collective-permute-done.refs_0_
  45.6 0.0 copy-start
  45.6 0.0 collective-permute-done.1.refs_1_
  45.7 0.0 copy-start.1
  45.7 0.0 collective-permute-done.4.refs_4_
  45.7 0.0 copy-start.2
  45.7 0.6 copy-done.3
  46.2 0.0 copy-done.4
  46.3 0.1 copy-done
  46.4 0.1 copy-done.1
  46.5 0.1 copy-done.2
  46.6 9.2 %boundary.1 = (bf16[1,1,256,2048]{3,2,1,0:T(8,128)(2,1)}, bf16[1,1,9,64,2048]{4,3,2,1,0:T(8,128)(2,1)}) custom-call(bf16[848,128]{1,0:T(8,128)(2,1)} %copy-done, bf16[848,128]{1,0:T(8,128)(2,1)} %copy-done.1, bf16[432,128]{1,0:T(8,128)(2,1)} %copy-done.3, bf16[432,128]{1,0:T(8,128)(2,1)} %copy-done.4, bf16[848,128]{1,0:T(8,128)(2,1)} %copy-done.2, ...), custom_call_target="tpu_custom_call" | custom-call | flops 1744830464 | bytes 13631488 | tf_op jit(solution)/shard_map/boundary/pallas_call | solution.py:420
Async XLA Ops:
  0.6 19.4 %copy-start.6 = (f32[256,4]{0,1:T(4,128)S(1)}, f32[256,4]{0,1:T(4,128)}, u32[]{:S(2)}) copy-start(f32[256,4]{0,1:T(4,128)} %param.24) | copy-start | bytes 12292
  0.6 20.2 %copy-start.5 = (bf16[256,192]{0,1:T(8,128)(2,1)S(1)}, bf16[256,192]{0,1:T(8,128)(2,1)}, u32[]{:S(2)}) copy-start(bf16[256,192]{0,1:T(8,128)(2,1)} %param.32) | copy-start | bytes 294916
  7.6 38.0 %collective-permute-start.2 = (bf16[432,128]{1,0:T(8,128)(2,1)}, bf16[432,128]{1,0:T(8,128)(2,1)S(1)}, u32[]{:S(2)}, u32[]{:S(2)}) collective-permute-start(bf16[432,128]{1,0:T(8,128)(2,1)} %get-tuple-element.14), channel_id=1, source_target_pairs={{0,2},{1,3},{2,4},{3,5},{4,6},{5,7},{6,8},{7,9},{8,10},{9,11},{10,... | collective-permute-start | bytes 331784 | tf_op jit(solution)/shard_map/ppermute | solution.py:373
  10.6 35.0 %collective-permute-start.3 = (bf16[432,128]{1,0:T(8,128)(2,1)}, bf16[432,128]{1,0:T(8,128)(2,1)S(1)}, u32[]{:S(2)}, u32[]{:S(2)}) collective-permute-start(bf16[432,128]{1,0:T(8,128)(2,1)} %get-tuple-element.15), channel_id=1, source_target_pairs={{0,30},{1,31},{2,0},{3,1},{4,2},{5,3},{6,4},{7,5},{8,6},{9,7},{10,... | collective-permute-start | bytes 331784 | tf_op jit(solution)/shard_map/ppermute | solution.py:373
  14.6 31.0 %collective-permute-start = (bf16[848,128]{1,0:T(8,128)(2,1)}, bf16[848,128]{1,0:T(8,128)(2,1)S(1)}, u32[]{:S(2)}, u32[]{:S(2)}) collective-permute-start(bf16[848,128]{1,0:T(8,128)(2,1)} %get-tuple-element.12), channel_id=1, source_target_pairs={{0,3},{1,2},{2,5},{3,4},{4,7},{5,6},{6,9},{7,8},{8,11},{9,10},{10,... | collective-permute-start | bytes 651272 | tf_op jit(solution)/shard_map/ppermute | solution.py:373
  14.6 31.0 %collective-permute-start.1 = (bf16[848,128]{1,0:T(8,128)(2,1)}, bf16[848,128]{1,0:T(8,128)(2,1)S(1)}, u32[]{:S(2)}, u32[]{:S(2)}) collective-permute-start(bf16[848,128]{1,0:T(8,128)(2,1)} %get-tuple-element.13), channel_id=1, source_target_pairs={{0,31},{1,30},{2,1},{3,0},{4,3},{5,2},{6,5},{7,4},{8,7},{9,6},{10,... | collective-permute-start | bytes 651272 | tf_op jit(solution)/shard_map/ppermute | solution.py:373
  20.0 25.7 %collective-permute-start.4 = (bf16[848,128]{1,0:T(8,128)(2,1)}, bf16[848,128]{1,0:T(8,128)(2,1)S(1)}, u32[]{:S(2)}, u32[]{:S(2)}) collective-permute-start(bf16[848,128]{1,0:T(8,128)(2,1)} %get-tuple-element.16), channel_id=1, source_target_pairs={{0,1},{1,0},{2,3},{3,2},{4,5},{5,4},{6,7},{7,6},{8,9},{9,8},{10,11... | collective-permute-start | bytes 651272 | tf_op jit(solution)/shard_map/ppermute | solution.py:373
  45.6 0.6 %copy-start.3 = (bf16[432,128]{1,0:T(8,128)(2,1)}, bf16[432,128]{1,0:T(8,128)(2,1)S(1)}, u32[]{:S(2)}) copy-start(bf16[432,128]{1,0:T(8,128)(2,1)S(1)} %collective-permute-done.2.refs_2_) | copy-start | bytes 331780
  45.6 0.7 %copy-start.4 = (bf16[432,128]{1,0:T(8,128)(2,1)}, bf16[432,128]{1,0:T(8,128)(2,1)S(1)}, u32[]{:S(2)}) copy-start(bf16[432,128]{1,0:T(8,128)(2,1)S(1)} %collective-permute-done.3.refs_3_) | copy-start | bytes 331780
  45.6 0.7 %copy-start = (bf16[848,128]{1,0:T(8,128)(2,1)}, bf16[848,128]{1,0:T(8,128)(2,1)S(1)}, u32[]{:S(2)}) copy-start(bf16[848,128]{1,0:T(8,128)(2,1)S(1)} %collective-permute-done.refs_0_) | copy-start | bytes 651268
  45.7 0.8 %copy-start.1 = (bf16[848,128]{1,0:T(8,128)(2,1)}, bf16[848,128]{1,0:T(8,128)(2,1)S(1)}, u32[]{:S(2)}) copy-start(bf16[848,128]{1,0:T(8,128)(2,1)S(1)} %collective-permute-done.1.refs_1_) | copy-start | bytes 651268
  45.7 0.9 %copy-start.2 = (bf16[848,128]{1,0:T(8,128)(2,1)}, bf16[848,128]{1,0:T(8,128)(2,1)S(1)}, u32[]{:S(2)}) copy-start(bf16[848,128]{1,0:T(8,128)(2,1)S(1)} %collective-permute-done.4.refs_4_) | copy-start | bytes 651268

commit v2 on v1

--- a/solution.py
+++ b/solution.py
@@ -33,6 +33,15 @@
     return jnp.dot(a, b, preferred_element_type=F32)
 
 
+def nt(a, b):
+    return lax.dot_general(a, b, (((1,), (1,)), ((), ())), preferred_element_type=F32)
+
+
+def eye(n):
+    rows = lax.broadcasted_iota(jnp.int32, (n, n), 0)
+    return (rows == lax.broadcasted_iota(jnp.int32, (n, n), 1)).astype(BF16)
+
+
 def embed(own, table, species):
     picked = table[:, 3:4]
     for j in (2, 1, 0):
@@ -53,7 +62,7 @@
 
 
 def invariants(own, rev):
-    product = own.astype(F32) * rev.astype(F32)
+    product = [own[k].astype(F32) * rev[k].astype(F32) for k in range(9)]
     return jnp.concatenate(
         [
             product[0],
@@ -81,25 +90,23 @@
     )
 
 
-def update_tensors(own, rev, gate, radial, mixing, vectors):
-    m = own.shape[1]
+def update_tensors(own, mixed, gate, radial, vectors):
+    m = own[0].shape[0]
     harmonic = harmonics(vectors)
     for k in range(9):
         degree = 0 if k == 0 else (1 if k < 4 else 2)
         rows = slice(degree * m, (degree + 1) * m)
-        mixed = mm(mixing, rev[k])
         tail = radial[rows] if harmonic[k] is None else radial[rows] * harmonic[k]
-        yield k, (own[k].astype(F32) + gate[rows] * mixed + tail).astype(BF16)
-
-
-def feed_forward(middle, incoming, w_expand, w_reverse, w_contract):
-    v = mm(w_expand, middle) + mm(w_reverse, incoming)
+        yield k, (own[k].astype(F32) + gate[rows] * mixed[k] + tail).astype(BF16)
+
+
+def contract(middle, v, w_contract):
     hidden = (v * jax.nn.sigmoid(v)).astype(BF16)
     return (middle.astype(F32) + mm(w_contract, hidden)).astype(BF16)
 
 
 def prepare_kernel(
-    groups, scalars, tensors, vectors, species, send_index, counts, own, where, *rest
+    groups, scalars, tensors, vectors, species, reverse, send_index, counts, own, where, rows, *rest
 ):
     sends, (s_buf, t_buf, sem) = rest[: len(groups)], rest[len(groups) :]
     copies = [
@@ -119,7 +126,11 @@
     )
     slots = index.shape[1]
     onehot = (lax.broadcasted_iota(jnp.int32, (edges, slots), 0) == index).astype(BF16)
-    vec = vectors[0, 0]
+    near = jnp.minimum(reverse[0], edges - 1) * 8
+    rows[...] = jnp.concatenate(
+        [near[:, j * 128 : (j + 1) * 128] for j in range(edges // 128)], axis=0
+    )
+    vec = jnp.concatenate([vectors[0, j] for j in range(3)], axis=0)
     high = vec.astype(BF16)
     left = vec - high.astype(F32)
     mid = left.astype(BF16)
@@ -156,12 +167,24 @@
         at += width
 
 
+def copy_rows(table, rows, first, gathered, width):
+    per = rows.shape[1]
+
+    def body(i, _):
+        for u in range(per):
+            source = pl.ds(pl.multiple_of(rows[first + i, u], 8), 8)
+            gathered[pl.ds(pl.multiple_of(i * (per * 8) + u * 8, 8), 8), :] = table[source, :]
+        return 0
+
+    lax.fori_loop(0, width // per, body, 0)
+
+
 def interior_kernel(
     scalars,
     tensors,
     vectors,
     species,
-    reverse,
+    rows,
     table,
     w_query,
     w_key,
@@ -175,41 +198,96 @@
     middle_out,
     message_out,
     tensors_out,
+    edge_rows,
+    gathered,
+    pair_mix,
+    w_shared,
 ):
     edges = scalars.shape[-1]
-    width = reverse.shape[-1]
+    width = species.shape[-1]
     channels = scalars.shape[2]
-    here = pl.ds(pl.multiple_of(pl.program_id(0) * width, 128), width)
     comps, m = tensors.shape[2:4]
-    onehot = (lax.broadcasted_iota(jnp.int32, (edges, width), 0) == reverse[0]).astype(BF16)
-    s_rev = mm(scalars[0, 0], onehot).astype(BF16)
-    t_rev = (
-        mm(tensors[0, 0].reshape(comps * m, edges), onehot).astype(BF16).reshape(comps, m, width)
-    )
-    embedded = embed(scalars[0, 0, :, here], table[...], species[0])
-    attended = attend(mm(w_query[...], embedded), mm(w_key[...], s_rev), mm(w_value[...], s_rev))
-    own_t = tensors[0, 0, :, :, here]
+    step = pl.program_id(0)
+    here = pl.ds(pl.multiple_of(step * width, 128), width)
+    pairs = [(k, k + 1) for k in range(0, comps - 1, 2)] + [(comps - 2, comps - 1)]
+
+    @pl.when(step == 0)
+    def _():
+        unit = eye(256)
+        half = eye(128)
+        mixing = w_mixing[...].astype(F32)
+        zero = jnp.zeros((m, m), F32)
+        pair_mix[...] = jnp.concatenate(
+            [
+                half.astype(F32),
+                jnp.concatenate([mixing, zero], axis=1),
+                jnp.concatenate([zero, mixing], axis=1),
+            ],
+            axis=0,
+        ).astype(BF16)
+        w_shared[...] = nt(unit, w_invariant[...]).astype(BF16)
+        for at in range(0, edges, 256):
+            tile = slice(at, at + 256)
+            pieces = [
+                scalars[0, 0, c : c + 128, tile] for c in range(0, channels, 128)
+            ] + [tensors[0, 0, k : k + 2, :, tile].reshape(2 * m, 256) for k, _ in pairs]
+            for j, piece in enumerate(pieces):
+                edge_rows[pl.ds(at * 8 + j, 256, stride=8), :] = nt(unit, piece)
+
+    copy_rows(edge_rows, rows, step * (width // rows.shape[1]), gathered, width)
+
+    def feature(j):
+        return gathered[pl.ds(j, width, stride=8), :].astype(BF16)
+
+    lead = channels // 128
+    s_rev = jnp.concatenate([feature(j) for j in range(lead)], axis=1)
+    t_rev, mixed = {}, {}
+    for j, (first, second) in enumerate(pairs):
+        both = nt(pair_mix[...], feature(lead + j))
+        t_rev[first], t_rev[second] = both[:m], both[m : 2 * m]
+        mixed[first], mixed[second] = both[2 * m : 3 * m], both[3 * m :]
+    embedded = embed(scalars[0, 0, :, here], jnp.transpose(table[...]), species[0])
+    attended = attend(mm(w_query[...], embedded), nt(w_key[...], s_rev), nt(w_value[...], s_rev))
+    own_t = [tensors[0, 0, k, :, here] for k in range(comps)]
     middle = (
         embedded.astype(F32)
         + mm(w_output[...], attended)
-        + mm(w_invariant[...], invariants(own_t, t_rev))
+        + mm(w_shared[...], invariants(own_t, t_rev))
     ).astype(BF16)
     middle_out[...] = middle
     message_out[...] = mm(w_message[...], middle).astype(BF16)
     gate = jax.nn.sigmoid(mm(w_gate[...], middle))
     radial = mm(w_radial[...], middle)
-    for k, new in update_tensors(own_t, t_rev, gate, radial, w_mixing[...], vectors[0, 0]):
+    vec = jnp.concatenate([vectors[0, j] for j in range(3)], axis=0)
+    for k, new in update_tensors(own_t, mixed, gate, radial, vec):
         tensors_out[k] = new
 
 
-def incoming_kernel(message, middle, reverse, w_expand, w_reverse, w_contract, scalars_out):
-    edges = message.shape[1]
-    width = reverse.shape[-1]
-    onehot = (lax.broadcasted_iota(jnp.int32, (edges, width), 0) == reverse[0]).astype(BF16)
-    incoming = mm(message[...], onehot).astype(BF16)
-    scalars_out[...] = feed_forward(
-        middle[...], incoming, w_expand[...], w_reverse[...], w_contract[...]
+def incoming_kernel(
+    message, middle, rows, w_expand, w_reverse, w_contract, scalars_out, edge_rows, gathered
+):
+    channels, edges = message.shape
+    width = middle.shape[1]
+    step = pl.program_id(0)
+
+    @pl.when(step == 0)
+    def _():
+        unit = eye(256)
+        for at in range(0, edges, 256):
+            for j in range(channels // 128):
+                piece = message[j * 128 : (j + 1) * 128, at : at + 256]
+                edge_rows[pl.ds(at * 8 + j, 256, stride=8), :] = nt(unit, piece)
+
+    copy_rows(edge_rows, rows, step * (width // rows.shape[1]), gathered, width)
+    incoming = jnp.concatenate(
+        [
+            gathered[pl.ds(j, width, stride=8), :].astype(BF16)
+            for j in range(channels // 128)
+        ],
+        axis=1,
     )
+    v = mm(w_expand[...], middle[...]) + nt(w_reverse[...], incoming)
+    scalars_out[...] = contract(middle[...], v, w_contract[...])
 
 
 def boundary_kernel(groups, block, edges, *refs):
@@ -269,20 +347,24 @@
                 [block_of(OPPOSITE[p]) for p in order[j : j + per]], axis=1
             )
         s_own, s_far = own[:channels, :], far[:channels, :]
-        t_own = own[channels:features, :].reshape(comps, m, slots)
-        t_far = far[channels:features, :].reshape(comps, m, slots)
-        e_own = embed(s_own, table[...], own[features : features + 1, :].astype(F32))
-        e_far = embed(s_far, table[...], far[features : features + 1, :].astype(F32))
-        shared = mm(w_invariant[...], invariants(t_own, t_far))
+        t_own = [own[channels + k * m : channels + (k + 1) * m, :] for k in range(comps)]
+        t_far = [far[channels + k * m : channels + (k + 1) * m, :] for k in range(comps)]
+        columns = jnp.transpose(table[...])
+        e_own = embed(s_own, columns, own[features : features + 1, :].astype(F32))
+        e_far = embed(s_far, columns, far[features : features + 1, :].astype(F32))
+        w_shared = nt(eye(channels), w_invariant[...]).astype(BF16)
+        shared = mm(w_shared, invariants(t_own, t_far))
         a_own = attend(mm(w_query[...], e_own), mm(w_key[...], s_far), mm(w_value[...], s_far))
         a_far = attend(mm(w_query[...], e_far), mm(w_key[...], s_own), mm(w_value[...], s_own))
         middle = (e_own.astype(F32) + mm(w_output[...], a_own) + shared).astype(BF16)
         middle_far = (e_far.astype(F32) + mm(w_output[...], a_far) + shared).astype(BF16)
         incoming = mm(w_message[...], middle_far).astype(BF16)
-        s_new[...] = feed_forward(middle, incoming, w_expand[...], w_reverse[...], w_contract[...])
+        v = mm(w_expand[...], middle) + mm(w_reverse[...], incoming)
+        s_new[...] = contract(middle, v, w_contract[...])
         gate = jax.nn.sigmoid(mm(w_gate[...], middle))
         radial = mm(w_radial[...], middle)
-        for k, new in update_tensors(t_own, t_far, gate, radial, w_mixing[...], where[...]):
+        mixed = [mm(w_mixing[...], t_far[k]) for k in range(comps)]
+        for k, new in update_tensors(t_own, mixed, gate, radial, where[...]):
             t_new[k * m : (k + 1) * m, :] = new
 
     target = reverse[0] - edges
@@ -330,13 +412,19 @@
         w_contract,
     ) = args
     groups = plan_groups(gx, gy)
+    vectors = jnp.transpose(vectors, (0, 2, 1, 3))
+    table = jnp.transpose(table)
+    w_invariant = jnp.transpose(w_invariant)
     _, _, channels, edges = scalars.shape
     comps, m = tensors.shape[2:4]
     features = channels + comps * m
     block = send_index.shape[-1]
     slots = len(DIRECTIONS) * block
     vmem = pl.BlockSpec(memory_space=pltpu.VMEM)
-    limit = pltpu.CompilerParams(vmem_limit_bytes=56 * 2**20)
+
+    def limit(mebibytes):
+        return pltpu.CompilerParams(vmem_limit_bytes=mebibytes * 2**20)
+
 
     def send_shape(members):
         width = len(members) * block
@@ -344,7 +432,7 @@
             return (features + EXTRA, width)
         return (features // 2 + EXTRA, 2 * width)
 
-    own, where, *sends = pl.pallas_call(
+    own, where, rows, *sends = pl.pallas_call(
         functools.partial(prepare_kernel, groups),
         in_specs=[
             pl.BlockSpec(memory_space=pl.ANY),
@@ -352,12 +440,14 @@
             vmem,
             vmem,
             vmem,
+            vmem,
             pl.BlockSpec(memory_space=pltpu.SMEM),
         ],
-        out_specs=[vmem] * (2 + len(groups)),
+        out_specs=[vmem] * (3 + len(groups)),
         out_shape=[
             jax.ShapeDtypeStruct((features + EXTRA, slots), BF16),
             jax.ShapeDtypeStruct((8, slots), F32),
+            jax.ShapeDtypeStruct((edges // 128, 128), jnp.int32),
         ]
         + [jax.ShapeDtypeStruct(send_shape(members), BF16) for _, members in groups],
         scratch_shapes=[
@@ -365,14 +455,19 @@
             pltpu.VMEM((comps, m, edges), BF16),
             pltpu.SemaphoreType.DMA((2,)),
         ],
-        compiler_params=limit,
+        compiler_params=limit(24),
         name="prepare",
-    )(scalars, tensors, vectors, species, send_index, counts)
-
-    received = [
-        lax.ppermute(send, ("gx", "gy"), pairs) for send, (pairs, _) in zip(sends, groups)
-    ]
-
+    )(scalars, tensors, vectors, species, reverse, send_index, counts)
+
+    received = [None] * len(sends)
+
+    def exchange(chosen):
+        for g in chosen:
+            received[g] = lax.ppermute(sends[g], ("gx", "gy"), groups[g][0])
+
+    early = range(2)
+    late = range(2, len(sends))
+    exchange(early)
     width = 512
     steps = edges // width
     row = pl.BlockSpec((1, 1, width), lambda i: (0, 0, i))
@@ -386,9 +481,9 @@
         in_specs=[
             whole(*scalars.shape),
             whole(*tensors.shape),
-            pl.BlockSpec((1, 1, 3, width), lambda i: (0, 0, 0, i)),
+            pl.BlockSpec((1, 3, 1, width), lambda i: (0, 0, 0, i)),
             row,
-            row,
+            pl.BlockSpec(memory_space=pltpu.SMEM),
             whole(*table.shape),
         ]
         + [whole(*w.shape) for w in first_weights],
@@ -398,24 +493,39 @@
             jax.ShapeDtypeStruct((channels, edges), BF16),
             jax.ShapeDtypeStruct((comps, m, edges), BF16),
         ],
-        compiler_params=limit,
+        scratch_shapes=[
+            pltpu.VMEM((edges * 8, 128), F32),
+            pltpu.VMEM((width * 8, 128), F32),
+            pltpu.VMEM((256, 128), BF16),
+            pltpu.VMEM((channels, w_invariant.shape[0]), BF16),
+        ],
+        compiler_params=limit(36),
         cost_estimate=pl.CostEstimate(
             flops=2 * edges * edges * features, bytes_accessed=4 * edges * features, transcendentals=0
         ),
         name="interior",
-    )(scalars, tensors, vectors, species, reverse, table, *first_weights)
+    )(scalars, tensors, vectors, species, rows, table, *first_weights)
+    *held, middle = lax.optimization_barrier((*[sends[g] for g in late], middle))
+    for g, send in zip(late, held):
+        sends[g] = send
+    exchange(late)
     s_inside = pl.pallas_call(
         incoming_kernel,
         grid=(steps,),
-        in_specs=[whole(channels, edges), flat, row] + [whole(*w.shape) for w in last_weights],
+        in_specs=[whole(channels, edges), flat, pl.BlockSpec(memory_space=pltpu.SMEM)]
+        + [whole(*w.shape) for w in last_weights],
         out_specs=flat,
         out_shape=jax.ShapeDtypeStruct((channels, edges), BF16),
-        compiler_params=limit,
+        scratch_shapes=[
+            pltpu.VMEM((edges * 8, 128), F32),
+            pltpu.VMEM((width * 8, 128), F32),
+        ],
+        compiler_params=limit(24),
         cost_estimate=pl.CostEstimate(
             flops=4 * edges * edges * channels, bytes_accessed=8 * edges * channels, transcendentals=0
         ),
         name="incoming",
-    )(message, middle, reverse, *last_weights)
+    )(message, middle, rows, *last_weights)
 
     return pl.pallas_call(
         functools.partial(boundary_kernel, groups, block, edges),
@@ -436,7 +546,7 @@
             pltpu.VMEM((comps * m, slots), BF16),
             pltpu.VMEM((features + EXTRA, slots), BF16),
         ],
-        compiler_params=limit,
+        compiler_params=limit(26),
         cost_estimate=pl.CostEstimate(
             flops=2 * edges * slots * features, bytes_accessed=8 * edges * features, transcendentals=0
         ),

time: 56 us -> 55.3 us (0.987)
  Pallas kernels: 38.7 us -> 28.1 us
  local copies, waits for them, and re-layouts: 3.84 us -> 13.6 us
    unnamed x17 -> x50, local copies, waits for them, and re-layouts: 3.84 us -> 13.6 us
    pallas_call x1, Pallas kernels: 16.2 us -> 12 us  [per_device(): pl.pallas_call(interior_kernel, grid=(steps,), in_specs=[whole(*scalars.s...]
    pallas_call x1, Pallas kernels: 9.15 us -> 6.43 us  [per_device(): pl.pallas_call(functools.partial(boundary_kernel, groups, block, edges),...]
    pallas_call x1, Pallas kernels: 5.52 us -> 3.58 us  [per_device(): pl.pallas_call(functools.partial(prepare_kernel, groups), in_specs=[pl.Bl...]
    pallas_call x1, Pallas kernels: 7.81 us -> 6.08 us  [per_device(): pl.pallas_call(incoming_kernel, grid=(steps,), in_specs=[whole(channels,...]
  transfers between devices with their start and end apart: 5 -> 5, of which waited for: 0 -> 0; matrix products, arithmetic and copies ran while one was open for 3% -> 0% of each run, Pallas kernels for 43% -> 33%
where the time goes in v2:
time: 55.3 us; the launch traced here: 54.8 us
  Pallas kernels  28.1 us (51%)
  local copies, waits for them, and re-layouts  13.6 us (25%)
  starting transfers between devices  12.3 us (22%)
  between operations  0.79 us (1%)
    unnamed x50, local copies, waits for them, and re-layouts  13.6 us
    ppermute x5, starting transfers between devices, exchange(): received[g] = lax.ppermute(sends[g], ('gx', 'gy'), groups[g][0])  12.3 us
    pallas_call x1, Pallas kernels, per_device(): pl.pallas_call(interior_kernel, grid=(steps,), in_specs=[whole(*scalars.s...  12 us
    pallas_call x1, Pallas kernels, per_device(): pl.pallas_call(functools.partial(boundary_kernel, groups, block, edges),...  6.43 us
    pallas_call x1, Pallas kernels, per_device(): pl.pallas_call(incoming_kernel, grid=(steps,), in_specs=[whole(channels,...  6.08 us
    pallas_call x1, Pallas kernels, per_device(): pl.pallas_call(functools.partial(prepare_kernel, groups), in_specs=[pl.Bl...  3.58 us
  transfers between devices with their start and end apart: 5, of which 0 were waited for; matrix products, arithmetic and copies ran while one was open for 0% of the time, Pallas kernels for 33%

profile of v2, /device:TPU:0, one launch (start us, length us, event | category | flops | bytes accessed | tf_op | source)
XLA Modules:
  0.0 54.8 jit_solution(4229528341662770373)
XLA Ops:
  0.6 0.0 copy-start
  0.6 1.7 %copy-done = bf16[1,1,9,64,2048]{4,3,2,1,0:T(8,128)(2,1)S(1)} copy-done((bf16[1,1,9,64,2048]{4,3,2,1,0:T(8,128)(2,1)S(1)}, bf16[1,1,9,64,2048]{4,3,2,1,0:T(8,128)(2,1)}, u32[]{:S(2)}) %copy-start) | copy-done | bytes 2359320
  2.3 0.0 copy-start.2
  2.3 1.2 %copy-done.2 = bf16[1,1,256,2048]{3,2,1,0:T(8,128)(2,1)S(1)} copy-done((bf16[1,1,256,2048]{3,2,1,0:T(8,128)(2,1)S(1)}, bf16[1,1,256,2048]{3,2,1,0:T(8,128)(2,1)}, u32[]{:S(2)}) %copy-start.2) | copy-done | bytes 1048600
  3.5 0.0 copy-start.15
  3.5 0.7 %copy-done.15 = s32[1,1,2048]{2,1,0:T(1,128)S(1)} copy-done((s32[1,1,2048]{2,1,0:T(1,128)S(1)}, s32[1,1,2048]{2,1,0:T(1,128)}, u32[]{:S(2)}) %copy-start.15) | copy-done | bytes 8216
  4.2 0.0 copy-start.17
  4.2 0.7 %copy-done.17 = f32[1,1,3,2048]{3,1,2,0:T(1,128)S(1)} copy-done((f32[1,1,3,2048]{3,1,2,0:T(1,128)S(1)}, f32[1,1,3,2048]{3,1,2,0:T(1,128)}, u32[]{:S(2)}) %copy-start.17) | copy-done | bytes 24600
  5.0 0.0 copy-start.20
  5.0 0.7 %copy-done.20 = s32[1,1,2048]{2,1,0:T(1,128)S(1)} copy-done((s32[1,1,2048]{2,1,0:T(1,128)S(1)}, s32[1,1,2048]{2,1,0:T(1,128)}, u32[]{:S(2)}) %copy-start.20) | copy-done | bytes 8216
  5.7 0.0 copy-start.22
  5.7 0.7 %copy-done.22 = s32[1,1,8,64]{3,2,1,0:T(8,128)S(1)} copy-done((s32[1,1,8,64]{3,2,1,0:T(8,128)S(1)}, s32[1,1,8,64]{3,2,1,0:T(8,128)}, u32[]{:S(2)}) %copy-start.22) | copy-done | bytes 2072
  6.3 0.7 %copy-done.24 = s32[1,1,8]{2,1,0:T(1,128)S(1)} copy-done((s32[1,1,8]{2,1,0:T(1,128)S(1)}, s32[1,1,8]{2,1,0:T(1,128)}, u32[]{:S(2)}) %copy-start.24) | copy-done | bytes 56
  7.0 0.0 copy-start.21
  7.0 0.0 copy-start.23
  7.0 3.6 %prepare.1 = (bf16[848,512]{1,0:T(8,128)(2,1)S(1)}, f32[8,512]{1,0:T(8,128)S(1)}, s32[16,128]{1,0:T(8,128)S(1)}, bf16[848,128]{1,0:T(8,128)(2,1)S(1)}, bf16[848,...) custom-call(bf16[1,1,256,2048]{3,2,1,0:T(8,128)(2,1)S(1)} %copy-done, ...), custom_call_target="tpu_custom_call" | custom-call | tf_op jit(solution)/shard_map/prepare/pallas_call | solution.py:435
  10.6 2.5 %collective-permute-start = (bf16[848,128]{1,0:T(8,128)(2,1)S(1)}, bf16[848,128]{1,0:T(8,128)(2,1)S(1)}, u32[]{:S(2)}, u32[]{:S(2)}) collective-permute-start(bf16[848,128]{1,0:T(8,128)(2,1)S(1)} %get-tuple-element.17), channel_id=1, source_target_pairs={{0,3},{1,2},{2,5},{3,4},{4,7},{5,6},{6,9},{7,8},{8,11},{9,10},{10,... | collective-permute-start | bytes 651272 | tf_op jit(solution)/shard_map/ppermute | solution.py:466
  13.1 4.1 %collective-permute-start.1 = (bf16[848,128]{1,0:T(8,128)(2,1)S(1)}, bf16[848,128]{1,0:T(8,128)(2,1)S(1)}, u32[]{:S(2)}, u32[]{:S(2)}) collective-permute-start(bf16[848,128]{1,0:T(8,128)(2,1)S(1)} %get-tuple-element.18), channel_id=1, source_target_pairs={{0,31},{1,30},{2,1},{3,0},{4,3},{5,2},{6,5},{7,4},{8,7},{9,6},{10,... | collective-permute-start | bytes 651272 | tf_op jit(solution)/shard_map/ppermute | solution.py:466
  17.1 0.0 copy-done.1
  17.1 0.0 copy-done.3
  17.1 0.0 copy-done.18
  17.1 0.0 copy-done.19
  17.2 0.0 copy-done.21
  17.2 0.0 copy-done.23
  17.2 0.0 copy-start.7
  17.2 0.9 %copy-done.7 = bf16[256,256]{1,0:T(8,128)(2,1)S(1)} copy-done((bf16[256,256]{1,0:T(8,128)(2,1)S(1)}, bf16[256,256]{1,0:T(8,128)(2,1)}, u32[]{:S(2)}) %copy-start.7) | copy-done | bytes 131096
  18.1 0.9 %copy-done.8 = bf16[256,256]{1,0:T(8,128)(2,1)S(1)} copy-done((bf16[256,256]{1,0:T(8,128)(2,1)S(1)}, bf16[256,256]{1,0:T(8,128)(2,1)}, u32[]{:S(2)}) %copy-start.8) | copy-done | bytes 131096
  19.0 0.9 %copy-done.9 = bf16[256,256]{1,0:T(8,128)(2,1)S(1)} copy-done((bf16[256,256]{1,0:T(8,128)(2,1)S(1)}, bf16[256,256]{1,0:T(8,128)(2,1)}, u32[]{:S(2)}) %copy-start.9) | copy-done | bytes 131096
  19.9 0.9 %copy-done.10 = bf16[256,256]{1,0:T(8,128)(2,1)S(1)} copy-done((bf16[256,256]{1,0:T(8,128)(2,1)S(1)}, bf16[256,256]{1,0:T(8,128)(2,1)}, u32[]{:S(2)}) %copy-start.10) | copy-done | bytes 131096
  20.8 0.9 %copy-done.11 = bf16[256,256]{1,0:T(8,128)(2,1)S(1)} copy-done((bf16[256,256]{1,0:T(8,128)(2,1)S(1)}, bf16[256,256]{1,0:T(8,128)(2,1)}, u32[]{:S(2)}) %copy-start.11) | copy-done | bytes 131096
  21.7 0.9 %copy-done.12 = bf16[256,192]{0,1:T(8,128)(2,1)S(1)} copy-done((bf16[256,192]{0,1:T(8,128)(2,1)S(1)}, bf16[256,192]{0,1:T(8,128)(2,1)}, u32[]{:S(2)}) %copy-start.12) | copy-done | bytes 98328
  22.6 0.9 %copy-done.13 = bf16[192,256]{1,0:T(8,128)(2,1)S(1)} copy-done((bf16[192,256]{1,0:T(8,128)(2,1)S(1)}, bf16[192,256]{1,0:T(8,128)(2,1)}, u32[]{:S(2)}) %copy-start.13) | copy-done | bytes 98328
  23.5 0.9 %copy-done.14 = bf16[192,256]{1,0:T(8,128)(2,1)S(1)} copy-done((bf16[192,256]{1,0:T(8,128)(2,1)S(1)}, bf16[192,256]{1,0:T(8,128)(2,1)}, u32[]{:S(2)}) %copy-start.14) | copy-done | bytes 98328
  24.4 12.0 %interior.1 = (bf16[256,2048]{1,0:T(8,128)(2,1)S(1)}, bf16[256,2048]{1,0:T(8,128)(2,1)S(1)}, bf16[9,64,2048]{2,1,0:T(8,128)(2,1)S(1)}) custom-call(bf16[1,1,256,2048]{3,2,1,0:T(8,128)(2,1)S(1)} %copy-done.3, bf16[1,1,9,64,2048]{4,3,2,1,0:T(8,128)(2,1)S(1)} %copy-done.1, f32[1,3,1,2048]{3,2,1,0:T(1,128)S(1)} %bitcast.6, s32[1,1,2048]{2,1,0:T(1,128)S(1)} %copy-done.21, ...), custom_call_target="tpu_custom_call" | custom-call | flops 6979321856 | bytes 6815744 | tf_op jit(solution)/shard_map/interior/pallas_call | solution.py:478
  36.4 0.1 collective-permute-start.2
  36.4 5.6 %collective-permute-start.3 = (bf16[432,128]{1,0:T(8,128)(2,1)S(1)}, bf16[432,128]{1,0:T(8,128)(2,1)S(1)}, u32[]{:S(2)}, u32[]{:S(2)}) collective-permute-start(bf16[432,128]{1,0:T(8,128)(2,1)S(1)} %get-tuple-element.25), channel_id=1, source_target_pairs={{0,30},{1,31},{2,0},{3,1},{4,2},{5,3},{6,4},{7,5},{8,6},{9,7},{10,... | collective-permute-start | bytes 331784 | tf_op jit(solution)/shard_map/ppermute | solution.py:466
  42.1 0.1 collective-permute-start.4
  42.2 0.0 copy-done.4
  42.2 0.0 copy-done.5
  42.2 0.0 copy-done.6
  42.2 6.1 %incoming.1.refs_8_ = bf16[256,2048]{1,0:T(8,128)(2,1)S(1)} custom-call(bf16[256,2048]{1,0:T(8,128)(2,1)S(1)} %get-tuple-element.29.message, bf16[256,2048]{1,0:T(8,128)(2,1)S(1)} %get-tuple-element.30.middle, s32[16,128]{1,0:T(8,128)S(1)} %get-tuple-element.22.rows, bf16[512,256]{1,0:T(8,128)(2,1)S(1)} %copy-done.4, bf16[512,256]{1,0:T(8,128)(2,1)S(1)} %copy-done.5, ...), custom_call_target="tpu_custom_call" | custom-call | flops 4294967296 | bytes 4194304 | tf_op jit(solution)/shard_map/incoming/pallas_call | solution.py:512
  48.3 0.0 collective-permute-done.2.refs_2_
  48.3 0.0 collective-permute-done.3.refs_3_
  48.3 0.0 collective-permute-done.refs_0_
  48.3 0.0 collective-permute-done.1.refs_1_
  48.3 0.0 collective-permute-done.4.refs_4_
  48.3 0.0 copy-done.16
  48.3 6.4 %boundary.1 = (bf16[1,1,256,2048]{3,2,1,0:T(8,128)(2,1)}, bf16[1,1,9,64,2048]{4,3,2,1,0:T(8,128)(2,1)}) custom-call(bf16[848,128]{1,0:T(8,128)(2,1)S(1)} %collective-permute-done.refs_0_, bf16[848,128]{1,0:T(8,128)(2,1)S(1)} %collective-permute-done.1.refs_1_, bf16[432,128]{1,0:T(8,128)(2,1)S(1)} %collective-permute-done.2.refs_2_, ...), custom_call_target="tpu_custom_call" | custom-call | flops 1744830464 | bytes 13631488 | tf_op jit(solution)/shard_map/boundary/pallas_call | solution.py:530
  (16 shorter events, 0.0 us)
Async XLA Ops:
  0.6 1.7 %copy-start = (bf16[1,1,9,64,2048]{4,3,2,1,0:T(8,128)(2,1)S(1)}, bf16[1,1,9,64,2048]{4,3,2,1,0:T(8,128)(2,1)}, u32[]{:S(2)}) copy-start(bf16[1,1,9,64,2048]{4,3,2,1,0:T(8,128)(2,1)} %tensors.3) | copy-start | bytes 7077892
  2.3 1.2 %copy-start.2 = (bf16[1,1,256,2048]{3,2,1,0:T(8,128)(2,1)S(1)}, bf16[1,1,256,2048]{3,2,1,0:T(8,128)(2,1)}, u32[]{:S(2)}) copy-start(bf16[1,1,256,2048]{3,2,1,0:T(8,128)(2,1)} %scalars.3) | copy-start | bytes 3145732
  3.5 0.7 %copy-start.15 = (s32[1,1,2048]{2,1,0:T(1,128)S(1)}, s32[1,1,2048]{2,1,0:T(1,128)}, u32[]{:S(2)}) copy-start(s32[1,1,2048]{2,1,0:T(1,128)} %refs_7_.1) | copy-start | bytes 24580
  4.2 0.7 %copy-start.17 = (f32[1,1,3,2048]{3,1,2,0:T(1,128)S(1)}, f32[1,1,3,2048]{3,1,2,0:T(1,128)}, u32[]{:S(2)}) copy-start(f32[1,1,3,2048]{3,1,2,0:T(1,128)} %param.22) | copy-start | bytes 73732
  5.0 0.7 %copy-start.20 = (s32[1,1,2048]{2,1,0:T(1,128)S(1)}, s32[1,1,2048]{2,1,0:T(1,128)}, u32[]{:S(2)}) copy-start(s32[1,1,2048]{2,1,0:T(1,128)} %species.3) | copy-start | bytes 24580
  5.7 0.7 %copy-start.22 = (s32[1,1,8,64]{3,2,1,0:T(8,128)S(1)}, s32[1,1,8,64]{3,2,1,0:T(8,128)}, u32[]{:S(2)}) copy-start(s32[1,1,8,64]{3,2,1,0:T(8,128)} %send_index.1) | copy-start | bytes 6148
  6.3 0.7 %copy-start.24 = (s32[1,1,8]{2,1,0:T(1,128)S(1)}, s32[1,1,8]{2,1,0:T(1,128)}, u32[]{:S(2)}) copy-start(s32[1,1,8]{2,1,0:T(1,128)} %counts.1) | copy-start | bytes 100
  7.0 10.1 %copy-start.1 = (bf16[1,1,9,64,2048]{4,3,2,1,0:T(8,128)(2,1)S(1)}, bf16[1,1,9,64,2048]{4,3,2,1,0:T(8,128)(2,1)}, u32[]{:S(2)}) copy-start(bf16[1,1,9,64,2048]{4,3,2,1,0:T(8,128)(2,1)} %tensors.3) | copy-start | bytes 7077892
  7.0 10.1 %copy-start.3 = (bf16[1,1,256,2048]{3,2,1,0:T(8,128)(2,1)S(1)}, bf16[1,1,256,2048]{3,2,1,0:T(8,128)(2,1)}, u32[]{:S(2)}) copy-start(bf16[1,1,256,2048]{3,2,1,0:T(8,128)(2,1)} %scalars.3) | copy-start | bytes 3145732
  7.0 10.1 %copy-start.18 = (f32[1,1,3,2048]{3,1,2,0:T(1,128)S(1)}, f32[1,1,3,2048]{3,1,2,0:T(1,128)}, u32[]{:S(2)}) copy-start(f32[1,1,3,2048]{3,1,2,0:T(1,128)} %param.22) | copy-start | bytes 73732
  7.0 10.1 %copy-start.19 = (bf16[64,64]{1,0:T(8,128)(2,1)S(1)}, bf16[64,64]{1,0:T(8,128)(2,1)}, u32[]{:S(2)}) copy-start(bf16[64,64]{1,0:T(8,128)(2,1)} %refs_19_.1) | copy-start | bytes 24580
  7.0 10.1 %copy-start.21 = (s32[1,1,2048]{2,1,0:T(1,128)S(1)}, s32[1,1,2048]{2,1,0:T(1,128)}, u32[]{:S(2)}) copy-start(s32[1,1,2048]{2,1,0:T(1,128)} %species.3) | copy-start | bytes 24580
  7.0 10.1 %copy-start.23 = (f32[256,4]{0,1:T(4,128)S(1)}, f32[256,4]{0,1:T(4,128)}, u32[]{:S(2)}) copy-start(f32[256,4]{0,1:T(4,128)} %param.24) | copy-start | bytes 12292
  10.6 37.7 %collective-permute-start = (bf16[848,128]{1,0:T(8,128)(2,1)S(1)}, bf16[848,128]{1,0:T(8,128)(2,1)S(1)}, u32[]{:S(2)}, u32[]{:S(2)}) collective-permute-start(bf16[848,128]{1,0:T(8,128)(2,1)S(1)} %get-tuple-element.17), channel_id=1, source_target_pairs={{0,3},{1,2},{2,5},{3,4},{4,7},{5,6},{6,9},{7,8},{8,11},{9,10},{10,... | collective-permute-start | bytes 651272 | tf_op jit(solution)/shard_map/ppermute | solution.py:466
  13.1 35.2 %collective-permute-start.1 = (bf16[848,128]{1,0:T(8,128)(2,1)S(1)}, bf16[848,128]{1,0:T(8,128)(2,1)S(1)}, u32[]{:S(2)}, u32[]{:S(2)}) collective-permute-start(bf16[848,128]{1,0:T(8,128)(2,1)S(1)} %get-tuple-element.18), channel_id=1, source_target_pairs={{0,31},{1,30},{2,1},{3,0},{4,3},{5,2},{6,5},{7,4},{8,7},{9,6},{10,... | collective-permute-start | bytes 651272 | tf_op jit(solution)/shard_map/ppermute | solution.py:466
  17.2 0.9 %copy-start.7 = (bf16[256,256]{1,0:T(8,128)(2,1)S(1)}, bf16[256,256]{1,0:T(8,128)(2,1)}, u32[]{:S(2)}) copy-start(bf16[256,256]{1,0:T(8,128)(2,1)} %refs_11_.1) | copy-start | bytes 393220
  18.1 0.9 %copy-start.8 = (bf16[256,256]{1,0:T(8,128)(2,1)S(1)}, bf16[256,256]{1,0:T(8,128)(2,1)}, u32[]{:S(2)}) copy-start(bf16[256,256]{1,0:T(8,128)(2,1)} %refs_12_.1) | copy-start | bytes 393220
  19.0 0.9 %copy-start.9 = (bf16[256,256]{1,0:T(8,128)(2,1)S(1)}, bf16[256,256]{1,0:T(8,128)(2,1)}, u32[]{:S(2)}) copy-start(bf16[256,256]{1,0:T(8,128)(2,1)} %refs_13_.1) | copy-start | bytes 393220
  19.9 0.9 %copy-start.10 = (bf16[256,256]{1,0:T(8,128)(2,1)S(1)}, bf16[256,256]{1,0:T(8,128)(2,1)}, u32[]{:S(2)}) copy-start(bf16[256,256]{1,0:T(8,128)(2,1)} %refs_14_.1) | copy-start | bytes 393220
  20.8 0.9 %copy-start.11 = (bf16[256,256]{1,0:T(8,128)(2,1)S(1)}, bf16[256,256]{1,0:T(8,128)(2,1)}, u32[]{:S(2)}) copy-start(bf16[256,256]{1,0:T(8,128)(2,1)} %refs_16_.1) | copy-start | bytes 393220
  21.7 0.9 %copy-start.12 = (bf16[256,192]{0,1:T(8,128)(2,1)S(1)}, bf16[256,192]{0,1:T(8,128)(2,1)}, u32[]{:S(2)}) copy-start(bf16[256,192]{0,1:T(8,128)(2,1)} %param.32) | copy-start | bytes 294916
  22.6 0.9 %copy-start.13 = (bf16[192,256]{1,0:T(8,128)(2,1)S(1)}, bf16[192,256]{1,0:T(8,128)(2,1)}, u32[]{:S(2)}) copy-start(bf16[192,256]{1,0:T(8,128)(2,1)} %refs_17_.1) | copy-start | bytes 294916
  23.5 0.9 %copy-start.14 = (bf16[192,256]{1,0:T(8,128)(2,1)S(1)}, bf16[192,256]{1,0:T(8,128)(2,1)}, u32[]{:S(2)}) copy-start(bf16[192,256]{1,0:T(8,128)(2,1)} %refs_18_.1) | copy-start | bytes 294916
  24.4 17.8 %copy-start.4 = (bf16[512,256]{1,0:T(8,128)(2,1)S(1)}, bf16[512,256]{1,0:T(8,128)(2,1)}, u32[]{:S(2)}) copy-start(bf16[512,256]{1,0:T(8,128)(2,1)} %refs_20_.1) | copy-start | bytes 786436
  24.4 17.8 %copy-start.5 = (bf16[512,256]{1,0:T(8,128)(2,1)S(1)}, bf16[512,256]{1,0:T(8,128)(2,1)}, u32[]{:S(2)}) copy-start(bf16[512,256]{1,0:T(8,128)(2,1)} %refs_21_.1) | copy-start | bytes 786436
  24.4 17.8 %copy-start.6 = (bf16[256,512]{1,0:T(8,128)(2,1)S(1)}, bf16[256,512]{1,0:T(8,128)(2,1)}, u32[]{:S(2)}) copy-start(bf16[256,512]{1,0:T(8,128)(2,1)} %refs_22_.1) | copy-start | bytes 786436
  36.4 11.9 %collective-permute-start.2 = (bf16[432,128]{1,0:T(8,128)(2,1)S(1)}, bf16[432,128]{1,0:T(8,128)(2,1)S(1)}, u32[]{:S(2)}, u32[]{:S(2)}) collective-permute-start(bf16[432,128]{1,0:T(8,128)(2,1)S(1)} %get-tuple-element.24), channel_id=1, source_target_pairs={{0,2},{1,3},{2,4},{3,5},{4,6},{5,7},{6,8},{7,9},{8,10},{9,11},{10,... | collective-permute-start | bytes 331784 | tf_op jit(solution)/shard_map/ppermute | solution.py:466
  36.4 11.8 %collective-permute-start.3 = (bf16[432,128]{1,0:T(8,128)(2,1)S(1)}, bf16[432,128]{1,0:T(8,128)(2,1)S(1)}, u32[]{:S(2)}, u32[]{:S(2)}) collective-permute-start(bf16[432,128]{1,0:T(8,128)(2,1)S(1)} %get-tuple-element.25), channel_id=1, source_target_pairs={{0,30},{1,31},{2,0},{3,1},{4,2},{5,3},{6,4},{7,5},{8,6},{9,7},{10,... | collective-permute-start | bytes 331784 | tf_op jit(solution)/shard_map/ppermute | solution.py:466
  42.1 6.2 %collective-permute-start.4 = (bf16[848,128]{1,0:T(8,128)(2,1)S(1)}, bf16[848,128]{1,0:T(8,128)(2,1)S(1)}, u32[]{:S(2)}, u32[]{:S(2)}) collective-permute-start(bf16[848,128]{1,0:T(8,128)(2,1)S(1)} %get-tuple-element.26), channel_id=1, source_target_pairs={{0,1},{1,0},{2,3},{3,2},{4,5},{5,4},{6,7},{7,6},{8,9},{9,8},{10,11... | collective-permute-start | bytes 651272 | tf_op jit(solution)/shard_map/ppermute | solution.py:466
  42.2 6.1 %copy-start.16 = (s32[1,1,2048]{2,1,0:T(1,128)S(1)}, s32[1,1,2048]{2,1,0:T(1,128)}, u32[]{:S(2)}) copy-start(s32[1,1,2048]{2,1,0:T(1,128)} %refs_7_.1) | copy-start | bytes 24580

commit v3 on v2

--- a/solution.py
+++ b/solution.py
@@ -8,6 +8,7 @@
 from jax.experimental.pallas import tpu as pltpu
 from jax.sharding import PartitionSpec as P
 
+
 HEADS = 8
 DIRECTIONS = ((1, 0), (-1, 0), (0, 1), (0, -1), (1, 1), (1, -1), (-1, 1), (-1, -1))
 OPPOSITE = tuple(DIRECTIONS.index((-dx, -dy)) for dx, dy in DIRECTIONS)
@@ -16,17 +17,62 @@
 F32 = jnp.float32
 
 
-def plan_groups(gx, gy):
-    groups = {}
-    for p in (4, 5, 7, 6, 0, 1, 2, 3):
-        dx, dy = DIRECTIONS[p]
-        pairs = tuple(
-            (a * gy + b, ((a + dx) % gx) * gy + (b + dy) % gy)
-            for a in range(gx)
-            for b in range(gy)
-        )
-        groups.setdefault(pairs, []).append(p)
-    return [(pairs, tuple(members)) for pairs, members in groups.items()]
+def ring(gx, gy, dx, dy):
+    return tuple(
+        (a * gy + b, ((a + dx) % gx) * gy + (b + dy) % gy) for a in range(gx) for b in range(gy)
+    )
+
+
+class Plan:
+    def __init__(self, gx, gy):
+        self.paired = gx % 2 == 0 and gy == 2
+        if self.paired:
+            self.orders = ((4, 5, 7, 6, 0, 1, 2, 3), (7, 6, 4, 5, 1, 0, 2, 3))
+            self.arrays = ((("wide", 0), ("fold", 4)), (("wide", 2), ("fold", 5)), (("wide", 6),))
+            self.facing = (
+                (3, 0, 0), (3, 0, 1), (4, 0, 0), (4, 0, 1), (0, 1, 0), (1, 1, 0), (2, 0, 1), (2, 0, 0),
+            )
+            self.parts = self.arrays + self.arrays[:2]
+            even = [(a, a + 1 - 2 * (a % 2)) for a in range(gx)]
+            odd = [(a, (a - 1 + 2 * (a % 2)) % gx) for a in range(gx)]
+            self.swaps = [
+                tuple((a * gy + b, c * gy + b) for a, c in pairs for b in range(gy))
+                for pairs in (even, odd)
+            ]
+            self.across = ring(gx, gy, 0, 1)
+        else:
+            groups = {}
+            for p in (4, 5, 7, 6, 0, 1, 2, 3):
+                groups.setdefault(ring(gx, gy, *DIRECTIONS[p]), []).append(p)
+            order, self.arrays, place = [], (), {}
+            for g, members in enumerate(groups.values()):
+                parts = ()
+                rest = members
+                while rest:
+                    taken = 2 if len(rest) > 1 else 1
+                    for n, p in enumerate(rest[:taken]):
+                        place[p] = (g, len(parts), n)
+                    parts += (("wide" if taken == 2 else "fold", len(order)),)
+                    order += rest[:taken]
+                    rest = rest[taken:]
+                self.arrays += (parts,)
+            self.orders = (tuple(order),) * 2
+            self.parts = self.arrays
+            self.facing = tuple(place[OPPOSITE[p]] for p in order)
+            self.pairs = list(groups)
+
+    def part_rows(self, kind, features):
+        return features + EXTRA if kind == "wide" else features // 2 + EXTRA
+
+    def offset(self, parts, number, features):
+        return sum(self.part_rows(kind, features) for kind, _ in parts[:number])
+
+    def rows(self, parts, features):
+        return self.offset(parts, len(parts), features)
+
+
+def pick(odd, pair):
+    return pair[0] if pair[0] == pair[1] else jnp.where(odd, pair[1], pair[0])
 
 
 def mm(a, b):
@@ -50,7 +96,7 @@
 
 
 def attend(queries, keys, values):
-    channels, width = queries.shape
+    channels, _ = queries.shape
     size = channels // HEADS
     product = queries * keys
     parts = []
@@ -105,23 +151,38 @@
     return (middle.astype(F32) + mm(w_contract, hidden)).astype(BF16)
 
 
-def prepare_kernel(
-    groups, scalars, tensors, vectors, species, reverse, send_index, counts, own, where, rows, *rest
-):
-    sends, (s_buf, t_buf, sem) = rest[: len(groups)], rest[len(groups) :]
+def fetch(sources, buffers, sem):
     copies = [
-        pltpu.make_async_copy(scalars.at[0, 0], s_buf, sem.at[0]),
-        pltpu.make_async_copy(tensors.at[0, 0], t_buf, sem.at[1]),
+        pltpu.make_async_copy(source, buffer, sem.at[n])
+        for n, (source, buffer) in enumerate(zip(sources, buffers))
     ]
     for copy in copies:
         copy.start()
-    channels, edges = s_buf.shape
+    return copies
+
+
+def prepare_kernel(plan, *refs):
+    inputs, own, where, rows, refs = refs[:7], refs[7], refs[8], refs[9], refs[10:]
+    sends, buffers, sem = refs[: len(plan.arrays)], refs[len(plan.arrays) : -1], refs[-1]
+    copies = fetch(inputs, buffers, sem)
+    send_index, counts, species, vectors, reverse, scalars, tensors = buffers
+    channels, edges = scalars.shape[2:]
+    comps, m = tensors.shape[2:4]
     block = send_index.shape[-1]
-    features = channels + t_buf.shape[0] * t_buf.shape[1]
+    features = channels + comps * m
+    odd = lax.rem(lax.axis_index("gx"), 2) == 1
     lane = lax.broadcasted_iota(jnp.int32, (1, block), 1)
-    order = [p for _, members in groups for p in members]
+    for copy in copies[:5]:
+        copy.wait()
+
+    def live(p):
+        return jnp.where(lane < counts[0, 0, p], send_index[0, 0, p : p + 1, :], -1)
+
     index = jnp.concatenate(
-        [jnp.where(lane < counts[0, 0, p], send_index[0, 0, p : p + 1, :], -1) for p in order],
+        [
+            live(p) if p == q else jnp.where(odd, live(q), live(p))
+            for p, q in zip(*plan.orders)
+        ],
         axis=1,
     )
     slots = index.shape[1]
@@ -148,23 +209,25 @@
     where[0:3, :] = extra[7:10] + extra[10:13] + extra[13:16]
     where[3:8, :] = jnp.zeros((5, slots), F32)
     own[features:, :] = jnp.broadcast_to(extra[0:1], (EXTRA, slots)).astype(BF16)
-    copies[0].wait()
-    own[:channels, :] = mm(s_buf[...], onehot).astype(BF16)
-    copies[1].wait()
-    own[channels:features, :] = mm(
-        t_buf[...].reshape(features - channels, edges), onehot
-    ).astype(BF16)
-    at = 0
-    for send, (_, members) in zip(sends, groups):
-        width = len(members) * block
-        if width % 128 == 0:
-            send[...] = own[:, at : at + width]
-        else:
-            half = features // 2
-            piece = own[:, at : at + width]
-            send[:half, :] = jnp.concatenate([piece[:half], piece[half:features]], axis=1)
-            send[half:, :] = jnp.concatenate([piece[features:], piece[features:]], axis=1)
-        at += width
+    copies[5].wait()
+    own[:channels, :] = mm(scalars[0, 0], onehot).astype(BF16)
+    copies[6].wait()
+    own[channels:features, :] = mm(tensors[0, 0].reshape(comps * m, edges), onehot).astype(BF16)
+    half = features // 2
+    for send, parts in zip(sends, plan.arrays):
+        at = 0
+        for kind, j in parts:
+            if kind == "wide":
+                send[at : at + features + EXTRA, :] = own[:, j * block : (j + 2) * block]
+            else:
+                piece = own[:, j * block : (j + 1) * block]
+                send[at : at + half, :] = jnp.concatenate(
+                    [piece[:half], piece[half:features]], axis=1
+                )
+                send[at + half : at + half + EXTRA, :] = jnp.concatenate(
+                    [piece[features:], piece[features:]], axis=1
+                )
+            at += plan.part_rows(kind, features)
 
 
 def copy_rows(table, rows, first, gathered, width):
@@ -179,32 +242,28 @@
     lax.fori_loop(0, width // per, body, 0)
 
 
-def interior_kernel(
-    scalars,
-    tensors,
-    vectors,
-    species,
-    rows,
-    table,
-    w_query,
-    w_key,
-    w_value,
-    w_output,
-    w_invariant,
-    w_message,
-    w_gate,
-    w_radial,
-    w_mixing,
-    middle_out,
-    message_out,
-    tensors_out,
-    edge_rows,
-    gathered,
-    pair_mix,
-    w_shared,
-):
+def interior_kernel(rows, *refs):
+    inputs, refs = refs[:14], refs[14:]
+    middle_out, message_out, tensors_out, edge_rows, gathered, pair_mix, w_shared, *refs = refs
+    buffers, sem = refs[:-1], refs[-1]
+    (
+        scalars,
+        tensors,
+        w_mixing,
+        w_invariant,
+        vectors,
+        species,
+        table,
+        w_query,
+        w_key,
+        w_value,
+        w_output,
+        w_message,
+        w_gate,
+        w_radial,
+    ) = buffers
     edges = scalars.shape[-1]
-    width = species.shape[-1]
+    width = middle_out.shape[-1]
     channels = scalars.shape[2]
     comps, m = tensors.shape[2:4]
     step = pl.program_id(0)
@@ -213,8 +272,11 @@
 
     @pl.when(step == 0)
     def _():
+        copies = fetch(inputs, buffers, sem)
         unit = eye(256)
         half = eye(128)
+        for copy in copies:
+            copy.wait()
         mixing = w_mixing[...].astype(F32)
         zero = jnp.zeros((m, m), F32)
         pair_mix[...] = jnp.concatenate(
@@ -228,11 +290,19 @@
         w_shared[...] = nt(unit, w_invariant[...]).astype(BF16)
         for at in range(0, edges, 256):
             tile = slice(at, at + 256)
-            pieces = [
-                scalars[0, 0, c : c + 128, tile] for c in range(0, channels, 128)
-            ] + [tensors[0, 0, k : k + 2, :, tile].reshape(2 * m, 256) for k, _ in pairs]
-            for j, piece in enumerate(pieces):
-                edge_rows[pl.ds(at * 8 + j, 256, stride=8), :] = nt(unit, piece)
+            pieces = [scalars[0, 0, c : c + 256, tile] for c in range(0, channels, 256)]
+            n = 0
+            while n < len(pairs):
+                taken = 2 if n + 2 < len(pairs) else 1
+                k = pairs[n][0]
+                pieces.append(tensors[0, 0, k : k + 2 * taken, :, tile].reshape(-1, 256))
+                n += taken
+            j = 0
+            for piece in pieces:
+                turned = nt(unit, piece)
+                for c in range(0, piece.shape[0], 128):
+                    edge_rows[pl.ds(at * 8 + j, 256, stride=8), :] = turned[:, c : c + 128]
+                    j += 1
 
     copy_rows(edge_rows, rows, step * (width // rows.shape[1]), gathered, width)
 
@@ -246,7 +316,7 @@
         both = nt(pair_mix[...], feature(lead + j))
         t_rev[first], t_rev[second] = both[:m], both[m : 2 * m]
         mixed[first], mixed[second] = both[2 * m : 3 * m], both[3 * m :]
-    embedded = embed(scalars[0, 0, :, here], jnp.transpose(table[...]), species[0])
+    embedded = embed(scalars[0, 0, :, here], jnp.transpose(table[...]), species[0, :, here])
     attended = attend(mm(w_query[...], embedded), nt(w_key[...], s_rev), nt(w_value[...], s_rev))
     own_t = [tensors[0, 0, k, :, here] for k in range(comps)]
     middle = (
@@ -258,25 +328,30 @@
     message_out[...] = mm(w_message[...], middle).astype(BF16)
     gate = jax.nn.sigmoid(mm(w_gate[...], middle))
     radial = mm(w_radial[...], middle)
-    vec = jnp.concatenate([vectors[0, j] for j in range(3)], axis=0)
+    vec = jnp.concatenate([vectors[0, j, :, here] for j in range(3)], axis=0)
     for k, new in update_tensors(own_t, mixed, gate, radial, vec):
         tensors_out[k] = new
 
 
-def incoming_kernel(
-    message, middle, rows, w_expand, w_reverse, w_contract, scalars_out, edge_rows, gathered
-):
+def incoming_kernel(message, middle, rows, *refs):
+    inputs, (scalars_out, edge_rows, gathered, *buffers, sem) = refs[:3], refs[3:]
+    w_expand, w_reverse, w_contract = buffers
     channels, edges = message.shape
     width = middle.shape[1]
     step = pl.program_id(0)
 
     @pl.when(step == 0)
     def _():
+        copies = fetch(inputs, buffers, sem)
         unit = eye(256)
         for at in range(0, edges, 256):
-            for j in range(channels // 128):
-                piece = message[j * 128 : (j + 1) * 128, at : at + 256]
-                edge_rows[pl.ds(at * 8 + j, 256, stride=8), :] = nt(unit, piece)
+            for first in range(0, channels, 256):
+                turned = nt(unit, message[first : first + 256, at : at + 256])
+                for c in range(0, 256, 128):
+                    row = at * 8 + (first + c) // 128
+                    edge_rows[pl.ds(row, 256, stride=8), :] = turned[:, c : c + 128]
+        for copy in copies:
+            copy.wait()
 
     copy_rows(edge_rows, rows, step * (width // rows.shape[1]), gathered, width)
     incoming = jnp.concatenate(
@@ -290,8 +365,8 @@
     scalars_out[...] = contract(middle[...], v, w_contract[...])
 
 
-def boundary_kernel(groups, block, edges, *refs):
-    count = len(groups)
+def boundary_kernel(plan, block, edges, *refs):
+    count = len(plan.parts)
     received, refs = refs[:count], refs[count:]
     (
         own,
@@ -318,34 +393,31 @@
         t_new,
         far,
     ) = refs
-    order = [p for _, members in groups for p in members]
+    odd = lax.rem(lax.axis_index("gx"), 2) == 1
     comps, m = tensors_in.shape[:2]
     channels = scalars_in.shape[0]
     features = channels + comps * m
-    slots = own.shape[1]
 
     @pl.when(pl.program_id(0) == 0)
     def _():
-        place = {}
-        for g, (_, members) in enumerate(groups):
-            for n, p in enumerate(members):
-                place[p] = (g, n, len(members))
-
-        def block_of(p):
-            g, n, total = place[p]
-            if (total * block) % 128 == 0:
-                return received[g][:, n * block : (n + 1) * block]
+        def block_of(g, part, n):
+            kind, _ = plan.parts[g][part]
+            at = plan.offset(plan.parts[g], part, features)
+            if kind == "wide":
+                return received[g][at : at + features + EXTRA, n * block : (n + 1) * block]
             half = features // 2
-            piece = received[g]
-            return jnp.concatenate(
-                [piece[:half, :block], piece[:half, block:], piece[half:, :block]], axis=0
-            )
-
-        per = 128 // block
-        for j in range(0, len(order), per):
-            far[:, j * block : (j + per) * block] = jnp.concatenate(
-                [block_of(OPPOSITE[p]) for p in order[j : j + per]], axis=1
-            )
+            upper = received[g][at : at + half, :]
+            extra = received[g][at + half : at + half + EXTRA, :block]
+            return jnp.concatenate([upper[:, :block], upper[:, block:], extra], axis=0)
+
+        for j in range(0, len(plan.facing), 2):
+            to = slice(j * block, (j + 2) * block)
+            (g, part, n), second = plan.facing[j : j + 2]
+            if n == 0 and second == (g, part, 1):
+                at = plan.offset(plan.parts[g], part, features)
+                far[:, to] = received[g][at : at + features + EXTRA, :]
+            else:
+                far[:, to] = jnp.concatenate([block_of(g, part, n), block_of(*second)], axis=1)
         s_own, s_far = own[:channels, :], far[:channels, :]
         t_own = [own[channels + k * m : channels + (k + 1) * m, :] for k in range(comps)]
         t_far = [far[channels + k * m : channels + (k + 1) * m, :] for k in range(comps)]
@@ -371,7 +443,11 @@
     width = target.shape[1]
     rows = lax.broadcasted_iota(jnp.int32, (block, width), 0)
     onehot = jnp.concatenate(
-        [(rows + OPPOSITE[p] * block == target).astype(F32) for p in order], axis=0
+        [
+            (rows + pick(odd, (OPPOSITE[p], OPPOSITE[q])) * block == target).astype(F32)
+            for p, q in zip(*plan.orders)
+        ],
+        axis=0,
     ).astype(BF16)
     crosses = target >= 0
     scalars_out[0, 0] = jnp.where(
@@ -382,6 +458,10 @@
         tensors_out[0, 0, k] = jnp.where(
             crosses, merged[k * m : (k + 1) * m], tensors_in[k].astype(F32)
         ).astype(BF16)
+
+
+def resident(*arrays):
+    return [pltpu.with_memory_space_constraint(x, pltpu.HBM) for x in arrays]
 
 
 def whole(*shape):
@@ -411,7 +491,7 @@
         w_reverse,
         w_contract,
     ) = args
-    groups = plan_groups(gx, gy)
+    plan = Plan(gx, gy)
     vectors = jnp.transpose(vectors, (0, 2, 1, 3))
     table = jnp.transpose(table)
     w_invariant = jnp.transpose(w_invariant)
@@ -426,48 +506,46 @@
         return pltpu.CompilerParams(vmem_limit_bytes=mebibytes * 2**20)
 
 
-    def send_shape(members):
-        width = len(members) * block
-        if width % 128 == 0:
-            return (features + EXTRA, width)
-        return (features // 2 + EXTRA, 2 * width)
-
+    hbm = pl.BlockSpec(memory_space=pltpu.HBM)
+
+    def buffers(*arrays):
+        return [pltpu.VMEM(x.shape, x.dtype) for x in arrays] + [
+            pltpu.SemaphoreType.DMA((len(arrays),))
+        ]
+
+    prepared = (send_index, counts, species, vectors, reverse, scalars, tensors)
+    prepared_buffers = buffers(*prepared)
+    prepared_buffers[1] = pltpu.SMEM(counts.shape, counts.dtype)
     own, where, rows, *sends = pl.pallas_call(
-        functools.partial(prepare_kernel, groups),
-        in_specs=[
-            pl.BlockSpec(memory_space=pl.ANY),
-            pl.BlockSpec(memory_space=pl.ANY),
-            vmem,
-            vmem,
-            vmem,
-            vmem,
-            pl.BlockSpec(memory_space=pltpu.SMEM),
-        ],
-        out_specs=[vmem] * (3 + len(groups)),
+        functools.partial(prepare_kernel, plan),
+        in_specs=[hbm] * len(prepared),
+        out_specs=[vmem] * (3 + len(plan.arrays)),
         out_shape=[
             jax.ShapeDtypeStruct((features + EXTRA, slots), BF16),
             jax.ShapeDtypeStruct((8, slots), F32),
             jax.ShapeDtypeStruct((edges // 128, 128), jnp.int32),
         ]
-        + [jax.ShapeDtypeStruct(send_shape(members), BF16) for _, members in groups],
-        scratch_shapes=[
-            pltpu.VMEM((channels, edges), BF16),
-            pltpu.VMEM((comps, m, edges), BF16),
-            pltpu.SemaphoreType.DMA((2,)),
-        ],
+        + [
+            jax.ShapeDtypeStruct((plan.rows(parts, features), 2 * block), BF16)
+            for parts in plan.arrays
+        ],
+        scratch_shapes=prepared_buffers,
         compiler_params=limit(24),
         name="prepare",
-    )(scalars, tensors, vectors, species, reverse, send_index, counts)
-
-    received = [None] * len(sends)
-
-    def exchange(chosen):
-        for g in chosen:
-            received[g] = lax.ppermute(sends[g], ("gx", "gy"), groups[g][0])
-
-    early = range(2)
-    late = range(2, len(sends))
-    exchange(early)
+    )(*resident(*prepared))
+
+    def exchange(x, pairs):
+        return lax.ppermute(x, ("gx", "gy"), pairs)
+
+    if plan.paired:
+        received = [
+            exchange(sends[0], plan.swaps[0]),
+            exchange(sends[1], plan.swaps[1]),
+            exchange(sends[2], plan.across),
+        ]
+    else:
+        received = [exchange(x, pairs) for x, pairs in zip(sends, plan.pairs)]
+
     width = 512
     steps = edges // width
     row = pl.BlockSpec((1, 1, width), lambda i: (0, 0, i))
@@ -475,18 +553,14 @@
     stack = pl.BlockSpec((comps, m, width), lambda i: (0, 0, i))
     first_weights = (w_query, w_key, w_value, w_output, w_invariant, w_message, w_gate, w_radial, w_mixing)
     last_weights = (w_expand, w_reverse, w_contract)
+    inside = (
+        scalars, tensors, w_mixing, w_invariant, vectors, species, table,
+        w_query, w_key, w_value, w_output, w_message, w_gate, w_radial,
+    )
     middle, message, t_inside = pl.pallas_call(
         interior_kernel,
         grid=(steps,),
-        in_specs=[
-            whole(*scalars.shape),
-            whole(*tensors.shape),
-            pl.BlockSpec((1, 3, 1, width), lambda i: (0, 0, 0, i)),
-            row,
-            pl.BlockSpec(memory_space=pltpu.SMEM),
-            whole(*table.shape),
-        ]
-        + [whole(*w.shape) for w in first_weights],
+        in_specs=[pl.BlockSpec(memory_space=pltpu.SMEM)] + [hbm] * len(inside),
         out_specs=[flat, flat, stack],
         out_shape=[
             jax.ShapeDtypeStruct((channels, edges), BF16),
@@ -498,37 +572,43 @@
             pltpu.VMEM((width * 8, 128), F32),
             pltpu.VMEM((256, 128), BF16),
             pltpu.VMEM((channels, w_invariant.shape[0]), BF16),
-        ],
+        ]
+        + buffers(*inside),
         compiler_params=limit(36),
         cost_estimate=pl.CostEstimate(
             flops=2 * edges * edges * features, bytes_accessed=4 * edges * features, transcendentals=0
         ),
         name="interior",
-    )(scalars, tensors, vectors, species, rows, table, *first_weights)
-    *held, middle = lax.optimization_barrier((*[sends[g] for g in late], middle))
-    for g, send in zip(late, held):
-        sends[g] = send
-    exchange(late)
+    )(rows, *resident(*inside))
+    if plan.paired:
+        first, middle = lax.optimization_barrier((received[0], middle))
+        received[0] = first
+        received.append(exchange(first, plan.across))
     s_inside = pl.pallas_call(
         incoming_kernel,
         grid=(steps,),
         in_specs=[whole(channels, edges), flat, pl.BlockSpec(memory_space=pltpu.SMEM)]
-        + [whole(*w.shape) for w in last_weights],
+        + [hbm] * len(last_weights),
         out_specs=flat,
         out_shape=jax.ShapeDtypeStruct((channels, edges), BF16),
         scratch_shapes=[
             pltpu.VMEM((edges * 8, 128), F32),
             pltpu.VMEM((width * 8, 128), F32),
-        ],
+        ]
+        + buffers(*last_weights),
         compiler_params=limit(24),
         cost_estimate=pl.CostEstimate(
             flops=4 * edges * edges * channels, bytes_accessed=8 * edges * channels, transcendentals=0
         ),
         name="incoming",
-    )(message, middle, rows, *last_weights)
+    )(message, middle, rows, *resident(*last_weights))
+    if plan.paired:
+        second, s_inside = lax.optimization_barrier((received[1], s_inside))
+        received[1] = second
+        received.append(exchange(second, plan.across))
 
     return pl.pallas_call(
-        functools.partial(boundary_kernel, groups, block, edges),
+        functools.partial(boundary_kernel, plan, block, edges),
         grid=(steps,),
         in_specs=[whole(*r.shape) for r in received]
         + [whole(*own.shape), whole(*where.shape), row, flat, stack, whole(*table.shape)]
@@ -555,8 +635,13 @@
 
 
 def solution(mesh):
-    return jax.shard_map(
-        functools.partial(per_device, mesh.shape["gx"], mesh.shape["gy"]),
+    gx, gy = mesh.shape["gx"], mesh.shape["gy"]
+
+    def body(*args):
+        return per_device(gx, gy, *args)
+
+    step = jax.shard_map(
+        body,
         mesh=mesh,
         in_specs=(
             P("gx", "gy", None, None),
@@ -572,3 +657,6 @@
         out_specs=(P("gx", "gy", None, None), P("gx", "gy", None, None, None)),
         check_vma=False,
     )
+    if not Plan(gx, gy).paired:
+        return step
+    return step

time: 55.3 us -> 41.5 us (0.75)
  local copies, waits for them, and re-layouts: 13.6 us -> 0.09 us
  starting transfers between devices: 12.3 us -> 8.21 us
  Pallas kernels: 28.1 us -> 30.3 us
  waiting for transfers between devices: 0.01 us -> 1.83 us
    unnamed x50 -> x28, local copies, waits for them, and re-layouts: 13.6 us -> 0.09 us
    ppermute x5, starting transfers between devices: 12.3 us -> 8.21 us  [exchange(): return lax.ppermute(x, ('gx', 'gy'), pairs)]
    ppermute x5, waiting for transfers between devices: 0.01 us -> 1.83 us  [exchange(): return lax.ppermute(x, ('gx', 'gy'), pairs)]
    pallas_call x3, Pallas kernels: 22 us -> 23.8 us  [the longest x1 13.7 us: per_device(): pl.pallas_call(interior_kernel, grid=(steps,), in_specs=[pl.BlockSpec(mem...]
  transfers between devices with their start and end apart: 5 -> 5, of which waited for: 0 -> 1; matrix products, arithmetic and copies ran while one was open for 0% -> 0% of each run, Pallas kernels for 33% -> 49%
where the time goes in v3:
time: 41.5 us; the launch traced here: 41.3 us
  Pallas kernels  30.3 us (73%)
  starting transfers between devices  8.21 us (20%)
  waiting for transfers between devices  1.83 us (4%)
  between operations  0.9 us (2%)
    pallas_call x1, Pallas kernels, per_device(): pl.pallas_call(interior_kernel, grid=(steps,), in_specs=[pl.BlockSpec(mem...  13.7 us
    ppermute x5, starting transfers between devices, exchange(): return lax.ppermute(x, ('gx', 'gy'), pairs)  8.21 us
    pallas_call x1, Pallas kernels, per_device(): pl.pallas_call(incoming_kernel, grid=(steps,), in_specs=[whole(channels,...  6.5 us
    pallas_call x1, Pallas kernels, per_device(): pl.pallas_call(functools.partial(boundary_kernel, plan, block, edges), gr...  6.41 us
    pallas_call x1, Pallas kernels, per_device(): pl.pallas_call(functools.partial(prepare_kernel, plan), in_specs=[hbm] *...  3.66 us
    ppermute x5, waiting for transfers between devices, exchange(): return lax.ppermute(x, ('gx', 'gy'), pairs)  1.83 us
  transfers between devices with their start and end apart: 5, of which 1 were waited for; matrix products, arithmetic and copies ran while one was open for 0% of the time, Pallas kernels for 49%

profile of v3, /device:TPU:0, one launch (start us, length us, event | category | flops | bytes accessed | tf_op | source)
XLA Modules:
  0.0 41.3 jit_solution(5688081693075041868)
XLA Ops:
  0.6 3.7 %prepare.1 = (bf16[848,512]{1,0:T(8,128)(2,1)S(1)}, f32[8,512]{1,0:T(8,128)S(1)}, s32[16,128]{1,0:T(8,128)S(1)}, bf16[1280,128]{1,0:T(8,128)(2,1)S(1)}, bf16[128...) custom-call(s32[1,1,8,64]{3,2,1,0:T(8,128)} %refs_0_.3, s32[1,1,8]{2,1,0:T(1,128)} %refs_1_.3, s32[1,1,2048]{2,1,0:T(1,128)} %refs_5_.3, ...), custom_call_target="tpu_custom_call" | custom-call | tf_op jit(solution)/shard_map/prepare/pallas_call | solution.py:519
  4.3 3.0 %collective-permute-start = (bf16[1280,128]{1,0:T(8,128)(2,1)S(1)}, bf16[1280,128]{1,0:T(8,128)(2,1)S(1)}, u32[]{:S(2)}, u32[]{:S(2)}) collective-permute-start(bf16[1280,128]{1,0:T(8,128)(2,1)S(1)} %get-tuple-element.15), channel_id=1, source_target_pairs={{0,2},{1,3},{2,0},{3,1},{4,6},{5,7},{6,4},{7,5},{8,10},{9,11},{10,... | collective-permute-start | bytes 983048 | tf_op jit(solution)/shard_map/ppermute | solution.py:538
  7.3 4.5 %collective-permute-start.1 = (bf16[1280,128]{1,0:T(8,128)(2,1)S(1)}, bf16[1280,128]{1,0:T(8,128)(2,1)S(1)}, u32[]{:S(2)}, u32[]{:S(2)}) collective-permute-start(bf16[1280,128]{1,0:T(8,128)(2,1)S(1)} %get-tuple-element.19), channel_id=1, source_target_pairs={{0,30},{1,31},{2,4},{3,5},{4,2},{5,3},{6,8},{7,9},{8,6},{9,7},{10,... | collective-permute-start | bytes 983048 | tf_op jit(solution)/shard_map/ppermute | solution.py:538
  11.9 13.7 %interior.1 = (bf16[256,2048]{1,0:T(8,128)(2,1)S(1)}, bf16[256,2048]{1,0:T(8,128)(2,1)S(1)}, bf16[9,64,2048]{2,1,0:T(8,128)(2,1)S(1)}) custom-call(s32[16,128]{1,0:T(8,128)S(1)} %get-tuple-element.16.rows, bf16[1,1,256,2048]{3,2,1,0:T(8,128)(2,1)} %refs_0_.4, bf16[1,1,9,64,2048]{4,3,2,1,0:T(8,128)(2,1)} %refs_1_.4, bf16[64,64]{1,0:T(8,128)(2,1)} %refs_19_.1, ...), custom_call_target="tpu_custom_call" | custom-call | flops 6979321856 | bytes 6815744 | tf_op jit(solution)/shard_map/interior/pallas_call | solution.py:560
  25.6 0.0 collective-permute-done.refs_0_
  25.6 0.0 copy-start
  25.6 0.0 copy-start.1
  25.6 0.0 copy-start.2
  25.6 0.0 copy-start.3
  25.6 0.0 copy-start.4
  25.6 0.0 copy-start.5
  25.7 0.0 copy-start.6
  25.7 0.0 copy-start.7
  25.7 0.0 copy-start.8
  25.7 0.0 copy-start.9
  25.7 0.0 copy-start.10
  25.7 0.0 copy-start.11
  25.7 0.0 copy-start.12
  25.7 0.0 copy-start.13
  25.8 6.5 %incoming.1.refs_8_ = bf16[256,2048]{1,0:T(8,128)(2,1)S(1)} custom-call(bf16[256,2048]{1,0:T(8,128)(2,1)S(1)} %get-tuple-element.20.message, bf16[256,2048]{1,0:T(8,128)(2,1)S(1)} %get-tuple-element.21.middle, s32[16,128]{1,0:T(8,128)S(1)} %get-tuple-element.16.rows, bf16[512,256]{1,0:T(8,128)(2,1)} %refs_20_.1, bf16[512,256]{1,0:T(8,128)(2,1)} %refs_21_.1, ...), custom_call_target="tpu_custom_call" | custom-call | flops 4294967296 | bytes 4194304 | tf_op jit(solution)/shard_map/incoming/pallas_call | solution.py:587
  32.3 0.0 collective-permute-done.1.refs_1_
  32.3 0.1 collective-permute-start.4
  32.4 0.5 %collective-permute-start.3 = (bf16[1280,128]{1,0:T(8,128)(2,1)S(1)}, bf16[1280,128]{1,0:T(8,128)(2,1)S(1)}, u32[]{:S(2)}, u32[]{:S(2)}) collective-permute-start(bf16[1280,128]{1,0:T(8,128)(2,1)S(1)} %collective-permute-done.refs_0_), channel_id=1, source_target_pairs={{0,1},{1,0},{2,3},{3,2},{4,5},{5,4},{6,7},{7,6},{8,9},{9,8},{10,11... | collective-permute-start | bytes 983048 | tf_op jit(solution)/shard_map/ppermute | solution.py:538
  32.8 0.1 collective-permute-start.2
  32.9 1.8 %collective-permute-done.2.refs_2_ = bf16[848,128]{1,0:T(8,128)(2,1)S(1)} collective-permute-done((bf16[848,128]{1,0:T(8,128)(2,1)S(1)}, bf16[848,128]{1,0:T(8,128)(2,1)S(1)}, u32[]{:S(2)}, u32[]{:S(2)}) %collective-permute-start.2) | collective-permute-done | bytes 217120 | tf_op jit(solution)/shard_map/ppermute | solution.py:538
  34.7 0.0 collective-permute-done.4.refs_4_
  34.8 0.0 collective-permute-done.3.refs_3_
  34.8 0.0 copy-done
  34.8 0.0 copy-done.1
  34.8 0.0 copy-done.2
  34.8 0.0 copy-done.3
  34.8 0.0 copy-done.4
  34.8 0.0 copy-done.5
  34.8 0.0 copy-done.6
  34.8 0.0 copy-done.7
  34.8 0.0 copy-done.8
  34.8 0.0 copy-done.9
  34.8 0.0 copy-done.10
  34.9 0.0 copy-done.11
  34.9 0.0 copy-done.12
  34.9 0.0 copy-done.13
  34.9 6.4 %boundary.1 = (bf16[1,1,256,2048]{3,2,1,0:T(8,128)(2,1)}, bf16[1,1,9,64,2048]{4,3,2,1,0:T(8,128)(2,1)}) custom-call(bf16[1280,128]{1,0:T(8,128)(2,1)S(1)} %collective-permute-done.refs_0_, bf16[1280,128]{1,0:T(8,128)(2,1)S(1)} %collective-permute-done.1.refs_1_, bf16[848,128]{1,0:T(8,128)(2,1)S(1)} %collective-permute-done.2.refs_2_, ...), custom_call_target="tpu_custom_call" | custom-call | flops 1744830464 | bytes 13631488 | tf_op jit(solution)/shard_map/boundary/pallas_call | solution.py:610
Async XLA Ops:
  4.3 21.3 %collective-permute-start = (bf16[1280,128]{1,0:T(8,128)(2,1)S(1)}, bf16[1280,128]{1,0:T(8,128)(2,1)S(1)}, u32[]{:S(2)}, u32[]{:S(2)}) collective-permute-start(bf16[1280,128]{1,0:T(8,128)(2,1)S(1)} %get-tuple-element.15), channel_id=1, source_target_pairs={{0,2},{1,3},{2,0},{3,1},{4,6},{5,7},{6,4},{7,5},{8,10},{9,11},{10,... | collective-permute-start | bytes 983048 | tf_op jit(solution)/shard_map/ppermute | solution.py:538
  7.3 24.9 %collective-permute-start.1 = (bf16[1280,128]{1,0:T(8,128)(2,1)S(1)}, bf16[1280,128]{1,0:T(8,128)(2,1)S(1)}, u32[]{:S(2)}, u32[]{:S(2)}) collective-permute-start(bf16[1280,128]{1,0:T(8,128)(2,1)S(1)} %get-tuple-element.19), channel_id=1, source_target_pairs={{0,30},{1,31},{2,4},{3,5},{4,2},{5,3},{6,8},{7,9},{8,6},{9,7},{10,... | collective-permute-start | bytes 983048 | tf_op jit(solution)/shard_map/ppermute | solution.py:538
  25.6 9.2 %copy-start = (bf16[512,256]{1,0:T(8,128)(2,1)S(1)}, bf16[512,256]{1,0:T(8,128)(2,1)}, u32[]{:S(2)}) copy-start(bf16[512,256]{1,0:T(8,128)(2,1)} %refs_20_.1) | copy-start | bytes 786436
  25.6 9.2 %copy-start.1 = (bf16[512,256]{1,0:T(8,128)(2,1)S(1)}, bf16[512,256]{1,0:T(8,128)(2,1)}, u32[]{:S(2)}) copy-start(bf16[512,256]{1,0:T(8,128)(2,1)} %refs_21_.1) | copy-start | bytes 786436
  25.6 9.2 %copy-start.2 = (bf16[256,512]{1,0:T(8,128)(2,1)S(1)}, bf16[256,512]{1,0:T(8,128)(2,1)}, u32[]{:S(2)}) copy-start(bf16[256,512]{1,0:T(8,128)(2,1)} %refs_22_.1) | copy-start | bytes 786436
  25.6 9.2 %copy-start.3 = (bf16[256,256]{1,0:T(8,128)(2,1)S(1)}, bf16[256,256]{1,0:T(8,128)(2,1)}, u32[]{:S(2)}) copy-start(bf16[256,256]{1,0:T(8,128)(2,1)} %refs_11_.3) | copy-start | bytes 393220
  25.6 9.2 %copy-start.4 = (bf16[256,256]{1,0:T(8,128)(2,1)S(1)}, bf16[256,256]{1,0:T(8,128)(2,1)}, u32[]{:S(2)}) copy-start(bf16[256,256]{1,0:T(8,128)(2,1)} %refs_12_.3) | copy-start | bytes 393220
  25.6 9.2 %copy-start.5 = (bf16[256,256]{1,0:T(8,128)(2,1)S(1)}, bf16[256,256]{1,0:T(8,128)(2,1)}, u32[]{:S(2)}) copy-start(bf16[256,256]{1,0:T(8,128)(2,1)} %refs_13_.3) | copy-start | bytes 393220
  25.7 9.1 %copy-start.6 = (bf16[256,256]{1,0:T(8,128)(2,1)S(1)}, bf16[256,256]{1,0:T(8,128)(2,1)}, u32[]{:S(2)}) copy-start(bf16[256,256]{1,0:T(8,128)(2,1)} %refs_14_.1) | copy-start | bytes 393220
  25.7 9.1 %copy-start.7 = (bf16[256,256]{1,0:T(8,128)(2,1)S(1)}, bf16[256,256]{1,0:T(8,128)(2,1)}, u32[]{:S(2)}) copy-start(bf16[256,256]{1,0:T(8,128)(2,1)} %refs_16_.1) | copy-start | bytes 393220
  25.7 9.1 %copy-start.8 = (bf16[256,192]{0,1:T(8,128)(2,1)S(1)}, bf16[256,192]{0,1:T(8,128)(2,1)}, u32[]{:S(2)}) copy-start(bf16[256,192]{0,1:T(8,128)(2,1)} %param.32) | copy-start | bytes 294916
  25.7 9.1 %copy-start.9 = (bf16[192,256]{1,0:T(8,128)(2,1)S(1)}, bf16[192,256]{1,0:T(8,128)(2,1)}, u32[]{:S(2)}) copy-start(bf16[192,256]{1,0:T(8,128)(2,1)} %refs_17_.1) | copy-start | bytes 294916
  25.7 9.1 %copy-start.10 = (bf16[192,256]{1,0:T(8,128)(2,1)S(1)}, bf16[192,256]{1,0:T(8,128)(2,1)}, u32[]{:S(2)}) copy-start(bf16[192,256]{1,0:T(8,128)(2,1)} %refs_18_.1) | copy-start | bytes 294916
  25.7 9.1 %copy-start.11 = (s32[1,1,2048]{2,1,0:T(1,128)S(1)}, s32[1,1,2048]{2,1,0:T(1,128)}, u32[]{:S(2)}) copy-start(s32[1,1,2048]{2,1,0:T(1,128)} %refs_7_.3) | copy-start | bytes 24580
  25.7 9.1 %copy-start.12 = (bf16[64,64]{1,0:T(8,128)(2,1)S(1)}, bf16[64,64]{1,0:T(8,128)(2,1)}, u32[]{:S(2)}) copy-start(bf16[64,64]{1,0:T(8,128)(2,1)} %refs_19_.1) | copy-start | bytes 24580
  25.7 9.1 %copy-start.13 = (f32[256,4]{0,1:T(4,128)S(1)}, f32[256,4]{0,1:T(4,128)}, u32[]{:S(2)}) copy-start(f32[256,4]{0,1:T(4,128)} %param.24) | copy-start | bytes 12292
  32.3 2.5 %collective-permute-start.4 = (bf16[1280,128]{1,0:T(8,128)(2,1)S(1)}, bf16[1280,128]{1,0:T(8,128)(2,1)S(1)}, u32[]{:S(2)}, u32[]{:S(2)}) collective-permute-start(bf16[1280,128]{1,0:T(8,128)(2,1)S(1)} %collective-permute-done.1.refs_1_), channel_id=1, source_target_pairs={{0,1},{1,0},{2,3},{3,2},{4,5},{5,4},{6,7},{7,6},{8,9},{9,8},{10,11... | collective-permute-start | bytes 983048 | tf_op jit(solution)/shard_map/ppermute | solution.py:538
  32.4 2.4 %collective-permute-start.3 = (bf16[1280,128]{1,0:T(8,128)(2,1)S(1)}, bf16[1280,128]{1,0:T(8,128)(2,1)S(1)}, u32[]{:S(2)}, u32[]{:S(2)}) collective-permute-start(bf16[1280,128]{1,0:T(8,128)(2,1)S(1)} %collective-permute-done.refs_0_), channel_id=1, source_target_pairs={{0,1},{1,0},{2,3},{3,2},{4,5},{5,4},{6,7},{7,6},{8,9},{9,8},{10,11... | collective-permute-start | bytes 983048 | tf_op jit(solution)/shard_map/ppermute | solution.py:538
  32.8 1.9 %collective-permute-start.2 = (bf16[848,128]{1,0:T(8,128)(2,1)S(1)}, bf16[848,128]{1,0:T(8,128)(2,1)S(1)}, u32[]{:S(2)}, u32[]{:S(2)}) collective-permute-start(bf16[848,128]{1,0:T(8,128)(2,1)S(1)} %get-tuple-element.23), channel_id=1, source_target_pairs={{0,1},{1,0},{2,3},{3,2},{4,5},{5,4},{6,7},{7,6},{8,9},{9,8},{10,11... | collective-permute-start | bytes 651272 | tf_op jit(solution)/shard_map/ppermute | solution.py:538

commit v4 on v3

--- a/solution.py
+++ b/solution.py
@@ -152,10 +152,16 @@
 
 
 def fetch(sources, buffers, sem):
-    copies = [
-        pltpu.make_async_copy(source, buffer, sem.at[n])
-        for n, (source, buffer) in enumerate(zip(sources, buffers))
-    ]
+    pieces = []
+    waiting = list(sources)
+    for buffer in buffers:
+        at = 0
+        while at < buffer.shape[0]:
+            source = waiting.pop(0)
+            part = buffer if source.shape == buffer.shape else buffer.at[pl.ds(at, source.shape[0])]
+            pieces.append((source, part))
+            at += source.shape[0]
+    copies = [pltpu.make_async_copy(*piece, sem.at[n]) for n, piece in enumerate(pieces)]
     for copy in copies:
         copy.start()
     return copies
@@ -230,16 +236,17 @@
             at += plan.part_rows(kind, features)
 
 
-def copy_rows(table, rows, first, gathered, width):
+def copy_rows(step, table, rows, gathered):
     per = rows.shape[1]
-
-    def body(i, _):
-        for u in range(per):
-            source = pl.ds(pl.multiple_of(rows[first + i, u], 8), 8)
-            gathered[pl.ds(pl.multiple_of(i * (per * 8) + u * 8, 8), 8), :] = table[source, :]
-        return 0
-
-    lax.fori_loop(0, width // per, body, 0)
+    width = gathered.shape[0] // 8
+    for t in range(rows.shape[0] * per // width):
+
+        @pl.when(step == t)
+        def _(first=t * width):
+            for e in range(width):
+                n = first + e
+                source = pl.ds(pl.multiple_of(rows[n // per, n % per], 8), 8)
+                gathered[e * 8 : e * 8 + 8, :] = table[source, :]
 
 
 def interior_kernel(rows, *refs):
@@ -255,12 +262,9 @@
         species,
         table,
         w_query,
-        w_key,
-        w_value,
         w_output,
-        w_message,
-        w_gate,
-        w_radial,
+        w_rev,
+        w_mid,
     ) = buffers
     edges = scalars.shape[-1]
     width = middle_out.shape[-1]
@@ -275,7 +279,26 @@
         copies = fetch(inputs, buffers, sem)
         unit = eye(256)
         half = eye(128)
-        for copy in copies:
+
+        def turn(at, j, piece):
+            turned = nt(unit, piece)
+            for c in range(0, piece.shape[0], 128):
+                edge_rows[pl.ds(at * 8 + j + c // 128, 256, stride=8), :] = turned[:, c : c + 128]
+
+        copies[0].wait()
+        for at in range(0, edges, 256):
+            for c in range(0, channels, 256):
+                turn(at, c // 128, scalars[0, 0, c : c + 256, at : at + 256])
+        copies[1].wait()
+        for at in range(0, edges, 256):
+            n = 0
+            while n < len(pairs):
+                taken = 2 if n + 2 < len(pairs) else 1
+                k = pairs[n][0]
+                piece = tensors[0, 0, k : k + 2 * taken, :, at : at + 256].reshape(-1, 256)
+                turn(at, channels // 128 + n, piece)
+                n += taken
+        for copy in copies[2:]:
             copy.wait()
         mixing = w_mixing[...].astype(F32)
         zero = jnp.zeros((m, m), F32)
@@ -288,23 +311,8 @@
             axis=0,
         ).astype(BF16)
         w_shared[...] = nt(unit, w_invariant[...]).astype(BF16)
-        for at in range(0, edges, 256):
-            tile = slice(at, at + 256)
-            pieces = [scalars[0, 0, c : c + 256, tile] for c in range(0, channels, 256)]
-            n = 0
-            while n < len(pairs):
-                taken = 2 if n + 2 < len(pairs) else 1
-                k = pairs[n][0]
-                pieces.append(tensors[0, 0, k : k + 2 * taken, :, tile].reshape(-1, 256))
-                n += taken
-            j = 0
-            for piece in pieces:
-                turned = nt(unit, piece)
-                for c in range(0, piece.shape[0], 128):
-                    edge_rows[pl.ds(at * 8 + j, 256, stride=8), :] = turned[:, c : c + 128]
-                    j += 1
-
-    copy_rows(edge_rows, rows, step * (width // rows.shape[1]), gathered, width)
+
+    copy_rows(step, edge_rows, rows, gathered)
 
     def feature(j):
         return gathered[pl.ds(j, width, stride=8), :].astype(BF16)
@@ -317,7 +325,8 @@
         t_rev[first], t_rev[second] = both[:m], both[m : 2 * m]
         mixed[first], mixed[second] = both[2 * m : 3 * m], both[3 * m :]
     embedded = embed(scalars[0, 0, :, here], jnp.transpose(table[...]), species[0, :, here])
-    attended = attend(mm(w_query[...], embedded), nt(w_key[...], s_rev), nt(w_value[...], s_rev))
+    both = nt(w_rev[...], s_rev)
+    attended = attend(mm(w_query[...], embedded), both[:channels], both[channels:])
     own_t = [tensors[0, 0, k, :, here] for k in range(comps)]
     middle = (
         embedded.astype(F32)
@@ -325,9 +334,10 @@
         + mm(w_shared[...], invariants(own_t, t_rev))
     ).astype(BF16)
     middle_out[...] = middle
-    message_out[...] = mm(w_message[...], middle).astype(BF16)
-    gate = jax.nn.sigmoid(mm(w_gate[...], middle))
-    radial = mm(w_radial[...], middle)
+    spread = mm(w_mid[...], middle)
+    message_out[...] = spread[:channels].astype(BF16)
+    gate = jax.nn.sigmoid(spread[channels : channels + 3 * m])
+    radial = spread[channels + 3 * m :]
     vec = jnp.concatenate([vectors[0, j, :, here] for j in range(3)], axis=0)
     for k, new in update_tensors(own_t, mixed, gate, radial, vec):
         tensors_out[k] = new
@@ -353,7 +363,7 @@
         for copy in copies:
             copy.wait()
 
-    copy_rows(edge_rows, rows, step * (width // rows.shape[1]), gathered, width)
+    copy_rows(step, edge_rows, rows, gathered)
     incoming = jnp.concatenate(
         [
             gathered[pl.ds(j, width, stride=8), :].astype(BF16)
@@ -538,15 +548,11 @@
         return lax.ppermute(x, ("gx", "gy"), pairs)
 
     if plan.paired:
-        received = [
-            exchange(sends[0], plan.swaps[0]),
-            exchange(sends[1], plan.swaps[1]),
-            exchange(sends[2], plan.across),
-        ]
+        received = [exchange(sends[0], plan.swaps[0]), exchange(sends[1], plan.swaps[1]), None]
     else:
         received = [exchange(x, pairs) for x, pairs in zip(sends, plan.pairs)]
 
-    width = 512
+    width = 1024 if edges % 1024 == 0 else edges
     steps = edges // width
     row = pl.BlockSpec((1, 1, width), lambda i: (0, 0, i))
     flat = pl.BlockSpec((channels, width), lambda i: (0, i))
@@ -555,8 +561,9 @@
     last_weights = (w_expand, w_reverse, w_contract)
     inside = (
         scalars, tensors, w_mixing, w_invariant, vectors, species, table,
-        w_query, w_key, w_value, w_output, w_message, w_gate, w_radial,
+        w_query, w_output, w_key, w_value, w_message, w_gate, w_radial,
     )
+    stacked = [pltpu.VMEM((2 * channels, channels), BF16), pltpu.VMEM((channels + 6 * m, channels), BF16)]
     middle, message, t_inside = pl.pallas_call(
         interior_kernel,
         grid=(steps,),
@@ -573,7 +580,9 @@
             pltpu.VMEM((256, 128), BF16),
             pltpu.VMEM((channels, w_invariant.shape[0]), BF16),
         ]
-        + buffers(*inside),
+        + buffers(*inside)[:9]
+        + stacked
+        + [pltpu.SemaphoreType.DMA((len(inside),))],
         compiler_params=limit(36),
         cost_estimate=pl.CostEstimate(
             flops=2 * edges * edges * features, bytes_accessed=4 * edges * features, transcendentals=0
@@ -581,8 +590,9 @@
         name="interior",
     )(rows, *resident(*inside))
     if plan.paired:
-        first, middle = lax.optimization_barrier((received[0], middle))
+        first, own_side, middle = lax.optimization_barrier((received[0], sends[2], middle))
         received[0] = first
+        received[2] = exchange(own_side, plan.across)
         received.append(exchange(first, plan.across))
     s_inside = pl.pallas_call(
         incoming_kernel,

time: 41.5 us -> 37.6 us (0.906)
  Pallas kernels: 30.3 us -> 26.4 us
    pallas_call x1, Pallas kernels: 13.7 us -> 11.4 us  [per_device(): pl.pallas_call(interior_kernel, grid=(steps,), in_specs=[pl.BlockSpec(mem...]
    pallas_call x1, Pallas kernels: 6.5 us -> 5.12 us  [per_device(): pl.pallas_call(incoming_kernel, grid=(steps,), in_specs=[whole(channels,...]
  transfers between devices with their start and end apart: 5 -> 5, of which waited for: 1 -> 1; matrix products, arithmetic and copies ran while one was open for 0% -> 0% of each run, Pallas kernels for 49% -> 44%
where the time goes in v4:
time: 37.6 us; the launch traced here: 37.4 us
  Pallas kernels  26.4 us (70%)
  starting transfers between devices  8.21 us (22%)
  waiting for transfers between devices  1.83 us (5%)
  between operations  0.9 us (2%)
    pallas_call x1, Pallas kernels, per_device(): pl.pallas_call(interior_kernel, grid=(steps,), in_specs=[pl.BlockSpec(mem...  11.4 us
    ppermute x5, starting transfers between devices, exchange(): return lax.ppermute(x, ('gx', 'gy'), pairs)  8.21 us
    pallas_call x1, Pallas kernels, per_device(): pl.pallas_call(functools.partial(boundary_kernel, plan, block, edges), gr...  6.15 us
    pallas_call x1, Pallas kernels, per_device(): pl.pallas_call(incoming_kernel, grid=(steps,), in_specs=[whole(channels,...  5.12 us
    pallas_call x1, Pallas kernels, per_device(): pl.pallas_call(functools.partial(prepare_kernel, plan), in_specs=[hbm] *...  3.66 us
    ppermute x5, waiting for transfers between devices, exchange(): return lax.ppermute(x, ('gx', 'gy'), pairs)  1.83 us
  transfers between devices with their start and end apart: 5, of which 1 were waited for; matrix products, arithmetic and copies ran while one was open for 0% of the time, Pallas kernels for 44%

profile of v4, /device:TPU:0, one launch (start us, length us, event | category | flops | bytes accessed | tf_op | source)
XLA Modules:
  0.0 37.4 jit_solution(8596294772714793533)
XLA Ops:
  0.6 3.7 %prepare.1 = (bf16[848,512]{1,0:T(8,128)(2,1)S(1)}, f32[8,512]{1,0:T(8,128)S(1)}, s32[16,128]{1,0:T(8,128)S(1)}, bf16[1280,128]{1,0:T(8,128)(2,1)S(1)}, bf16[128...) custom-call(s32[1,1,8,64]{3,2,1,0:T(8,128)} %refs_0_.3, s32[1,1,8]{2,1,0:T(1,128)} %refs_1_.3, s32[1,1,2048]{2,1,0:T(1,128)} %refs_5_.3, ...), custom_call_target="tpu_custom_call" | custom-call | tf_op jit(solution)/shard_map/prepare/pallas_call | solution.py:529
  4.3 3.0 %collective-permute-start = (bf16[1280,128]{1,0:T(8,128)(2,1)S(1)}, bf16[1280,128]{1,0:T(8,128)(2,1)S(1)}, u32[]{:S(2)}, u32[]{:S(2)}) collective-permute-start(bf16[1280,128]{1,0:T(8,128)(2,1)S(1)} %get-tuple-element.16), channel_id=1, source_target_pairs={{0,2},{1,3},{2,0},{3,1},{4,6},{5,7},{6,4},{7,5},{8,10},{9,11},{10,... | collective-permute-start | bytes 983048 | tf_op jit(solution)/shard_map/ppermute | solution.py:548
  7.3 4.5 %collective-permute-start.1 = (bf16[1280,128]{1,0:T(8,128)(2,1)S(1)}, bf16[1280,128]{1,0:T(8,128)(2,1)S(1)}, u32[]{:S(2)}, u32[]{:S(2)}) collective-permute-start(bf16[1280,128]{1,0:T(8,128)(2,1)S(1)} %get-tuple-element.21), channel_id=1, source_target_pairs={{0,30},{1,31},{2,4},{3,5},{4,2},{5,3},{6,8},{7,9},{8,6},{9,7},{10,... | collective-permute-start | bytes 983048 | tf_op jit(solution)/shard_map/ppermute | solution.py:548
  11.9 11.4 %interior.1 = (bf16[256,2048]{1,0:T(8,128)(2,1)S(1)}, bf16[256,2048]{1,0:T(8,128)(2,1)S(1)}, bf16[9,64,2048]{2,1,0:T(8,128)(2,1)S(1)}) custom-call(s32[16,128]{1,0:T(8,128)S(1)} %get-tuple-element.18.rows, bf16[1,1,256,2048]{3,2,1,0:T(8,128)(2,1)} %refs_0_.4, bf16[1,1,9,64,2048]{4,3,2,1,0:T(8,128)(2,1)} %refs_1_.4, bf16[64,64]{1,0:T(8,128)(2,1)} %refs_19_.1, ...), custom_call_target="tpu_custom_call" | custom-call | flops 6979321856 | bytes 6815744 | tf_op jit(solution)/shard_map/interior/pallas_call | solution.py:567
  23.3 0.0 collective-permute-done.refs_0_
  23.3 0.0 copy-start
  23.3 0.0 copy-start.1
  23.3 0.0 copy-start.2
  23.3 0.0 copy-start.3
  23.4 0.0 copy-start.4
  23.4 0.0 copy-start.5
  23.4 0.0 copy-start.6
  23.4 0.0 copy-start.7
  23.4 0.0 copy-start.8
  23.4 0.0 copy-start.9
  23.4 0.0 copy-start.10
  23.4 0.0 copy-start.11
  23.5 0.0 copy-start.12
  23.5 0.0 copy-start.13
  23.5 5.1 %incoming.1.refs_8_ = bf16[256,2048]{1,0:T(8,128)(2,1)S(1)} custom-call(bf16[256,2048]{1,0:T(8,128)(2,1)S(1)} %get-tuple-element.22.message, bf16[256,2048]{1,0:T(8,128)(2,1)S(1)} %get-tuple-element.23.middle, s32[16,128]{1,0:T(8,128)S(1)} %get-tuple-element.18.rows, bf16[512,256]{1,0:T(8,128)(2,1)} %refs_20_.1, bf16[512,256]{1,0:T(8,128)(2,1)} %refs_21_.1, ...), custom_call_target="tpu_custom_call" | custom-call | flops 4294967296 | bytes 4194304 | tf_op jit(solution)/shard_map/incoming/pallas_call | solution.py:597
  28.6 0.0 collective-permute-done.1.refs_1_
  28.6 0.1 collective-permute-start.4
  28.7 0.5 %collective-permute-start.3 = (bf16[1280,128]{1,0:T(8,128)(2,1)S(1)}, bf16[1280,128]{1,0:T(8,128)(2,1)S(1)}, u32[]{:S(2)}, u32[]{:S(2)}) collective-permute-start(bf16[1280,128]{1,0:T(8,128)(2,1)S(1)} %collective-permute-done.refs_0_), channel_id=1, source_target_pairs={{0,1},{1,0},{2,3},{3,2},{4,5},{5,4},{6,7},{7,6},{8,9},{9,8},{10,11... | collective-permute-start | bytes 983048 | tf_op jit(solution)/shard_map/ppermute | solution.py:548
  29.2 0.1 collective-permute-start.2
  29.3 1.8 %collective-permute-done.2.refs_2_ = bf16[848,128]{1,0:T(8,128)(2,1)S(1)} collective-permute-done((bf16[848,128]{1,0:T(8,128)(2,1)S(1)}, bf16[848,128]{1,0:T(8,128)(2,1)S(1)}, u32[]{:S(2)}, u32[]{:S(2)}) %collective-permute-start.2) | collective-permute-done | bytes 217120 | tf_op jit(solution)/shard_map/ppermute | solution.py:548
  31.1 0.0 collective-permute-done.4.refs_4_
  31.1 0.0 collective-permute-done.3.refs_3_
  31.1 0.0 copy-done
  31.1 0.0 copy-done.1
  31.1 0.0 copy-done.2
  31.1 0.0 copy-done.3
  31.1 0.0 copy-done.4
  31.1 0.0 copy-done.5
  31.2 0.0 copy-done.6
  31.2 0.0 copy-done.7
  31.2 0.0 copy-done.8
  31.2 0.0 copy-done.9
  31.2 0.0 copy-done.10
  31.2 0.0 copy-done.11
  31.2 0.0 copy-done.12
  31.2 0.0 copy-done.13
  31.2 6.1 %boundary.1 = (bf16[1,1,256,2048]{3,2,1,0:T(8,128)(2,1)}, bf16[1,1,9,64,2048]{4,3,2,1,0:T(8,128)(2,1)}) custom-call(bf16[1280,128]{1,0:T(8,128)(2,1)S(1)} %collective-permute-done.refs_0_, bf16[1280,128]{1,0:T(8,128)(2,1)S(1)} %collective-permute-done.1.refs_1_, bf16[848,128]{1,0:T(8,128)(2,1)S(1)} %collective-permute-done.2.refs_2_, ...), custom_call_target="tpu_custom_call" | custom-call | flops 1744830464 | bytes 13631488 | tf_op jit(solution)/shard_map/boundary/pallas_call | solution.py:620
Async XLA Ops:
  4.3 19.0 %collective-permute-start = (bf16[1280,128]{1,0:T(8,128)(2,1)S(1)}, bf16[1280,128]{1,0:T(8,128)(2,1)S(1)}, u32[]{:S(2)}, u32[]{:S(2)}) collective-permute-start(bf16[1280,128]{1,0:T(8,128)(2,1)S(1)} %get-tuple-element.16), channel_id=1, source_target_pairs={{0,2},{1,3},{2,0},{3,1},{4,6},{5,7},{6,4},{7,5},{8,10},{9,11},{10,... | collective-permute-start | bytes 983048 | tf_op jit(solution)/shard_map/ppermute | solution.py:548
  7.3 21.3 %collective-permute-start.1 = (bf16[1280,128]{1,0:T(8,128)(2,1)S(1)}, bf16[1280,128]{1,0:T(8,128)(2,1)S(1)}, u32[]{:S(2)}, u32[]{:S(2)}) collective-permute-start(bf16[1280,128]{1,0:T(8,128)(2,1)S(1)} %get-tuple-element.21), channel_id=1, source_target_pairs={{0,30},{1,31},{2,4},{3,5},{4,2},{5,3},{6,8},{7,9},{8,6},{9,7},{10,... | collective-permute-start | bytes 983048 | tf_op jit(solution)/shard_map/ppermute | solution.py:548
  23.3 7.8 %copy-start = (bf16[512,256]{1,0:T(8,128)(2,1)S(1)}, bf16[512,256]{1,0:T(8,128)(2,1)}, u32[]{:S(2)}) copy-start(bf16[512,256]{1,0:T(8,128)(2,1)} %refs_20_.1) | copy-start | bytes 786436
  23.3 7.8 %copy-start.1 = (bf16[512,256]{1,0:T(8,128)(2,1)S(1)}, bf16[512,256]{1,0:T(8,128)(2,1)}, u32[]{:S(2)}) copy-start(bf16[512,256]{1,0:T(8,128)(2,1)} %refs_21_.1) | copy-start | bytes 786436
  23.3 7.8 %copy-start.2 = (bf16[256,512]{1,0:T(8,128)(2,1)S(1)}, bf16[256,512]{1,0:T(8,128)(2,1)}, u32[]{:S(2)}) copy-start(bf16[256,512]{1,0:T(8,128)(2,1)} %refs_22_.1) | copy-start | bytes 786436
  23.3 7.8 %copy-start.3 = (bf16[256,256]{1,0:T(8,128)(2,1)S(1)}, bf16[256,256]{1,0:T(8,128)(2,1)}, u32[]{:S(2)}) copy-start(bf16[256,256]{1,0:T(8,128)(2,1)} %refs_11_.3) | copy-start | bytes 393220
  23.4 7.8 %copy-start.4 = (bf16[256,256]{1,0:T(8,128)(2,1)S(1)}, bf16[256,256]{1,0:T(8,128)(2,1)}, u32[]{:S(2)}) copy-start(bf16[256,256]{1,0:T(8,128)(2,1)} %refs_14_.1) | copy-start | bytes 393220
  23.4 7.8 %copy-start.5 = (bf16[256,256]{1,0:T(8,128)(2,1)S(1)}, bf16[256,256]{1,0:T(8,128)(2,1)}, u32[]{:S(2)}) copy-start(bf16[256,256]{1,0:T(8,128)(2,1)} %refs_12_.3) | copy-start | bytes 393220
  23.4 7.8 %copy-start.6 = (bf16[256,256]{1,0:T(8,128)(2,1)S(1)}, bf16[256,256]{1,0:T(8,128)(2,1)}, u32[]{:S(2)}) copy-start(bf16[256,256]{1,0:T(8,128)(2,1)} %refs_13_.3) | copy-start | bytes 393220
  23.4 7.8 %copy-start.7 = (bf16[256,256]{1,0:T(8,128)(2,1)S(1)}, bf16[256,256]{1,0:T(8,128)(2,1)}, u32[]{:S(2)}) copy-start(bf16[256,256]{1,0:T(8,128)(2,1)} %refs_16_.1) | copy-start | bytes 393220
  23.4 7.8 %copy-start.8 = (bf16[256,192]{0,1:T(8,128)(2,1)S(1)}, bf16[256,192]{0,1:T(8,128)(2,1)}, u32[]{:S(2)}) copy-start(bf16[256,192]{0,1:T(8,128)(2,1)} %param.32) | copy-start | bytes 294916
  23.4 7.8 %copy-start.9 = (bf16[192,256]{1,0:T(8,128)(2,1)S(1)}, bf16[192,256]{1,0:T(8,128)(2,1)}, u32[]{:S(2)}) copy-start(bf16[192,256]{1,0:T(8,128)(2,1)} %refs_17_.1) | copy-start | bytes 294916
  23.4 7.8 %copy-start.10 = (bf16[192,256]{1,0:T(8,128)(2,1)S(1)}, bf16[192,256]{1,0:T(8,128)(2,1)}, u32[]{:S(2)}) copy-start(bf16[192,256]{1,0:T(8,128)(2,1)} %refs_18_.1) | copy-start | bytes 294916
  23.4 7.8 %copy-start.11 = (s32[1,1,2048]{2,1,0:T(1,128)S(1)}, s32[1,1,2048]{2,1,0:T(1,128)}, u32[]{:S(2)}) copy-start(s32[1,1,2048]{2,1,0:T(1,128)} %refs_7_.3) | copy-start | bytes 24580
  23.5 7.8 %copy-start.12 = (bf16[64,64]{1,0:T(8,128)(2,1)S(1)}, bf16[64,64]{1,0:T(8,128)(2,1)}, u32[]{:S(2)}) copy-start(bf16[64,64]{1,0:T(8,128)(2,1)} %refs_19_.1) | copy-start | bytes 24580
  23.5 7.8 %copy-start.13 = (f32[256,4]{0,1:T(4,128)S(1)}, f32[256,4]{0,1:T(4,128)}, u32[]{:S(2)}) copy-start(f32[256,4]{0,1:T(4,128)} %param.24) | copy-start | bytes 12292
  28.6 2.5 %collective-permute-start.4 = (bf16[1280,128]{1,0:T(8,128)(2,1)S(1)}, bf16[1280,128]{1,0:T(8,128)(2,1)S(1)}, u32[]{:S(2)}, u32[]{:S(2)}) collective-permute-start(bf16[1280,128]{1,0:T(8,128)(2,1)S(1)} %collective-permute-done.1.refs_1_), channel_id=1, source_target_pairs={{0,1},{1,0},{2,3},{3,2},{4,5},{5,4},{6,7},{7,6},{8,9},{9,8},{10,11... | collective-permute-start | bytes 983048 | tf_op jit(solution)/shard_map/ppermute | solution.py:548
  28.7 2.4 %collective-permute-start.3 = (bf16[1280,128]{1,0:T(8,128)(2,1)S(1)}, bf16[1280,128]{1,0:T(8,128)(2,1)S(1)}, u32[]{:S(2)}, u32[]{:S(2)}) collective-permute-start(bf16[1280,128]{1,0:T(8,128)(2,1)S(1)} %collective-permute-done.refs_0_), channel_id=1, source_target_pairs={{0,1},{1,0},{2,3},{3,2},{4,5},{5,4},{6,7},{7,6},{8,9},{9,8},{10,11... | collective-permute-start | bytes 983048 | tf_op jit(solution)/shard_map/ppermute | solution.py:548
  29.2 1.9 %collective-permute-start.2 = (bf16[848,128]{1,0:T(8,128)(2,1)S(1)}, bf16[848,128]{1,0:T(8,128)(2,1)S(1)}, u32[]{:S(2)}, u32[]{:S(2)}) collective-permute-start(bf16[848,128]{1,0:T(8,128)(2,1)S(1)} %get-tuple-element.25), channel_id=1, source_target_pairs={{0,1},{1,0},{2,3},{3,2},{4,5},{5,4},{6,7},{7,6},{8,9},{9,8},{10,11... | collective-permute-start | bytes 651272 | tf_op jit(solution)/shard_map/ppermute | solution.py:548

commit v5 on v4

--- a/solution.py
+++ b/solution.py
@@ -170,6 +170,7 @@
 def prepare_kernel(plan, *refs):
     inputs, own, where, rows, refs = refs[:7], refs[7], refs[8], refs[9], refs[10:]
     sends, buffers, sem = refs[: len(plan.arrays)], refs[len(plan.arrays) : -1], refs[-1]
+    onehot, *buffers = buffers
     copies = fetch(inputs, buffers, sem)
     send_index, counts, species, vectors, reverse, scalars, tensors = buffers
     channels, edges = scalars.shape[2:]
@@ -192,7 +193,7 @@
         axis=1,
     )
     slots = index.shape[1]
-    onehot = (lax.broadcasted_iota(jnp.int32, (edges, slots), 0) == index).astype(BF16)
+    onehot[...] = (lax.broadcasted_iota(jnp.int32, (edges, slots), 0) == index).astype(BF16)
     near = jnp.minimum(reverse[0], edges - 1) * 8
     rows[...] = jnp.concatenate(
         [near[:, j * 128 : (j + 1) * 128] for j in range(edges // 128)], axis=0
@@ -211,14 +212,16 @@
         ],
         axis=0,
     ).astype(BF16)
-    extra = mm(extra, onehot)
+    extra = mm(extra, onehot[...])
     where[0:3, :] = extra[7:10] + extra[10:13] + extra[13:16]
     where[3:8, :] = jnp.zeros((5, slots), F32)
     own[features:, :] = jnp.broadcast_to(extra[0:1], (EXTRA, slots)).astype(BF16)
     copies[5].wait()
-    own[:channels, :] = mm(scalars[0, 0], onehot).astype(BF16)
+    own[:channels, :] = mm(scalars[0, 0], onehot[...]).astype(BF16)
     copies[6].wait()
-    own[channels:features, :] = mm(tensors[0, 0].reshape(comps * m, edges), onehot).astype(BF16)
+    own[channels:features, :] = mm(
+        tensors[0, 0].reshape(comps * m, edges), onehot[...]
+    ).astype(BF16)
     half = features // 2
     for send, parts in zip(sends, plan.arrays):
         at = 0
@@ -267,7 +270,7 @@
         w_mid,
     ) = buffers
     edges = scalars.shape[-1]
-    width = middle_out.shape[-1]
+    width = gathered.shape[0] // 8
     channels = scalars.shape[2]
     comps, m = tensors.shape[2:4]
     step = pl.program_id(0)
@@ -333,22 +336,23 @@
         + mm(w_output[...], attended)
         + mm(w_shared[...], invariants(own_t, t_rev))
     ).astype(BF16)
-    middle_out[...] = middle
+    middle_out[:, here] = middle
     spread = mm(w_mid[...], middle)
-    message_out[...] = spread[:channels].astype(BF16)
+    message_out[:, here] = spread[:channels].astype(BF16)
     gate = jax.nn.sigmoid(spread[channels : channels + 3 * m])
     radial = spread[channels + 3 * m :]
     vec = jnp.concatenate([vectors[0, j, :, here] for j in range(3)], axis=0)
     for k, new in update_tensors(own_t, mixed, gate, radial, vec):
-        tensors_out[k] = new
-
-
-def incoming_kernel(message, middle, rows, *refs):
-    inputs, (scalars_out, edge_rows, gathered, *buffers, sem) = refs[:3], refs[3:]
-    w_expand, w_reverse, w_contract = buffers
+        tensors_out[k, :, here] = new
+
+
+def incoming_kernel(plan, block, message, middle, rows, *refs):
+    inputs, (scalars_out, merge, edge_rows, gathered, *buffers, sem) = refs[:4], refs[4:]
+    reverse, w_expand, w_reverse, w_contract = buffers
     channels, edges = message.shape
-    width = middle.shape[1]
+    width = gathered.shape[0] // 8
     step = pl.program_id(0)
+    here = pl.ds(pl.multiple_of(step * width, 128), width)
 
     @pl.when(step == 0)
     def _():
@@ -371,8 +375,15 @@
         ],
         axis=1,
     )
-    v = mm(w_expand[...], middle[...]) + nt(w_reverse[...], incoming)
-    scalars_out[...] = contract(middle[...], v, w_contract[...])
+    v = mm(w_expand[...], middle[:, here]) + nt(w_reverse[...], incoming)
+    scalars_out[:, here] = contract(middle[:, here], v, w_contract[...])
+    target = reverse[0, :, here] - edges
+    odd = lax.rem(lax.axis_index("gx"), 2) == 1
+    at = lax.broadcasted_iota(jnp.int32, (block, width), 0)
+    for j, (p, q) in enumerate(zip(*plan.orders)):
+        merge[j * block : (j + 1) * block, here] = (
+            at + pick(odd, (OPPOSITE[p], OPPOSITE[q])) * block == target
+        ).astype(BF16)
 
 
 def boundary_kernel(plan, block, edges, *refs):
@@ -381,6 +392,7 @@
     (
         own,
         where,
+        merge,
         reverse,
         scalars_in,
         tensors_in,
@@ -403,10 +415,10 @@
         t_new,
         far,
     ) = refs
-    odd = lax.rem(lax.axis_index("gx"), 2) == 1
     comps, m = tensors_in.shape[:2]
     channels = scalars_in.shape[0]
     features = channels + comps * m
+    slots = own.shape[1]
 
     @pl.when(pl.program_id(0) == 0)
     def _():
@@ -436,38 +448,43 @@
         e_far = embed(s_far, columns, far[features : features + 1, :].astype(F32))
         w_shared = nt(eye(channels), w_invariant[...]).astype(BF16)
         shared = mm(w_shared, invariants(t_own, t_far))
-        a_own = attend(mm(w_query[...], e_own), mm(w_key[...], s_far), mm(w_value[...], s_far))
-        a_far = attend(mm(w_query[...], e_far), mm(w_key[...], s_own), mm(w_value[...], s_own))
-        middle = (e_own.astype(F32) + mm(w_output[...], a_own) + shared).astype(BF16)
-        middle_far = (e_far.astype(F32) + mm(w_output[...], a_far) + shared).astype(BF16)
-        incoming = mm(w_message[...], middle_far).astype(BF16)
-        v = mm(w_expand[...], middle) + mm(w_reverse[...], incoming)
+        embedded = jnp.concatenate([e_own, e_far], axis=1)
+        w_rev = jnp.concatenate([w_key[...], w_value[...]], axis=0)
+        both = mm(w_rev, jnp.concatenate([s_far, s_own], axis=1))
+        attended = attend(mm(w_query[...], embedded), both[:channels], both[channels:])
+        middles = (
+            embedded.astype(F32)
+            + mm(w_output[...], attended)
+            + jnp.concatenate([shared, shared], axis=1)
+        ).astype(BF16)
+        middle = middles[:, :slots]
+        incoming = mm(w_message[...], middles[:, slots:]).astype(BF16)
+        w_mid = jnp.concatenate([w_expand[...], w_gate[...], w_radial[...]], axis=0)
+        spread = mm(w_mid, middle)
+        hidden = w_expand.shape[0]
+        v = spread[:hidden] + mm(w_reverse[...], incoming)
         s_new[...] = contract(middle, v, w_contract[...])
-        gate = jax.nn.sigmoid(mm(w_gate[...], middle))
-        radial = mm(w_radial[...], middle)
+        gate = jax.nn.sigmoid(spread[hidden : hidden + 3 * m])
+        radial = spread[hidden + 3 * m :]
         mixed = [mm(w_mixing[...], t_far[k]) for k in range(comps)]
         for k, new in update_tensors(t_own, mixed, gate, radial, where[...]):
             t_new[k * m : (k + 1) * m, :] = new
 
-    target = reverse[0] - edges
-    width = target.shape[1]
-    rows = lax.broadcasted_iota(jnp.int32, (block, width), 0)
-    onehot = jnp.concatenate(
-        [
-            (rows + pick(odd, (OPPOSITE[p], OPPOSITE[q])) * block == target).astype(F32)
-            for p, q in zip(*plan.orders)
-        ],
-        axis=0,
-    ).astype(BF16)
-    crosses = target >= 0
-    scalars_out[0, 0] = jnp.where(
-        crosses, mm(s_new[...], onehot), scalars_in[...].astype(F32)
-    ).astype(BF16)
-    merged = mm(t_new[...], onehot)
+    width = scalars_out.shape[-1]
+    here = pl.ds(pl.multiple_of(pl.program_id(0) * width, 128), width)
+    onehot = merge[:, here]
+    crosses = jnp.broadcast_to((reverse[0, :, here] >= edges).astype(F32), (m, width))
+    crosses = crosses.astype(BF16) > 0
+
+    def merged(new, old):
+        return jnp.where(crosses, new.astype(BF16), old)
+
+    s_all = mm(s_new[...], onehot)
+    for c in range(0, channels, m):
+        scalars_out[0, 0, c : c + m] = merged(s_all[c : c + m], scalars_in[c : c + m, here])
+    t_all = mm(t_new[...], onehot)
     for k in range(comps):
-        tensors_out[0, 0, k] = jnp.where(
-            crosses, merged[k * m : (k + 1) * m], tensors_in[k].astype(F32)
-        ).astype(BF16)
+        tensors_out[0, 0, k] = merged(t_all[k * m : (k + 1) * m], tensors_in[k, :, here])
 
 
 def resident(*arrays):
@@ -526,6 +543,7 @@
     prepared = (send_index, counts, species, vectors, reverse, scalars, tensors)
     prepared_buffers = buffers(*prepared)
     prepared_buffers[1] = pltpu.SMEM(counts.shape, counts.dtype)
+    prepared_buffers.insert(0, pltpu.VMEM((edges, slots), BF16))
     own, where, rows, *sends = pl.pallas_call(
         functools.partial(prepare_kernel, plan),
         in_specs=[hbm] * len(prepared),
@@ -554,9 +572,7 @@
 
     width = 1024 if edges % 1024 == 0 else edges
     steps = edges // width
-    row = pl.BlockSpec((1, 1, width), lambda i: (0, 0, i))
-    flat = pl.BlockSpec((channels, width), lambda i: (0, i))
-    stack = pl.BlockSpec((comps, m, width), lambda i: (0, 0, i))
+    flat = whole(channels, edges)
     first_weights = (w_query, w_key, w_value, w_output, w_invariant, w_message, w_gate, w_radial, w_mixing)
     last_weights = (w_expand, w_reverse, w_contract)
     inside = (
@@ -568,7 +584,7 @@
         interior_kernel,
         grid=(steps,),
         in_specs=[pl.BlockSpec(memory_space=pltpu.SMEM)] + [hbm] * len(inside),
-        out_specs=[flat, flat, stack],
+        out_specs=[flat, flat, whole(comps, m, edges)],
         out_shape=[
             jax.ShapeDtypeStruct((channels, edges), BF16),
             jax.ShapeDtypeStruct((channels, edges), BF16),
@@ -589,39 +605,42 @@
         ),
         name="interior",
     )(rows, *resident(*inside))
-    if plan.paired:
-        first, own_side, middle = lax.optimization_barrier((received[0], sends[2], middle))
-        received[0] = first
-        received[2] = exchange(own_side, plan.across)
-        received.append(exchange(first, plan.across))
-    s_inside = pl.pallas_call(
-        incoming_kernel,
+    last_weights = (w_expand, w_reverse, w_contract)
+    brought = (reverse, *last_weights)
+    s_inside, merge = pl.pallas_call(
+        functools.partial(incoming_kernel, plan, block),
         grid=(steps,),
         in_specs=[whole(channels, edges), flat, pl.BlockSpec(memory_space=pltpu.SMEM)]
-        + [hbm] * len(last_weights),
-        out_specs=flat,
-        out_shape=jax.ShapeDtypeStruct((channels, edges), BF16),
+        + [hbm] * len(brought),
+        out_specs=[flat, whole(slots, edges)],
+        out_shape=[
+            jax.ShapeDtypeStruct((channels, edges), BF16),
+            jax.ShapeDtypeStruct((slots, edges), BF16),
+        ],
         scratch_shapes=[
             pltpu.VMEM((edges * 8, 128), F32),
             pltpu.VMEM((width * 8, 128), F32),
         ]
-        + buffers(*last_weights),
+        + buffers(*brought),
         compiler_params=limit(24),
         cost_estimate=pl.CostEstimate(
             flops=4 * edges * edges * channels, bytes_accessed=8 * edges * channels, transcendentals=0
         ),
         name="incoming",
-    )(message, middle, rows, *resident(*last_weights))
+    )(message, middle, rows, *resident(*brought))
     if plan.paired:
-        second, s_inside = lax.optimization_barrier((received[1], s_inside))
-        received[1] = second
-        received.append(exchange(second, plan.across))
+        held = lax.optimization_barrier((received[0], received[1], sends[2], s_inside))
+        received[0], received[1], own_side, s_inside = held
+        received[2] = exchange(own_side, plan.across)
+        received.append(exchange(received[0], plan.across))
+        received.append(exchange(received[1], plan.across))
 
     return pl.pallas_call(
         functools.partial(boundary_kernel, plan, block, edges),
         grid=(steps,),
         in_specs=[whole(*r.shape) for r in received]
-        + [whole(*own.shape), whole(*where.shape), row, flat, stack, whole(*table.shape)]
+        + [whole(*own.shape), whole(*where.shape), whole(slots, edges)]
+        + [whole(*reverse.shape), flat, whole(comps, m, edges), whole(*table.shape)]
         + [whole(*w.shape) for w in first_weights + last_weights],
         out_specs=[
             pl.BlockSpec((1, 1, channels, width), lambda i: (0, 0, 0, i)),
@@ -641,7 +660,7 @@
             flops=2 * edges * slots * features, bytes_accessed=8 * edges * features, transcendentals=0
         ),
         name="boundary",
-    )(*received, own, where, reverse, s_inside, t_inside, table, *first_weights, *last_weights)
+    )(*received, own, where, merge, reverse, s_inside, t_inside, table, *first_weights, *last_weights)
 
 
 def solution(mesh):

time: 37.6 us -> 36.8 us (0.979)
  Pallas kernels: 26.4 us -> 25.6 us
    pallas_call x1, Pallas kernels: 6.15 us -> 5.58 us  [per_device(): pl.pallas_call(functools.partial(boundary_kernel, plan, block, edges), gr...]
  transfers between devices with their start and end apart: 5 -> 5, of which waited for: 1 -> 1; matrix products, arithmetic and copies ran while one was open for 0% -> 0% of each run, Pallas kernels for 44% -> 45%
where the time goes in v5:
time: 36.8 us; the launch traced here: 36.6 us
  Pallas kernels  25.6 us (70%)
  starting transfers between devices  8.21 us (22%)
  waiting for transfers between devices  1.83 us (5%)
  between operations  0.9 us (2%)
    pallas_call x1, Pallas kernels, per_device(): pl.pallas_call(interior_kernel, grid=(steps,), in_specs=[pl.BlockSpec(mem...  11.1 us
    ppermute x5, starting transfers between devices, exchange(): return lax.ppermute(x, ('gx', 'gy'), pairs)  8.21 us
    pallas_call x1, Pallas kernels, per_device(): pl.pallas_call(functools.partial(boundary_kernel, plan, block, edges), gr...  5.58 us
    pallas_call x1, Pallas kernels, per_device(): pl.pallas_call(functools.partial(incoming_kernel, plan, block), grid=(ste...  5.23 us
    pallas_call x1, Pallas kernels, per_device(): pl.pallas_call(functools.partial(prepare_kernel, plan), in_specs=[hbm] *...  3.66 us
    ppermute x5, waiting for transfers between devices, exchange(): return lax.ppermute(x, ('gx', 'gy'), pairs)  1.83 us
  transfers between devices with their start and end apart: 5, of which 1 were waited for; matrix products, arithmetic and copies ran while one was open for 0% of the time, Pallas kernels for 45%

profile of v5, /device:TPU:0, one launch (start us, length us, event | category | flops | bytes accessed | tf_op | source)
XLA Modules:
  0.0 36.6 jit_solution(10252840181539718034)
XLA Ops:
  0.6 3.7 %prepare.1 = (bf16[848,512]{1,0:T(8,128)(2,1)S(1)}, f32[8,512]{1,0:T(8,128)S(1)}, s32[16,128]{1,0:T(8,128)S(1)}, bf16[1280,128]{1,0:T(8,128)(2,1)S(1)}, bf16[128...) custom-call(s32[1,1,8,64]{3,2,1,0:T(8,128)} %refs_0_.3, s32[1,1,8]{2,1,0:T(1,128)} %refs_1_.3, s32[1,1,2048]{2,1,0:T(1,128)} %refs_5_.3, ...), custom_call_target="tpu_custom_call" | custom-call | tf_op jit(solution)/shard_map/prepare/pallas_call | solution.py:547
  4.3 3.0 %collective-permute-start = (bf16[1280,128]{1,0:T(8,128)(2,1)S(1)}, bf16[1280,128]{1,0:T(8,128)(2,1)S(1)}, u32[]{:S(2)}, u32[]{:S(2)}) collective-permute-start(bf16[1280,128]{1,0:T(8,128)(2,1)S(1)} %get-tuple-element.17), channel_id=1, source_target_pairs={{0,2},{1,3},{2,0},{3,1},{4,6},{5,7},{6,4},{7,5},{8,10},{9,11},{10,... | collective-permute-start | bytes 983048 | tf_op jit(solution)/shard_map/ppermute | solution.py:566
  7.3 4.5 %collective-permute-start.1 = (bf16[1280,128]{1,0:T(8,128)(2,1)S(1)}, bf16[1280,128]{1,0:T(8,128)(2,1)S(1)}, u32[]{:S(2)}, u32[]{:S(2)}) collective-permute-start(bf16[1280,128]{1,0:T(8,128)(2,1)S(1)} %get-tuple-element.18), channel_id=1, source_target_pairs={{0,30},{1,31},{2,4},{3,5},{4,2},{5,3},{6,8},{7,9},{8,6},{9,7},{10,... | collective-permute-start | bytes 983048 | tf_op jit(solution)/shard_map/ppermute | solution.py:566
  11.9 11.1 %interior.1 = (bf16[256,2048]{1,0:T(8,128)(2,1)S(1)}, bf16[256,2048]{1,0:T(8,128)(2,1)S(1)}, bf16[9,64,2048]{2,1,0:T(8,128)(2,1)S(1)}) custom-call(s32[16,128]{1,0:T(8,128)S(1)} %get-tuple-element.20.rows, bf16[1,1,256,2048]{3,2,1,0:T(8,128)(2,1)} %refs_0_.4, bf16[1,1,9,64,2048]{4,3,2,1,0:T(8,128)(2,1)} %refs_1_.4, bf16[64,64]{1,0:T(8,128)(2,1)} %refs_20_.1, ...), custom_call_target="tpu_custom_call" | custom-call | flops 6979321856 | bytes 6815744 | tf_op jit(solution)/shard_map/interior/pallas_call | solution.py:583
  23.0 0.0 copy-start
  23.0 0.0 copy-start.1
  23.0 0.0 copy-start.2
  23.0 0.0 copy-start.3
  23.0 0.0 copy-start.4
  23.1 0.0 copy-start.5
  23.1 0.0 copy-start.6
  23.1 0.0 copy-start.7
  23.1 0.0 copy-start.8
  23.1 0.0 copy-start.9
  23.1 0.0 copy-start.10
  23.1 0.0 copy-start.11
  23.1 0.0 copy-start.12
  23.2 0.0 copy-start.13
  23.2 5.2 %incoming.1 = (bf16[256,2048]{1,0:T(8,128)(2,1)S(1)}, bf16[512,2048]{1,0:T(8,128)(2,1)S(1)}) custom-call(bf16[256,2048]{1,0:T(8,128)(2,1)S(1)} %get-tuple-element.21.message, bf16[256,2048]{1,0:T(8,128)(2,1)S(1)} %get-tuple-element.22.middle, s32[16,128]{1,0:T(8,128)S(1)} %get-tuple-element.20.rows, s32[1,1,2048]{2,1,0:T(1,128)} %refs_8_.3, ...), custom_call_target="tpu_custom_call" | custom-call | flops 4294967296 | bytes 4194304 | tf_op jit(solution)/shard_map/incoming/pallas_call | solution.py:610
  28.4 0.0 collective-permute-done.refs_0_
  28.4 0.0 collective-permute-done.1.refs_1_
  28.4 0.1 collective-permute-start.3
  28.5 0.5 %collective-permute-start.4 = (bf16[1280,128]{1,0:T(8,128)(2,1)S(1)}, bf16[1280,128]{1,0:T(8,128)(2,1)S(1)}, u32[]{:S(2)}, u32[]{:S(2)}) collective-permute-start(bf16[1280,128]{1,0:T(8,128)(2,1)S(1)} %collective-permute-done.1.refs_1_), channel_id=1, source_target_pairs={{0,1},{1,0},{2,3},{3,2},{4,5},{5,4},{6,7},{7,6},{8,9},{9,8},{10,11... | collective-permute-start | bytes 983048 | tf_op jit(solution)/shard_map/ppermute | solution.py:566
  29.0 0.1 collective-permute-start.2
  29.1 1.8 %collective-permute-done.2.refs_2_ = bf16[848,128]{1,0:T(8,128)(2,1)S(1)} collective-permute-done((bf16[848,128]{1,0:T(8,128)(2,1)S(1)}, bf16[848,128]{1,0:T(8,128)(2,1)S(1)}, u32[]{:S(2)}, u32[]{:S(2)}) %collective-permute-start.2) | collective-permute-done | bytes 217120 | tf_op jit(solution)/shard_map/ppermute | solution.py:566
  30.9 0.0 collective-permute-done.3.refs_3_
  30.9 0.0 collective-permute-done.4.refs_4_
  30.9 0.0 copy-done
  30.9 0.0 copy-done.1
  30.9 0.0 copy-done.2
  30.9 0.0 copy-done.3
  30.9 0.0 copy-done.4
  30.9 0.0 copy-done.5
  31.0 0.0 copy-done.6
  31.0 0.0 copy-done.7
  31.0 0.0 copy-done.8
  31.0 0.0 copy-done.9
  31.0 0.0 copy-done.10
  31.0 0.0 copy-done.11
  31.0 0.0 copy-done.12
  31.0 0.0 copy-done.13
  31.0 5.6 %boundary.1 = (bf16[1,1,256,2048]{3,2,1,0:T(8,128)(2,1)}, bf16[1,1,9,64,2048]{4,3,2,1,0:T(8,128)(2,1)}) custom-call(bf16[1280,128]{1,0:T(8,128)(2,1)S(1)} %collective-permute-done.refs_0_, bf16[1280,128]{1,0:T(8,128)(2,1)S(1)} %collective-permute-done.1.refs_1_, bf16[848,128]{1,0:T(8,128)(2,1)S(1)} %collective-permute-done.2.refs_2_, ...), custom_call_target="tpu_custom_call" | custom-call | flops 1744830464 | bytes 13631488 | tf_op jit(solution)/shard_map/boundary/pallas_call | solution.py:638
Async XLA Ops:
  4.3 24.1 %collective-permute-start = (bf16[1280,128]{1,0:T(8,128)(2,1)S(1)}, bf16[1280,128]{1,0:T(8,128)(2,1)S(1)}, u32[]{:S(2)}, u32[]{:S(2)}) collective-permute-start(bf16[1280,128]{1,0:T(8,128)(2,1)S(1)} %get-tuple-element.17), channel_id=1, source_target_pairs={{0,2},{1,3},{2,0},{3,1},{4,6},{5,7},{6,4},{7,5},{8,10},{9,11},{10,... | collective-permute-start | bytes 983048 | tf_op jit(solution)/shard_map/ppermute | solution.py:566
  7.3 21.1 %collective-permute-start.1 = (bf16[1280,128]{1,0:T(8,128)(2,1)S(1)}, bf16[1280,128]{1,0:T(8,128)(2,1)S(1)}, u32[]{:S(2)}, u32[]{:S(2)}) collective-permute-start(bf16[1280,128]{1,0:T(8,128)(2,1)S(1)} %get-tuple-element.18), channel_id=1, source_target_pairs={{0,30},{1,31},{2,4},{3,5},{4,2},{5,3},{6,8},{7,9},{8,6},{9,7},{10,... | collective-permute-start | bytes 983048 | tf_op jit(solution)/shard_map/ppermute | solution.py:566
  23.0 7.9 %copy-start = (bf16[512,256]{1,0:T(8,128)(2,1)S(1)}, bf16[512,256]{1,0:T(8,128)(2,1)}, u32[]{:S(2)}) copy-start(bf16[512,256]{1,0:T(8,128)(2,1)} %refs_21_.1) | copy-start | bytes 786436
  23.0 7.9 %copy-start.1 = (bf16[512,256]{1,0:T(8,128)(2,1)S(1)}, bf16[512,256]{1,0:T(8,128)(2,1)}, u32[]{:S(2)}) copy-start(bf16[512,256]{1,0:T(8,128)(2,1)} %refs_22_.1) | copy-start | bytes 786436
  23.0 7.9 %copy-start.2 = (bf16[256,512]{1,0:T(8,128)(2,1)S(1)}, bf16[256,512]{1,0:T(8,128)(2,1)}, u32[]{:S(2)}) copy-start(bf16[256,512]{1,0:T(8,128)(2,1)} %refs_23_.1) | copy-start | bytes 786436
  23.0 7.9 %copy-start.3 = (bf16[256,256]{1,0:T(8,128)(2,1)S(1)}, bf16[256,256]{1,0:T(8,128)(2,1)}, u32[]{:S(2)}) copy-start(bf16[256,256]{1,0:T(8,128)(2,1)} %refs_12_.3) | copy-start | bytes 393220
  23.0 7.9 %copy-start.4 = (bf16[256,256]{1,0:T(8,128)(2,1)S(1)}, bf16[256,256]{1,0:T(8,128)(2,1)}, u32[]{:S(2)}) copy-start(bf16[256,256]{1,0:T(8,128)(2,1)} %refs_15_.1) | copy-start | bytes 393220
  23.1 7.9 %copy-start.5 = (bf16[256,256]{1,0:T(8,128)(2,1)S(1)}, bf16[256,256]{1,0:T(8,128)(2,1)}, u32[]{:S(2)}) copy-start(bf16[256,256]{1,0:T(8,128)(2,1)} %refs_13_.3) | copy-start | bytes 393220
  23.1 7.9 %copy-start.6 = (bf16[256,256]{1,0:T(8,128)(2,1)S(1)}, bf16[256,256]{1,0:T(8,128)(2,1)}, u32[]{:S(2)}) copy-start(bf16[256,256]{1,0:T(8,128)(2,1)} %refs_14_.1) | copy-start | bytes 393220
  23.1 7.9 %copy-start.7 = (bf16[256,256]{1,0:T(8,128)(2,1)S(1)}, bf16[256,256]{1,0:T(8,128)(2,1)}, u32[]{:S(2)}) copy-start(bf16[256,256]{1,0:T(8,128)(2,1)} %refs_17_.1) | copy-start | bytes 393220
  23.1 7.9 %copy-start.8 = (bf16[256,192]{0,1:T(8,128)(2,1)S(1)}, bf16[256,192]{0,1:T(8,128)(2,1)}, u32[]{:S(2)}) copy-start(bf16[256,192]{0,1:T(8,128)(2,1)} %param.32) | copy-start | bytes 294916
  23.1 7.9 %copy-start.9 = (bf16[192,256]{1,0:T(8,128)(2,1)S(1)}, bf16[192,256]{1,0:T(8,128)(2,1)}, u32[]{:S(2)}) copy-start(bf16[192,256]{1,0:T(8,128)(2,1)} %refs_18_.1) | copy-start | bytes 294916
  23.1 7.9 %copy-start.10 = (bf16[192,256]{1,0:T(8,128)(2,1)S(1)}, bf16[192,256]{1,0:T(8,128)(2,1)}, u32[]{:S(2)}) copy-start(bf16[192,256]{1,0:T(8,128)(2,1)} %refs_19_.1) | copy-start | bytes 294916
  23.1 7.9 %copy-start.11 = (s32[1,1,2048]{2,1,0:T(1,128)S(1)}, s32[1,1,2048]{2,1,0:T(1,128)}, u32[]{:S(2)}) copy-start(s32[1,1,2048]{2,1,0:T(1,128)} %refs_8_.3) | copy-start | bytes 24580
  23.1 7.9 %copy-start.12 = (bf16[64,64]{1,0:T(8,128)(2,1)S(1)}, bf16[64,64]{1,0:T(8,128)(2,1)}, u32[]{:S(2)}) copy-start(bf16[64,64]{1,0:T(8,128)(2,1)} %refs_20_.1) | copy-start | bytes 24580
  23.2 7.9 %copy-start.13 = (f32[256,4]{0,1:T(4,128)S(1)}, f32[256,4]{0,1:T(4,128)}, u32[]{:S(2)}) copy-start(f32[256,4]{0,1:T(4,128)} %param.24) | copy-start | bytes 12292
  28.4 2.5 %collective-permute-start.3 = (bf16[1280,128]{1,0:T(8,128)(2,1)S(1)}, bf16[1280,128]{1,0:T(8,128)(2,1)S(1)}, u32[]{:S(2)}, u32[]{:S(2)}) collective-permute-start(bf16[1280,128]{1,0:T(8,128)(2,1)S(1)} %collective-permute-done.refs_0_), channel_id=1, source_target_pairs={{0,1},{1,0},{2,3},{3,2},{4,5},{5,4},{6,7},{7,6},{8,9},{9,8},{10,11... | collective-permute-start | bytes 983048 | tf_op jit(solution)/shard_map/ppermute | solution.py:566
  28.5 2.4 %collective-permute-start.4 = (bf16[1280,128]{1,0:T(8,128)(2,1)S(1)}, bf16[1280,128]{1,0:T(8,128)(2,1)S(1)}, u32[]{:S(2)}, u32[]{:S(2)}) collective-permute-start(bf16[1280,128]{1,0:T(8,128)(2,1)S(1)} %collective-permute-done.1.refs_1_), channel_id=1, source_target_pairs={{0,1},{1,0},{2,3},{3,2},{4,5},{5,4},{6,7},{7,6},{8,9},{9,8},{10,11... | collective-permute-start | bytes 983048 | tf_op jit(solution)/shard_map/ppermute | solution.py:566
  29.0 1.9 %collective-permute-start.2 = (bf16[848,128]{1,0:T(8,128)(2,1)S(1)}, bf16[848,128]{1,0:T(8,128)(2,1)S(1)}, u32[]{:S(2)}, u32[]{:S(2)}) collective-permute-start(bf16[848,128]{1,0:T(8,128)(2,1)S(1)} %get-tuple-element.26), channel_id=1, source_target_pairs={{0,1},{1,0},{2,3},{3,2},{4,5},{5,4},{6,7},{7,6},{8,9},{9,8},{10,11... | collective-permute-start | bytes 651272 | tf_op jit(solution)/shard_map/ppermute | solution.py:566

commit v6 on v5

--- a/solution.py
+++ b/solution.py
@@ -168,11 +168,10 @@
 
 
 def prepare_kernel(plan, *refs):
-    inputs, own, where, rows, refs = refs[:7], refs[7], refs[8], refs[9], refs[10:]
-    sends, buffers, sem = refs[: len(plan.arrays)], refs[len(plan.arrays) : -1], refs[-1]
-    onehot, *buffers = buffers
-    copies = fetch(inputs, buffers, sem)
-    send_index, counts, species, vectors, reverse, scalars, tensors = buffers
+    inputs, (own, where, rows, scalars, tensors), refs = refs[:7], refs[7:12], refs[12:]
+    sends, (onehot, *buffers, sem) = refs[: len(plan.arrays)], refs[len(plan.arrays) :]
+    copies = fetch(inputs, (*buffers, scalars, tensors), sem)
+    send_index, counts, species, vectors, reverse = buffers
     channels, edges = scalars.shape[2:]
     comps, m = tensors.shape[2:4]
     block = send_index.shape[-1]
@@ -252,13 +251,11 @@
                 gathered[e * 8 : e * 8 + 8, :] = table[source, :]
 
 
-def interior_kernel(rows, *refs):
-    inputs, refs = refs[:14], refs[14:]
+def interior_kernel(rows, scalars, tensors, *refs):
+    inputs, refs = refs[:12], refs[12:]
     middle_out, message_out, tensors_out, edge_rows, gathered, pair_mix, w_shared, *refs = refs
     buffers, sem = refs[:-1], refs[-1]
     (
-        scalars,
-        tensors,
         w_mixing,
         w_invariant,
         vectors,
@@ -288,11 +285,9 @@
             for c in range(0, piece.shape[0], 128):
                 edge_rows[pl.ds(at * 8 + j + c // 128, 256, stride=8), :] = turned[:, c : c + 128]
 
-        copies[0].wait()
         for at in range(0, edges, 256):
             for c in range(0, channels, 256):
                 turn(at, c // 128, scalars[0, 0, c : c + 256, at : at + 256])
-        copies[1].wait()
         for at in range(0, edges, 256):
             n = 0
             while n < len(pairs):
@@ -301,7 +296,7 @@
                 piece = tensors[0, 0, k : k + 2 * taken, :, at : at + 256].reshape(-1, 256)
                 turn(at, channels // 128 + n, piece)
                 n += taken
-        for copy in copies[2:]:
+        for copy in copies:
             copy.wait()
         mixing = w_mixing[...].astype(F32)
         zero = jnp.zeros((m, m), F32)
@@ -542,16 +537,19 @@
 
     prepared = (send_index, counts, species, vectors, reverse, scalars, tensors)
     prepared_buffers = buffers(*prepared)
+    del prepared_buffers[5:7]
     prepared_buffers[1] = pltpu.SMEM(counts.shape, counts.dtype)
     prepared_buffers.insert(0, pltpu.VMEM((edges, slots), BF16))
-    own, where, rows, *sends = pl.pallas_call(
+    own, where, rows, scalars, tensors, *sends = pl.pallas_call(
         functools.partial(prepare_kernel, plan),
         in_specs=[hbm] * len(prepared),
-        out_specs=[vmem] * (3 + len(plan.arrays)),
+        out_specs=[vmem] * (5 + len(plan.arrays)),
         out_shape=[
             jax.ShapeDtypeStruct((features + EXTRA, slots), BF16),
             jax.ShapeDtypeStruct((8, slots), F32),
             jax.ShapeDtypeStruct((edges // 128, 128), jnp.int32),
+            jax.ShapeDtypeStruct(scalars.shape, BF16),
+            jax.ShapeDtypeStruct(tensors.shape, BF16),
         ]
         + [
             jax.ShapeDtypeStruct((plan.rows(parts, features), 2 * block), BF16)
@@ -566,7 +564,11 @@
         return lax.ppermute(x, ("gx", "gy"), pairs)
 
     if plan.paired:
-        received = [exchange(sends[0], plan.swaps[0]), exchange(sends[1], plan.swaps[1]), None]
+        received = [
+            exchange(sends[0], plan.swaps[0]),
+            exchange(sends[1], plan.swaps[1]),
+            exchange(sends[2], plan.across),
+        ]
     else:
         received = [exchange(x, pairs) for x, pairs in zip(sends, plan.pairs)]
 
@@ -576,14 +578,16 @@
     first_weights = (w_query, w_key, w_value, w_output, w_invariant, w_message, w_gate, w_radial, w_mixing)
     last_weights = (w_expand, w_reverse, w_contract)
     inside = (
-        scalars, tensors, w_mixing, w_invariant, vectors, species, table,
+        w_mixing, w_invariant, vectors, species, table,
         w_query, w_output, w_key, w_value, w_message, w_gate, w_radial,
     )
     stacked = [pltpu.VMEM((2 * channels, channels), BF16), pltpu.VMEM((channels + 6 * m, channels), BF16)]
     middle, message, t_inside = pl.pallas_call(
         interior_kernel,
         grid=(steps,),
-        in_specs=[pl.BlockSpec(memory_space=pltpu.SMEM)] + [hbm] * len(inside),
+        in_specs=[pl.BlockSpec(memory_space=pltpu.SMEM)]
+        + [whole(*scalars.shape), whole(*tensors.shape)]
+        + [hbm] * len(inside),
         out_specs=[flat, flat, whole(comps, m, edges)],
         out_shape=[
             jax.ShapeDtypeStruct((channels, edges), BF16),
@@ -596,7 +600,7 @@
             pltpu.VMEM((256, 128), BF16),
             pltpu.VMEM((channels, w_invariant.shape[0]), BF16),
         ]
-        + buffers(*inside)[:9]
+        + buffers(*inside)[:7]
         + stacked
         + [pltpu.SemaphoreType.DMA((len(inside),))],
         compiler_params=limit(36),
@@ -604,7 +608,7 @@
             flops=2 * edges * edges * features, bytes_accessed=4 * edges * features, transcendentals=0
         ),
         name="interior",
-    )(rows, *resident(*inside))
+    )(rows, scalars, tensors, *resident(*inside))
     last_weights = (w_expand, w_reverse, w_contract)
     brought = (reverse, *last_weights)
     s_inside, merge = pl.pallas_call(
@@ -629,9 +633,8 @@
         name="incoming",
     )(message, middle, rows, *resident(*brought))
     if plan.paired:
-        held = lax.optimization_barrier((received[0], received[1], sends[2], s_inside))
-        received[0], received[1], own_side, s_inside = held
-        received[2] = exchange(own_side, plan.across)
+        held = lax.optimization_barrier((received[0], received[1], s_inside))
+        received[0], received[1], s_inside = held
         received.append(exchange(received[0], plan.across))
         received.append(exchange(received[1], plan.across))
 

time: 36.8 us -> 35.4 us (0.962)
  Pallas kernels: 25.6 us -> 24.2 us
    pallas_call x1, Pallas kernels: 11.1 us -> 9.68 us  [per_device(): pl.pallas_call(interior_kernel, grid=(steps,), in_specs=[pl.BlockSpec(mem...]
  transfers between devices with their start and end apart: 5 -> 5, of which waited for: 1 -> 1; matrix products, arithmetic and copies ran while one was open for 0% -> 0% of each run, Pallas kernels for 45% -> 42%
where the time goes in v6:
time: 35.4 us; the launch traced here: 35.2 us
  Pallas kernels  24.2 us (68%)
  starting transfers between devices  8.21 us (23%)
  waiting for transfers between devices  1.83 us (5%)
  between operations  0.9 us (3%)
    pallas_call x1, Pallas kernels, per_device(): pl.pallas_call(interior_kernel, grid=(steps,), in_specs=[pl.BlockSpec(mem...  9.68 us
    ppermute x5, starting transfers between devices, exchange(): return lax.ppermute(x, ('gx', 'gy'), pairs)  8.21 us
    pallas_call x1, Pallas kernels, per_device(): pl.pallas_call(functools.partial(boundary_kernel, plan, block, edges), gr...  5.58 us
    pallas_call x1, Pallas kernels, per_device(): pl.pallas_call(functools.partial(incoming_kernel, plan, block), grid=(ste...  5.23 us
    pallas_call x1, Pallas kernels, per_device(): pl.pallas_call(functools.partial(prepare_kernel, plan), in_specs=[hbm] *...  3.67 us
    ppermute x5, waiting for transfers between devices, exchange(): return lax.ppermute(x, ('gx', 'gy'), pairs)  1.83 us
  transfers between devices with their start and end apart: 5, of which 1 were waited for; matrix products, arithmetic and copies ran while one was open for 0% of the time, Pallas kernels for 42%

profile of v6, /device:TPU:0, one launch (start us, length us, event | category | flops | bytes accessed | tf_op | source)
XLA Modules:
  0.0 35.2 jit_solution(12217974797116098074)
XLA Ops:
  0.6 3.7 %prepare.1 = (bf16[848,512]{1,0:T(8,128)(2,1)S(1)}, f32[8,512]{1,0:T(8,128)S(1)}, s32[16,128]{1,0:T(8,128)S(1)}, bf16[1,1,256,2048]{3,2,1,0:T(8,128)(2,1)S(1)}, ...) custom-call(s32[1,1,8,64]{3,2,1,0:T(8,128)} %refs_0_.3, ...), custom_call_target="tpu_custom_call" | custom-call | tf_op jit(solution)/shard_map/prepare/pallas_call | solution.py:543
  4.3 3.0 %collective-permute-start = (bf16[1280,128]{1,0:T(8,128)(2,1)S(1)}, bf16[1280,128]{1,0:T(8,128)(2,1)S(1)}, u32[]{:S(2)}, u32[]{:S(2)}) collective-permute-start(bf16[1280,128]{1,0:T(8,128)(2,1)S(1)} %get-tuple-element.18), channel_id=1, source_target_pairs={{0,2},{1,3},{2,0},{3,1},{4,6},{5,7},{6,4},{7,5},{8,10},{9,11},{10,... | collective-permute-start | bytes 983048 | tf_op jit(solution)/shard_map/ppermute | solution.py:564
  7.3 4.5 %collective-permute-start.1 = (bf16[1280,128]{1,0:T(8,128)(2,1)S(1)}, bf16[1280,128]{1,0:T(8,128)(2,1)S(1)}, u32[]{:S(2)}, u32[]{:S(2)}) collective-permute-start(bf16[1280,128]{1,0:T(8,128)(2,1)S(1)} %get-tuple-element.19), channel_id=1, source_target_pairs={{0,30},{1,31},{2,4},{3,5},{4,2},{5,3},{6,8},{7,9},{8,6},{9,7},{10,... | collective-permute-start | bytes 983048 | tf_op jit(solution)/shard_map/ppermute | solution.py:564
  11.9 9.7 %interior.1 = (bf16[256,2048]{1,0:T(8,128)(2,1)S(1)}, bf16[256,2048]{1,0:T(8,128)(2,1)S(1)}, bf16[9,64,2048]{2,1,0:T(8,128)(2,1)S(1)}) custom-call(s32[16,128]{1,0:T(8,128)S(1)} %get-tuple-element.20.rows, bf16[1,1,256,2048]{3,2,1,0:T(8,128)(2,1)S(1)} %get-tuple-element.21.scalars, bf16[1,1,9,64,2048]{4,3,2,1,0:T(8,128)(2,1)S(1)} %get-tuple-element.22.tensors, ...), custom_call_target="tpu_custom_call" | custom-call | flops 6979321856 | bytes 6815744 | tf_op jit(solution)/shard_map/interior/pallas_call | solution.py:585
  21.6 0.0 copy-start
  21.6 0.0 copy-start.1
  21.6 0.0 copy-start.2
  21.6 0.0 copy-start.3
  21.6 0.0 copy-start.4
  21.6 0.0 copy-start.5
  21.6 0.0 copy-start.6
  21.6 0.0 copy-start.7
  21.6 0.0 copy-start.8
  21.7 0.0 copy-start.9
  21.7 0.0 copy-start.10
  21.7 0.0 copy-start.11
  21.7 0.0 copy-start.12
  21.7 0.0 copy-start.13
  21.7 5.2 %incoming.1 = (bf16[256,2048]{1,0:T(8,128)(2,1)S(1)}, bf16[512,2048]{1,0:T(8,128)(2,1)S(1)}) custom-call(bf16[256,2048]{1,0:T(8,128)(2,1)S(1)} %get-tuple-element.23.message, bf16[256,2048]{1,0:T(8,128)(2,1)S(1)} %get-tuple-element.24.middle, s32[16,128]{1,0:T(8,128)S(1)} %get-tuple-element.20.rows, s32[1,1,2048]{2,1,0:T(1,128)} %refs_8_.3, ...), custom_call_target="tpu_custom_call" | custom-call | flops 4294967296 | bytes 4194304 | tf_op jit(solution)/shard_map/incoming/pallas_call | solution.py:614
  27.0 0.0 collective-permute-done.refs_0_
  27.0 0.0 collective-permute-done.1.refs_1_
  27.0 0.1 collective-permute-start.3
  27.1 0.5 %collective-permute-start.4 = (bf16[1280,128]{1,0:T(8,128)(2,1)S(1)}, bf16[1280,128]{1,0:T(8,128)(2,1)S(1)}, u32[]{:S(2)}, u32[]{:S(2)}) collective-permute-start(bf16[1280,128]{1,0:T(8,128)(2,1)S(1)} %collective-permute-done.1.refs_1_), channel_id=1, source_target_pairs={{0,1},{1,0},{2,3},{3,2},{4,5},{5,4},{6,7},{7,6},{8,9},{9,8},{10,11... | collective-permute-start | bytes 983048 | tf_op jit(solution)/shard_map/ppermute | solution.py:564
  27.6 0.1 collective-permute-start.2
  27.6 1.8 %collective-permute-done.2.refs_2_ = bf16[848,128]{1,0:T(8,128)(2,1)S(1)} collective-permute-done((bf16[848,128]{1,0:T(8,128)(2,1)S(1)}, bf16[848,128]{1,0:T(8,128)(2,1)S(1)}, u32[]{:S(2)}, u32[]{:S(2)}) %collective-permute-start.2) | collective-permute-done | bytes 217120 | tf_op jit(solution)/shard_map/ppermute | solution.py:564
  29.5 0.0 collective-permute-done.3.refs_3_
  29.5 0.0 collective-permute-done.4.refs_4_
  29.5 0.0 copy-done
  29.5 0.0 copy-done.1
  29.5 0.0 copy-done.2
  29.5 0.0 copy-done.3
  29.5 0.0 copy-done.4
  29.5 0.0 copy-done.5
  29.5 0.0 copy-done.6
  29.5 0.0 copy-done.7
  29.5 0.0 copy-done.8
  29.5 0.0 copy-done.9
  29.6 0.0 copy-done.10
  29.6 0.0 copy-done.11
  29.6 0.0 copy-done.12
  29.6 0.0 copy-done.13
  29.6 5.6 %boundary.1 = (bf16[1,1,256,2048]{3,2,1,0:T(8,128)(2,1)}, bf16[1,1,9,64,2048]{4,3,2,1,0:T(8,128)(2,1)}) custom-call(bf16[1280,128]{1,0:T(8,128)(2,1)S(1)} %collective-permute-done.refs_0_, bf16[1280,128]{1,0:T(8,128)(2,1)S(1)} %collective-permute-done.1.refs_1_, bf16[848,128]{1,0:T(8,128)(2,1)S(1)} %collective-permute-done.2.refs_2_, ...), custom_call_target="tpu_custom_call" | custom-call | flops 1744830464 | bytes 13631488 | tf_op jit(solution)/shard_map/boundary/pallas_call | solution.py:641
Async XLA Ops:
  4.3 22.7 %collective-permute-start = (bf16[1280,128]{1,0:T(8,128)(2,1)S(1)}, bf16[1280,128]{1,0:T(8,128)(2,1)S(1)}, u32[]{:S(2)}, u32[]{:S(2)}) collective-permute-start(bf16[1280,128]{1,0:T(8,128)(2,1)S(1)} %get-tuple-element.18), channel_id=1, source_target_pairs={{0,2},{1,3},{2,0},{3,1},{4,6},{5,7},{6,4},{7,5},{8,10},{9,11},{10,... | collective-permute-start | bytes 983048 | tf_op jit(solution)/shard_map/ppermute | solution.py:564
  7.3 19.6 %collective-permute-start.1 = (bf16[1280,128]{1,0:T(8,128)(2,1)S(1)}, bf16[1280,128]{1,0:T(8,128)(2,1)S(1)}, u32[]{:S(2)}, u32[]{:S(2)}) collective-permute-start(bf16[1280,128]{1,0:T(8,128)(2,1)S(1)} %get-tuple-element.19), channel_id=1, source_target_pairs={{0,30},{1,31},{2,4},{3,5},{4,2},{5,3},{6,8},{7,9},{8,6},{9,7},{10,... | collective-permute-start | bytes 983048 | tf_op jit(solution)/shard_map/ppermute | solution.py:564
  21.6 7.9 %copy-start = (bf16[512,256]{1,0:T(8,128)(2,1)S(1)}, bf16[512,256]{1,0:T(8,128)(2,1)}, u32[]{:S(2)}) copy-start(bf16[512,256]{1,0:T(8,128)(2,1)} %refs_21_.1) | copy-start | bytes 786436
  21.6 7.9 %copy-start.1 = (bf16[512,256]{1,0:T(8,128)(2,1)S(1)}, bf16[512,256]{1,0:T(8,128)(2,1)}, u32[]{:S(2)}) copy-start(bf16[512,256]{1,0:T(8,128)(2,1)} %refs_22_.1) | copy-start | bytes 786436
  21.6 7.9 %copy-start.2 = (bf16[256,512]{1,0:T(8,128)(2,1)S(1)}, bf16[256,512]{1,0:T(8,128)(2,1)}, u32[]{:S(2)}) copy-start(bf16[256,512]{1,0:T(8,128)(2,1)} %refs_23_.1) | copy-start | bytes 786436
  21.6 7.9 %copy-start.3 = (bf16[256,256]{1,0:T(8,128)(2,1)S(1)}, bf16[256,256]{1,0:T(8,128)(2,1)}, u32[]{:S(2)}) copy-start(bf16[256,256]{1,0:T(8,128)(2,1)} %refs_12_.1) | copy-start | bytes 393220
  21.6 7.9 %copy-start.4 = (bf16[256,256]{1,0:T(8,128)(2,1)S(1)}, bf16[256,256]{1,0:T(8,128)(2,1)}, u32[]{:S(2)}) copy-start(bf16[256,256]{1,0:T(8,128)(2,1)} %refs_15_.1) | copy-start | bytes 393220
  21.6 7.9 %copy-start.5 = (bf16[256,256]{1,0:T(8,128)(2,1)S(1)}, bf16[256,256]{1,0:T(8,128)(2,1)}, u32[]{:S(2)}) copy-start(bf16[256,256]{1,0:T(8,128)(2,1)} %refs_13_.1) | copy-start | bytes 393220
  21.6 7.9 %copy-start.6 = (bf16[256,256]{1,0:T(8,128)(2,1)S(1)}, bf16[256,256]{1,0:T(8,128)(2,1)}, u32[]{:S(2)}) copy-start(bf16[256,256]{1,0:T(8,128)(2,1)} %refs_14_.1) | copy-start | bytes 393220
  21.6 7.9 %copy-start.7 = (bf16[256,256]{1,0:T(8,128)(2,1)S(1)}, bf16[256,256]{1,0:T(8,128)(2,1)}, u32[]{:S(2)}) copy-start(bf16[256,256]{1,0:T(8,128)(2,1)} %refs_17_.1) | copy-start | bytes 393220
  21.6 7.9 %copy-start.8 = (bf16[256,192]{0,1:T(8,128)(2,1)S(1)}, bf16[256,192]{0,1:T(8,128)(2,1)}, u32[]{:S(2)}) copy-start(bf16[256,192]{0,1:T(8,128)(2,1)} %param.32) | copy-start | bytes 294916
  21.7 7.9 %copy-start.9 = (bf16[192,256]{1,0:T(8,128)(2,1)S(1)}, bf16[192,256]{1,0:T(8,128)(2,1)}, u32[]{:S(2)}) copy-start(bf16[192,256]{1,0:T(8,128)(2,1)} %refs_18_.1) | copy-start | bytes 294916
  21.7 7.9 %copy-start.10 = (bf16[192,256]{1,0:T(8,128)(2,1)S(1)}, bf16[192,256]{1,0:T(8,128)(2,1)}, u32[]{:S(2)}) copy-start(bf16[192,256]{1,0:T(8,128)(2,1)} %refs_19_.1) | copy-start | bytes 294916
  21.7 7.9 %copy-start.11 = (s32[1,1,2048]{2,1,0:T(1,128)S(1)}, s32[1,1,2048]{2,1,0:T(1,128)}, u32[]{:S(2)}) copy-start(s32[1,1,2048]{2,1,0:T(1,128)} %refs_8_.3) | copy-start | bytes 24580
  21.7 7.9 %copy-start.12 = (bf16[64,64]{1,0:T(8,128)(2,1)S(1)}, bf16[64,64]{1,0:T(8,128)(2,1)}, u32[]{:S(2)}) copy-start(bf16[64,64]{1,0:T(8,128)(2,1)} %refs_20_.1) | copy-start | bytes 24580
  21.7 7.9 %copy-start.13 = (f32[256,4]{0,1:T(4,128)S(1)}, f32[256,4]{0,1:T(4,128)}, u32[]{:S(2)}) copy-start(f32[256,4]{0,1:T(4,128)} %param.24) | copy-start | bytes 12292
  27.0 2.5 %collective-permute-start.3 = (bf16[1280,128]{1,0:T(8,128)(2,1)S(1)}, bf16[1280,128]{1,0:T(8,128)(2,1)S(1)}, u32[]{:S(2)}, u32[]{:S(2)}) collective-permute-start(bf16[1280,128]{1,0:T(8,128)(2,1)S(1)} %collective-permute-done.refs_0_), channel_id=1, source_target_pairs={{0,1},{1,0},{2,3},{3,2},{4,5},{5,4},{6,7},{7,6},{8,9},{9,8},{10,11... | collective-permute-start | bytes 983048 | tf_op jit(solution)/shard_map/ppermute | solution.py:564
  27.1 2.4 %collective-permute-start.4 = (bf16[1280,128]{1,0:T(8,128)(2,1)S(1)}, bf16[1280,128]{1,0:T(8,128)(2,1)S(1)}, u32[]{:S(2)}, u32[]{:S(2)}) collective-permute-start(bf16[1280,128]{1,0:T(8,128)(2,1)S(1)} %collective-permute-done.1.refs_1_), channel_id=1, source_target_pairs={{0,1},{1,0},{2,3},{3,2},{4,5},{5,4},{6,7},{7,6},{8,9},{9,8},{10,11... | collective-permute-start | bytes 983048 | tf_op jit(solution)/shard_map/ppermute | solution.py:564
  27.6 1.9 %collective-permute-start.2 = (bf16[848,128]{1,0:T(8,128)(2,1)S(1)}, bf16[848,128]{1,0:T(8,128)(2,1)S(1)}, u32[]{:S(2)}, u32[]{:S(2)}) collective-permute-start(bf16[848,128]{1,0:T(8,128)(2,1)S(1)} %get-tuple-element.28), channel_id=1, source_target_pairs={{0,1},{1,0},{2,3},{3,2},{4,5},{5,4},{6,7},{7,6},{8,9},{9,8},{10,11... | collective-permute-start | bytes 651272 | tf_op jit(solution)/shard_map/ppermute | solution.py:564

commit v7 on v6

--- a/solution.py
+++ b/solution.py
@@ -381,17 +381,8 @@
         ).astype(BF16)
 
 
-def boundary_kernel(plan, block, edges, *refs):
-    count = len(plan.parts)
-    received, refs = refs[:count], refs[count:]
+def settle(plan, block, positions, base, received, own, where, table, weights, far, s_new, t_new):
     (
-        own,
-        where,
-        merge,
-        reverse,
-        scalars_in,
-        tensors_in,
-        table,
         w_query,
         w_key,
         w_value,
@@ -404,80 +395,104 @@
         w_expand,
         w_reverse,
         w_contract,
-        scalars_out,
-        tensors_out,
-        s_new,
-        t_new,
-        far,
-    ) = refs
+    ) = weights
+    m = w_mixing.shape[0]
+    channels = w_query.shape[0]
+    comps = t_new.shape[0] // m
+    features = channels + comps * m
+    columns = slice(positions[0] * block, (positions[-1] + 1) * block)
+    slots = len(positions) * block
+
+    def block_of(g, part, n):
+        kind, _ = plan.parts[g][part]
+        at = plan.offset(plan.parts[g], part, features)
+        if kind == "wide":
+            return received[g - base][at : at + features + EXTRA, n * block : (n + 1) * block]
+        half = features // 2
+        upper = received[g - base][at : at + half, :]
+        extra = received[g - base][at + half : at + half + EXTRA, :block]
+        return jnp.concatenate([upper[:, :block], upper[:, block:], extra], axis=0)
+
+    for j in range(0, len(positions), 2):
+        to = slice(j * block, (j + 2) * block)
+        (g, part, n), second = (plan.facing[p] for p in positions[j : j + 2])
+        if n == 0 and second == (g, part, 1):
+            at = plan.offset(plan.parts[g], part, features)
+            far[:, to] = received[g - base][at : at + features + EXTRA, :]
+        else:
+            far[:, to] = jnp.concatenate([block_of(g, part, n), block_of(*second)], axis=1)
+    s_own, s_far = own[:channels, columns], far[:channels, :]
+    t_own = [own[channels + k * m : channels + (k + 1) * m, columns] for k in range(comps)]
+    t_far = [far[channels + k * m : channels + (k + 1) * m, :] for k in range(comps)]
+    picks = jnp.transpose(table[...])
+    e_own = embed(s_own, picks, own[features : features + 1, columns].astype(F32))
+    e_far = embed(s_far, picks, far[features : features + 1, :].astype(F32))
+    w_shared = nt(eye(channels), w_invariant[...]).astype(BF16)
+    shared = mm(w_shared, invariants(t_own, t_far))
+    embedded = jnp.concatenate([e_own, e_far], axis=1)
+    w_rev = jnp.concatenate([w_key[...], w_value[...]], axis=0)
+    both = mm(w_rev, jnp.concatenate([s_far, s_own], axis=1))
+    attended = attend(mm(w_query[...], embedded), both[:channels], both[channels:])
+    middles = (
+        embedded.astype(F32)
+        + mm(w_output[...], attended)
+        + jnp.concatenate([shared, shared], axis=1)
+    ).astype(BF16)
+    middle = middles[:, :slots]
+    incoming = mm(w_message[...], middles[:, slots:]).astype(BF16)
+    w_mid = jnp.concatenate([w_expand[...], w_gate[...], w_radial[...]], axis=0)
+    spread = mm(w_mid, middle)
+    hidden = w_expand.shape[0]
+    v = spread[:hidden] + mm(w_reverse[...], incoming)
+    s_new[...] = contract(middle, v, w_contract[...])
+    gate = jax.nn.sigmoid(spread[hidden : hidden + 3 * m])
+    radial = spread[hidden + 3 * m :]
+    mixed = [mm(w_mixing[...], t_far[k]) for k in range(comps)]
+    for k, new in update_tensors(t_own, mixed, gate, radial, where[:, columns]):
+        t_new[k * m : (k + 1) * m, :] = new
+
+
+def near_kernel(plan, block, positions, *refs):
+    received, (own, where, table, *refs) = refs[:3], refs[3:]
+    weights, (s_new, t_new, far) = refs[:12], refs[12:]
+    settle(plan, block, positions, 0, received, own, where, table, weights, far, s_new, t_new)
+
+
+def boundary_kernel(plan, block, positions, base, count, done, edges, *refs):
+    received, refs = refs[:count], refs[count:]
+    settled, (own, where, merge, reverse, scalars_in, tensors_in, table, *refs) = (
+        refs[:done],
+        refs[done:],
+    )
+    weights, (scalars_out, tensors_out, s_new, t_new, far) = refs[:12], refs[12:]
     comps, m = tensors_in.shape[:2]
     channels = scalars_in.shape[0]
-    features = channels + comps * m
-    slots = own.shape[1]
 
     @pl.when(pl.program_id(0) == 0)
     def _():
-        def block_of(g, part, n):
-            kind, _ = plan.parts[g][part]
-            at = plan.offset(plan.parts[g], part, features)
-            if kind == "wide":
-                return received[g][at : at + features + EXTRA, n * block : (n + 1) * block]
-            half = features // 2
-            upper = received[g][at : at + half, :]
-            extra = received[g][at + half : at + half + EXTRA, :block]
-            return jnp.concatenate([upper[:, :block], upper[:, block:], extra], axis=0)
-
-        for j in range(0, len(plan.facing), 2):
-            to = slice(j * block, (j + 2) * block)
-            (g, part, n), second = plan.facing[j : j + 2]
-            if n == 0 and second == (g, part, 1):
-                at = plan.offset(plan.parts[g], part, features)
-                far[:, to] = received[g][at : at + features + EXTRA, :]
-            else:
-                far[:, to] = jnp.concatenate([block_of(g, part, n), block_of(*second)], axis=1)
-        s_own, s_far = own[:channels, :], far[:channels, :]
-        t_own = [own[channels + k * m : channels + (k + 1) * m, :] for k in range(comps)]
-        t_far = [far[channels + k * m : channels + (k + 1) * m, :] for k in range(comps)]
-        columns = jnp.transpose(table[...])
-        e_own = embed(s_own, columns, own[features : features + 1, :].astype(F32))
-        e_far = embed(s_far, columns, far[features : features + 1, :].astype(F32))
-        w_shared = nt(eye(channels), w_invariant[...]).astype(BF16)
-        shared = mm(w_shared, invariants(t_own, t_far))
-        embedded = jnp.concatenate([e_own, e_far], axis=1)
-        w_rev = jnp.concatenate([w_key[...], w_value[...]], axis=0)
-        both = mm(w_rev, jnp.concatenate([s_far, s_own], axis=1))
-        attended = attend(mm(w_query[...], embedded), both[:channels], both[channels:])
-        middles = (
-            embedded.astype(F32)
-            + mm(w_output[...], attended)
-            + jnp.concatenate([shared, shared], axis=1)
-        ).astype(BF16)
-        middle = middles[:, :slots]
-        incoming = mm(w_message[...], middles[:, slots:]).astype(BF16)
-        w_mid = jnp.concatenate([w_expand[...], w_gate[...], w_radial[...]], axis=0)
-        spread = mm(w_mid, middle)
-        hidden = w_expand.shape[0]
-        v = spread[:hidden] + mm(w_reverse[...], incoming)
-        s_new[...] = contract(middle, v, w_contract[...])
-        gate = jax.nn.sigmoid(spread[hidden : hidden + 3 * m])
-        radial = spread[hidden + 3 * m :]
-        mixed = [mm(w_mixing[...], t_far[k]) for k in range(comps)]
-        for k, new in update_tensors(t_own, mixed, gate, radial, where[...]):
-            t_new[k * m : (k + 1) * m, :] = new
+        settle(
+            plan, block, positions, base, received, own, where, table, weights, far, s_new, t_new
+        )
 
     width = scalars_out.shape[-1]
     here = pl.ds(pl.multiple_of(pl.program_id(0) * width, 128), width)
-    onehot = merge[:, here]
+    first = len(positions) * block
     crosses = jnp.broadcast_to((reverse[0, :, here] >= edges).astype(F32), (m, width))
     crosses = crosses.astype(BF16) > 0
 
+    def spread(new, n):
+        total = mm(new[...], merge[:first, here])
+        if done:
+            total = total + mm(settled[n][...], merge[first:, here])
+        return total
+
     def merged(new, old):
         return jnp.where(crosses, new.astype(BF16), old)
 
-    s_all = mm(s_new[...], onehot)
+    s_all = spread(s_new, 0)
     for c in range(0, channels, m):
         scalars_out[0, 0, c : c + m] = merged(s_all[c : c + m], scalars_in[c : c + m, here])
-    t_all = mm(t_new[...], onehot)
+    t_all = spread(t_new, 1)
     for k in range(comps):
         tensors_out[0, 0, k] = merged(t_all[k * m : (k + 1) * m], tensors_in[k, :, here])
 
@@ -635,13 +650,35 @@
     if plan.paired:
         held = lax.optimization_barrier((received[0], received[1], s_inside))
         received[0], received[1], s_inside = held
-        received.append(exchange(received[0], plan.across))
-        received.append(exchange(received[1], plan.across))
-
+        relayed = [exchange(received[0], plan.across), exchange(received[1], plan.across)]
+        positions, near = tuple(range(4)), tuple(range(4, 8))
+        columns = len(near) * block
+        settled = pl.pallas_call(
+            functools.partial(near_kernel, plan, block, near),
+            in_specs=[vmem] * (6 + len(first_weights + last_weights)),
+            out_specs=[vmem, vmem],
+            out_shape=[
+                jax.ShapeDtypeStruct((channels, columns), BF16),
+                jax.ShapeDtypeStruct((comps * m, columns), BF16),
+            ],
+            scratch_shapes=[pltpu.VMEM((features + EXTRA, columns), BF16)],
+            compiler_params=limit(16),
+            cost_estimate=pl.CostEstimate(
+                flops=4 * columns * channels * features, bytes_accessed=4 * columns * features, transcendentals=0
+            ),
+            name="near",
+        )(*received, own, where, table, *first_weights, *last_weights)
+        base, received = 3, relayed
+    else:
+        positions, base, settled = tuple(range(len(DIRECTIONS))), 0, []
+
+    columns = len(positions) * block
     return pl.pallas_call(
-        functools.partial(boundary_kernel, plan, block, edges),
+        functools.partial(
+            boundary_kernel, plan, block, positions, base, len(received), len(settled), edges
+        ),
         grid=(steps,),
-        in_specs=[whole(*r.shape) for r in received]
+        in_specs=[whole(*r.shape) for r in (*received, *settled)]
         + [whole(*own.shape), whole(*where.shape), whole(slots, edges)]
         + [whole(*reverse.shape), flat, whole(comps, m, edges), whole(*table.shape)]
         + [whole(*w.shape) for w in first_weights + last_weights],
@@ -650,20 +687,23 @@
             pl.BlockSpec((1, 1, comps, m, width), lambda i: (0, 0, 0, 0, i)),
         ],
         out_shape=[
-            jax.ShapeDtypeStruct(scalars.shape, BF16),
-            jax.ShapeDtypeStruct(tensors.shape, BF16),
+            jax.ShapeDtypeStruct((1, 1, channels, edges), BF16),
+            jax.ShapeDtypeStruct((1, 1, comps, m, edges), BF16),
         ],
         scratch_shapes=[
-            pltpu.VMEM((channels, slots), BF16),
-            pltpu.VMEM((comps * m, slots), BF16),
-            pltpu.VMEM((features + EXTRA, slots), BF16),
+            pltpu.VMEM((channels, columns), BF16),
+            pltpu.VMEM((comps * m, columns), BF16),
+            pltpu.VMEM((features + EXTRA, columns), BF16),
         ],
         compiler_params=limit(26),
         cost_estimate=pl.CostEstimate(
             flops=2 * edges * slots * features, bytes_accessed=8 * edges * features, transcendentals=0
         ),
         name="boundary",
-    )(*received, own, where, merge, reverse, s_inside, t_inside, table, *first_weights, *last_weights)
+    )(
+        *received, *settled, own, where, merge, reverse, s_inside, t_inside, table,
+        *first_weights, *last_weights,
+    )
 
 
 def solution(mesh):

time: 35.4 us -> 36.6 us (1.034)
  Pallas kernels: 24.2 us -> 25.4 us
    pallas_call x1 -> x2, Pallas kernels: 5.58 us -> 6.87 us  [the longest x1 4.98 us: per_device(): pl.pallas_call(functools.partial(boundary_kernel, plan, block, positions,...]
  transfers between devices with their start and end apart: 5 -> 5, of which waited for: 1 -> 1; matrix products, arithmetic and copies ran while one was open for 0% -> 0% of each run, Pallas kernels for 42% -> 46%
where the time goes in v7:
time: 36.6 us; the launch traced here: 36.5 us
  Pallas kernels  25.4 us (69%)
  starting transfers between devices  8.21 us (22%)
  waiting for transfers between devices  1.83 us (5%)
  between operations  0.9 us (2%)
    pallas_call x1, Pallas kernels, per_device(): pl.pallas_call(interior_kernel, grid=(steps,), in_specs=[pl.BlockSpec(mem...  9.68 us
    ppermute x5, starting transfers between devices, exchange(): return lax.ppermute(x, ('gx', 'gy'), pairs)  8.21 us
    pallas_call x1, Pallas kernels, per_device(): pl.pallas_call(functools.partial(incoming_kernel, plan, block), grid=(ste...  5.23 us
    pallas_call x1, Pallas kernels, per_device(): pl.pallas_call(functools.partial(boundary_kernel, plan, block, positions,...  4.98 us
    pallas_call x1, Pallas kernels, per_device(): pl.pallas_call(functools.partial(prepare_kernel, plan), in_specs=[hbm] *...  3.67 us
    pallas_call x1, Pallas kernels, per_device(): pl.pallas_call(functools.partial(near_kernel, plan, block, near), in_spec...  1.89 us
    ppermute x5, waiting for transfers between devices, exchange(): return lax.ppermute(x, ('gx', 'gy'), pairs)  1.83 us
  transfers between devices with their start and end apart: 5, of which 1 were waited for; matrix products, arithmetic and copies ran while one was open for 0% of the time, Pallas kernels for 46%

profile of v7, /device:TPU:0, one launch (start us, length us, event | category | flops | bytes accessed | tf_op | source)
XLA Modules:
  0.0 36.5 jit_solution(3855420539963925237)
XLA Ops:
  0.6 3.7 %prepare.1 = (bf16[848,512]{1,0:T(8,128)(2,1)S(1)}, f32[8,512]{1,0:T(8,128)S(1)}, s32[16,128]{1,0:T(8,128)S(1)}, bf16[1,1,256,2048]{3,2,1,0:T(8,128)(2,1)S(1)}, ...) custom-call(s32[1,1,8,64]{3,2,1,0:T(8,128)} %refs_0_.3, ...), custom_call_target="tpu_custom_call" | custom-call | tf_op jit(solution)/shard_map/prepare/pallas_call | solution.py:558
  4.3 3.0 %collective-permute-start = (bf16[1280,128]{1,0:T(8,128)(2,1)S(1)}, bf16[1280,128]{1,0:T(8,128)(2,1)S(1)}, u32[]{:S(2)}, u32[]{:S(2)}) collective-permute-start(bf16[1280,128]{1,0:T(8,128)(2,1)S(1)} %get-tuple-element.20), channel_id=1, source_target_pairs={{0,2},{1,3},{2,0},{3,1},{4,6},{5,7},{6,4},{7,5},{8,10},{9,11},{10,... | collective-permute-start | bytes 983048 | tf_op jit(solution)/shard_map/ppermute | solution.py:579
  7.3 4.5 %collective-permute-start.1 = (bf16[1280,128]{1,0:T(8,128)(2,1)S(1)}, bf16[1280,128]{1,0:T(8,128)(2,1)S(1)}, u32[]{:S(2)}, u32[]{:S(2)}) collective-permute-start(bf16[1280,128]{1,0:T(8,128)(2,1)S(1)} %get-tuple-element.21), channel_id=1, source_target_pairs={{0,30},{1,31},{2,4},{3,5},{4,2},{5,3},{6,8},{7,9},{8,6},{9,7},{10,... | collective-permute-start | bytes 983048 | tf_op jit(solution)/shard_map/ppermute | solution.py:579
  11.9 9.7 %interior.1 = (bf16[256,2048]{1,0:T(8,128)(2,1)S(1)}, bf16[256,2048]{1,0:T(8,128)(2,1)S(1)}, bf16[9,64,2048]{2,1,0:T(8,128)(2,1)S(1)}) custom-call(s32[16,128]{1,0:T(8,128)S(1)} %get-tuple-element.22.rows, bf16[1,1,256,2048]{3,2,1,0:T(8,128)(2,1)S(1)} %get-tuple-element.23.scalars, bf16[1,1,9,64,2048]{4,3,2,1,0:T(8,128)(2,1)S(1)} %get-tuple-element.24.tensors, ...), custom_call_target="tpu_custom_call" | custom-call | flops 6979321856 | bytes 6815744 | tf_op jit(solution)/shard_map/interior/pallas_call | solution.py:600
  21.6 0.0 copy-start
  21.6 0.0 copy-start.1
  21.6 0.0 copy-start.2
  21.6 0.0 copy-start.3
  21.6 0.0 copy-start.4
  21.6 0.0 copy-start.5
  21.6 0.0 copy-start.6
  21.6 0.0 copy-start.7
  21.6 0.0 copy-start.8
  21.7 0.0 copy-start.9
  21.7 0.0 copy-start.10
  21.7 0.0 copy-start.11
  21.7 0.0 copy-start.13
  21.7 5.2 %incoming.1 = (bf16[256,2048]{1,0:T(8,128)(2,1)S(1)}, bf16[512,2048]{1,0:T(8,128)(2,1)S(1)}) custom-call(bf16[256,2048]{1,0:T(8,128)(2,1)S(1)} %get-tuple-element.25.message, bf16[256,2048]{1,0:T(8,128)(2,1)S(1)} %get-tuple-element.26.middle, s32[16,128]{1,0:T(8,128)S(1)} %get-tuple-element.22.rows, s32[1,1,2048]{2,1,0:T(1,128)} %refs_7_.5, ...), custom_call_target="tpu_custom_call" | custom-call | flops 4294967296 | bytes 4194304 | tf_op jit(solution)/shard_map/incoming/pallas_call | solution.py:629
  26.9 0.0 copy-start.12
  27.0 0.0 collective-permute-done.refs_0_
  27.0 0.0 collective-permute-done.1.refs_1_
  27.0 0.1 collective-permute-start.2
  27.1 0.5 %collective-permute-start.3 = (bf16[1280,128]{1,0:T(8,128)(2,1)S(1)}, bf16[1280,128]{1,0:T(8,128)(2,1)S(1)}, u32[]{:S(2)}, u32[]{:S(2)}) collective-permute-start(bf16[1280,128]{1,0:T(8,128)(2,1)S(1)} %collective-permute-done.1.refs_1_), channel_id=1, source_target_pairs={{0,1},{1,0},{2,3},{3,2},{4,5},{5,4},{6,7},{7,6},{8,9},{9,8},{10,11... | collective-permute-start | bytes 983048 | tf_op jit(solution)/shard_map/ppermute | solution.py:579
  27.6 0.1 collective-permute-start.4
  27.6 1.8 %collective-permute-done.4.refs_2_ = bf16[848,128]{1,0:T(8,128)(2,1)S(1)} collective-permute-done((bf16[848,128]{1,0:T(8,128)(2,1)S(1)}, bf16[848,128]{1,0:T(8,128)(2,1)S(1)}, u32[]{:S(2)}, u32[]{:S(2)}) %collective-permute-start.4) | collective-permute-done | bytes 217120 | tf_op jit(solution)/shard_map/ppermute | solution.py:579
  29.4 0.0 copy-done
  29.5 0.0 copy-done.1
  29.5 0.0 copy-done.2
  29.5 0.0 copy-done.3
  29.5 0.0 copy-done.4
  29.5 0.0 copy-done.5
  29.5 0.0 copy-done.6
  29.5 0.0 copy-done.7
  29.5 0.0 copy-done.8
  29.5 0.0 copy-done.9
  29.5 0.0 copy-done.10
  29.5 0.0 copy-done.11
  29.6 0.0 copy-done.13
  29.6 1.9 %near.1 = (bf16[256,256]{1,0:T(8,128)(2,1)S(1)}, bf16[576,256]{1,0:T(8,128)(2,1)S(1)}) custom-call(bf16[1280,128]{1,0:T(8,128)(2,1)S(1)} %collective-permute-done.refs_0_, bf16[1280,128]{1,0:T(8,128)(2,1)S(1)} %collective-permute-done.1.refs_1_, bf16[848,128]{1,0:T(8,128)(2,1)S(1)} %collective-permute-done.4.refs_2_, ...), custom_call_target="tpu_custom_call" | custom-call | flops 218103808 | bytes 851968 | tf_op jit(solution)/shard_map/near/pallas_call | solution.py:656
  31.5 0.0 collective-permute-done.2.refs_0_
  31.5 0.0 collective-permute-done.3.refs_1_
  31.5 0.0 copy-done.12
  31.5 5.0 %boundary.1 = (bf16[1,1,256,2048]{3,2,1,0:T(8,128)(2,1)}, bf16[1,1,9,64,2048]{4,3,2,1,0:T(8,128)(2,1)}) custom-call(bf16[1280,128]{1,0:T(8,128)(2,1)S(1)} %collective-permute-done.2.refs_0_, bf16[1280,128]{1,0:T(8,128)(2,1)S(1)} %collective-permute-done.3.refs_1_, bf16[256,256]{1,0:T(8,128)(2,1)S(1)} %get-tuple-element.33.refs_2_, ...), custom_call_target="tpu_custom_call" | custom-call | flops 1744830464 | bytes 13631488 | tf_op jit(solution)/shard_map/boundary/pallas_call | solution.py:676
Async XLA Ops:
  4.3 22.7 %collective-permute-start = (bf16[1280,128]{1,0:T(8,128)(2,1)S(1)}, bf16[1280,128]{1,0:T(8,128)(2,1)S(1)}, u32[]{:S(2)}, u32[]{:S(2)}) collective-permute-start(bf16[1280,128]{1,0:T(8,128)(2,1)S(1)} %get-tuple-element.20), channel_id=1, source_target_pairs={{0,2},{1,3},{2,0},{3,1},{4,6},{5,7},{6,4},{7,5},{8,10},{9,11},{10,... | collective-permute-start | bytes 983048 | tf_op jit(solution)/shard_map/ppermute | solution.py:579
  7.3 19.6 %collective-permute-start.1 = (bf16[1280,128]{1,0:T(8,128)(2,1)S(1)}, bf16[1280,128]{1,0:T(8,128)(2,1)S(1)}, u32[]{:S(2)}, u32[]{:S(2)}) collective-permute-start(bf16[1280,128]{1,0:T(8,128)(2,1)S(1)} %get-tuple-element.21), channel_id=1, source_target_pairs={{0,30},{1,31},{2,4},{3,5},{4,2},{5,3},{6,8},{7,9},{8,6},{9,7},{10,... | collective-permute-start | bytes 983048 | tf_op jit(solution)/shard_map/ppermute | solution.py:579
  21.6 7.9 %copy-start = (bf16[512,256]{1,0:T(8,128)(2,1)S(1)}, bf16[512,256]{1,0:T(8,128)(2,1)}, u32[]{:S(2)}) copy-start(bf16[512,256]{1,0:T(8,128)(2,1)} %refs_20_.1) | copy-start | bytes 786436
  21.6 7.9 %copy-start.1 = (bf16[512,256]{1,0:T(8,128)(2,1)S(1)}, bf16[512,256]{1,0:T(8,128)(2,1)}, u32[]{:S(2)}) copy-start(bf16[512,256]{1,0:T(8,128)(2,1)} %refs_21_.1) | copy-start | bytes 786436
  21.6 7.9 %copy-start.2 = (bf16[256,512]{1,0:T(8,128)(2,1)S(1)}, bf16[256,512]{1,0:T(8,128)(2,1)}, u32[]{:S(2)}) copy-start(bf16[256,512]{1,0:T(8,128)(2,1)} %refs_22_.1) | copy-start | bytes 786436
  21.6 7.9 %copy-start.3 = (bf16[256,256]{1,0:T(8,128)(2,1)S(1)}, bf16[256,256]{1,0:T(8,128)(2,1)}, u32[]{:S(2)}) copy-start(bf16[256,256]{1,0:T(8,128)(2,1)} %refs_11_.5) | copy-start | bytes 393220
  21.6 7.9 %copy-start.4 = (bf16[256,256]{1,0:T(8,128)(2,1)S(1)}, bf16[256,256]{1,0:T(8,128)(2,1)}, u32[]{:S(2)}) copy-start(bf16[256,256]{1,0:T(8,128)(2,1)} %refs_12_.3) | copy-start | bytes 393220
  21.6 7.9 %copy-start.5 = (bf16[256,256]{1,0:T(8,128)(2,1)S(1)}, bf16[256,256]{1,0:T(8,128)(2,1)}, u32[]{:S(2)}) copy-start(bf16[256,256]{1,0:T(8,128)(2,1)} %refs_13_.3) | copy-start | bytes 393220
  21.6 7.9 %copy-start.6 = (bf16[256,256]{1,0:T(8,128)(2,1)S(1)}, bf16[256,256]{1,0:T(8,128)(2,1)}, u32[]{:S(2)}) copy-start(bf16[256,256]{1,0:T(8,128)(2,1)} %refs_14_.3) | copy-start | bytes 393220
  21.6 7.9 %copy-start.7 = (bf16[256,256]{1,0:T(8,128)(2,1)S(1)}, bf16[256,256]{1,0:T(8,128)(2,1)}, u32[]{:S(2)}) copy-start(bf16[256,256]{1,0:T(8,128)(2,1)} %refs_16_.3) | copy-start | bytes 393220
  21.6 7.9 %copy-start.8 = (bf16[256,192]{0,1:T(8,128)(2,1)S(1)}, bf16[256,192]{0,1:T(8,128)(2,1)}, u32[]{:S(2)}) copy-start(bf16[256,192]{0,1:T(8,128)(2,1)} %param.32) | copy-start | bytes 294916
  21.7 7.9 %copy-start.9 = (bf16[192,256]{1,0:T(8,128)(2,1)S(1)}, bf16[192,256]{1,0:T(8,128)(2,1)}, u32[]{:S(2)}) copy-start(bf16[192,256]{1,0:T(8,128)(2,1)} %refs_17_.3) | copy-start | bytes 294916
  21.7 7.9 %copy-start.10 = (bf16[192,256]{1,0:T(8,128)(2,1)S(1)}, bf16[192,256]{1,0:T(8,128)(2,1)}, u32[]{:S(2)}) copy-start(bf16[192,256]{1,0:T(8,128)(2,1)} %refs_18_.1) | copy-start | bytes 294916
  21.7 7.9 %copy-start.11 = (bf16[64,64]{1,0:T(8,128)(2,1)S(1)}, bf16[64,64]{1,0:T(8,128)(2,1)}, u32[]{:S(2)}) copy-start(bf16[64,64]{1,0:T(8,128)(2,1)} %refs_19_.1) | copy-start | bytes 24580
  21.7 7.9 %copy-start.13 = (f32[256,4]{0,1:T(4,128)S(1)}, f32[256,4]{0,1:T(4,128)}, u32[]{:S(2)}) copy-start(f32[256,4]{0,1:T(4,128)} %param.24) | copy-start | bytes 12292
  26.9 4.5 %copy-start.12 = (s32[1,1,2048]{2,1,0:T(1,128)S(1)}, s32[1,1,2048]{2,1,0:T(1,128)}, u32[]{:S(2)}) copy-start(s32[1,1,2048]{2,1,0:T(1,128)} %refs_7_.5) | copy-start | bytes 24580
  27.0 4.5 %collective-permute-start.2 = (bf16[1280,128]{1,0:T(8,128)(2,1)S(1)}, bf16[1280,128]{1,0:T(8,128)(2,1)S(1)}, u32[]{:S(2)}, u32[]{:S(2)}) collective-permute-start(bf16[1280,128]{1,0:T(8,128)(2,1)S(1)} %collective-permute-done.refs_0_), channel_id=1, source_target_pairs={{0,1},{1,0},{2,3},{3,2},{4,5},{5,4},{6,7},{7,6},{8,9},{9,8},{10,11... | collective-permute-start | bytes 983048 | tf_op jit(solution)/shard_map/ppermute | solution.py:579
  27.1 4.4 %collective-permute-start.3 = (bf16[1280,128]{1,0:T(8,128)(2,1)S(1)}, bf16[1280,128]{1,0:T(8,128)(2,1)S(1)}, u32[]{:S(2)}, u32[]{:S(2)}) collective-permute-start(bf16[1280,128]{1,0:T(8,128)(2,1)S(1)} %collective-permute-done.1.refs_1_), channel_id=1, source_target_pairs={{0,1},{1,0},{2,3},{3,2},{4,5},{5,4},{6,7},{7,6},{8,9},{9,8},{10,11... | collective-permute-start | bytes 983048 | tf_op jit(solution)/shard_map/ppermute | solution.py:579
  27.6 1.9 %collective-permute-start.4 = (bf16[848,128]{1,0:T(8,128)(2,1)S(1)}, bf16[848,128]{1,0:T(8,128)(2,1)S(1)}, u32[]{:S(2)}, u32[]{:S(2)}) collective-permute-start(bf16[848,128]{1,0:T(8,128)(2,1)S(1)} %get-tuple-element.30), channel_id=1, source_target_pairs={{0,1},{1,0},{2,3},{3,2},{4,5},{5,4},{6,7},{7,6},{8,9},{9,8},{10,11... | collective-permute-start | bytes 651272 | tf_op jit(solution)/shard_map/ppermute | solution.py:579

commit v8 on v7

--- a/solution.py
+++ b/solution.py
@@ -158,7 +158,8 @@
         at = 0
         while at < buffer.shape[0]:
             source = waiting.pop(0)
-            part = buffer if source.shape == buffer.shape else buffer.at[pl.ds(at, source.shape[0])]
+            same = source.shape == buffer.shape
+            part = buffer if same else buffer.at[pl.ds(at, source.shape[0])]
             pieces.append((source, part))
             at += source.shape[0]
     copies = [pltpu.make_async_copy(*piece, sem.at[n]) for n, piece in enumerate(pieces)]
@@ -170,7 +171,13 @@
 def prepare_kernel(plan, *refs):
     inputs, (own, where, rows, scalars, tensors), refs = refs[:7], refs[7:12], refs[12:]
     sends, (onehot, *buffers, sem) = refs[: len(plan.arrays)], refs[len(plan.arrays) :]
-    copies = fetch(inputs, (*buffers, scalars, tensors), sem)
+    comps = tensors.shape[2]
+    chunks = [pl.ds(k, min(4, comps - k)) for k in range(0, comps, 4)]
+    copies = fetch(
+        (*inputs[:6], *[inputs[6].at[0, 0, chunk] for chunk in chunks]),
+        (*buffers, scalars, *[tensors.at[0, 0, chunk] for chunk in chunks]),
+        sem,
+    )
     send_index, counts, species, vectors, reverse = buffers
     channels, edges = scalars.shape[2:]
     comps, m = tensors.shape[2:4]
@@ -192,7 +199,11 @@
         axis=1,
     )
     slots = index.shape[1]
-    onehot[...] = (lax.broadcasted_iota(jnp.int32, (edges, slots), 0) == index).astype(BF16)
+    low = lax.broadcasted_iota(jnp.int32, (256, slots), 0).astype(F32).astype(BF16)
+    for at in range(0, edges, 256):
+        inside = jnp.logical_and(index >= at, index < at + 256)
+        key = jnp.where(inside, index - at, -1).astype(F32).astype(BF16)
+        onehot[at : at + 256, :] = jnp.where(low == key, BF16(1), BF16(0))
     near = jnp.minimum(reverse[0], edges - 1) * 8
     rows[...] = jnp.concatenate(
         [near[:, j * 128 : (j + 1) * 128] for j in range(edges // 128)], axis=0
@@ -217,10 +228,12 @@
     own[features:, :] = jnp.broadcast_to(extra[0:1], (EXTRA, slots)).astype(BF16)
     copies[5].wait()
     own[:channels, :] = mm(scalars[0, 0], onehot[...]).astype(BF16)
-    copies[6].wait()
-    own[channels:features, :] = mm(
-        tensors[0, 0].reshape(comps * m, edges), onehot[...]
-    ).astype(BF16)
+    for copy, chunk in zip(copies[6:], chunks):
+        copy.wait()
+        piece = tensors[0, 0, chunk].reshape(chunk.size * m, edges)
+        own[pl.ds(channels + chunk.start * m, chunk.size * m), :] = mm(
+            piece, onehot[...]
+        ).astype(BF16)
     half = features // 2
     for send, parts in zip(sends, plan.arrays):
         at = 0
@@ -374,11 +387,12 @@
     scalars_out[:, here] = contract(middle[:, here], v, w_contract[...])
     target = reverse[0, :, here] - edges
     odd = lax.rem(lax.axis_index("gx"), 2) == 1
-    at = lax.broadcasted_iota(jnp.int32, (block, width), 0)
+    low = lax.broadcasted_iota(jnp.int32, (block, width), 0).astype(F32).astype(BF16)
     for j, (p, q) in enumerate(zip(*plan.orders)):
-        merge[j * block : (j + 1) * block, here] = (
-            at + pick(odd, (OPPOSITE[p], OPPOSITE[q])) * block == target
-        ).astype(BF16)
+        at = pick(odd, (OPPOSITE[p], OPPOSITE[q])) * block
+        inside = jnp.logical_and(target >= at, target < at + block)
+        key = jnp.where(inside, target - at, -1).astype(F32).astype(BF16)
+        merge[j * block : (j + 1) * block, here] = jnp.where(low == key, BF16(1), BF16(0))
 
 
 def settle(plan, block, positions, base, received, own, where, table, weights, far, s_new, t_new):
@@ -552,7 +566,7 @@
 
     prepared = (send_index, counts, species, vectors, reverse, scalars, tensors)
     prepared_buffers = buffers(*prepared)
-    del prepared_buffers[5:7]
+    prepared_buffers[5:] = [pltpu.SemaphoreType.DMA((6 + pl.cdiv(comps, 4),))]
     prepared_buffers[1] = pltpu.SMEM(counts.shape, counts.dtype)
     prepared_buffers.insert(0, pltpu.VMEM((edges, slots), BF16))
     own, where, rows, scalars, tensors, *sends = pl.pallas_call(

time: 36.6 us -> 37 us (1.011)
    pallas_call x1, Pallas kernels: 3.67 us -> 4.16 us  [per_device(): pl.pallas_call(functools.partial(prepare_kernel, plan), in_specs=[hbm] *...]
  transfers between devices with their start and end apart: 5 -> 5, of which waited for: 1 -> 1; matrix products, arithmetic and copies ran while one was open for 0% -> 0% of each run, Pallas kernels for 46% -> 45%
where the time goes in v8:
time: 37 us; the launch traced here: 36.8 us
  Pallas kernels  25.7 us (69%)
  starting transfers between devices  8.21 us (22%)
  waiting for transfers between devices  1.83 us (5%)
  between operations  0.9 us (2%)
    pallas_call x1, Pallas kernels, per_device(): pl.pallas_call(interior_kernel, grid=(steps,), in_specs=[pl.BlockSpec(mem...  9.67 us
    ppermute x5, starting transfers between devices, exchange(): return lax.ppermute(x, ('gx', 'gy'), pairs)  8.21 us
    pallas_call x1, Pallas kernels, per_device(): pl.pallas_call(functools.partial(incoming_kernel, plan, block), grid=(ste...  5.06 us
    pallas_call x1, Pallas kernels, per_device(): pl.pallas_call(functools.partial(boundary_kernel, plan, block, positions,...  4.98 us
    pallas_call x1, Pallas kernels, per_device(): pl.pallas_call(functools.partial(prepare_kernel, plan), in_specs=[hbm] *...  4.16 us
    pallas_call x1, Pallas kernels, per_device(): pl.pallas_call(functools.partial(near_kernel, plan, block, near), in_spec...  1.89 us
    ppermute x5, waiting for transfers between devices, exchange(): return lax.ppermute(x, ('gx', 'gy'), pairs)  1.83 us
  transfers between devices with their start and end apart: 5, of which 1 were waited for; matrix products, arithmetic and copies ran while one was open for 0% of the time, Pallas kernels for 45%

profile of v8, /device:TPU:0, one launch (start us, length us, event | category | flops | bytes accessed | tf_op | source)
XLA Modules:
  0.0 36.8 jit_solution(2597190370395322077)
XLA Ops:
  0.6 4.2 %prepare.1 = (bf16[848,512]{1,0:T(8,128)(2,1)S(1)}, f32[8,512]{1,0:T(8,128)S(1)}, s32[16,128]{1,0:T(8,128)S(1)}, bf16[1,1,256,2048]{3,2,1,0:T(8,128)(2,1)S(1)}, ...) custom-call(s32[1,1,8,64]{3,2,1,0:T(8,128)} %refs_0_.3, ...), custom_call_target="tpu_custom_call" | custom-call | tf_op jit(solution)/shard_map/prepare/pallas_call | solution.py:572
  4.8 3.0 %collective-permute-start = (bf16[1280,128]{1,0:T(8,128)(2,1)S(1)}, bf16[1280,128]{1,0:T(8,128)(2,1)S(1)}, u32[]{:S(2)}, u32[]{:S(2)}) collective-permute-start(bf16[1280,128]{1,0:T(8,128)(2,1)S(1)} %get-tuple-element.20), channel_id=1, source_target_pairs={{0,2},{1,3},{2,0},{3,1},{4,6},{5,7},{6,4},{7,5},{8,10},{9,11},{10,... | collective-permute-start | bytes 983048 | tf_op jit(solution)/shard_map/ppermute | solution.py:593
  7.8 4.5 %collective-permute-start.1 = (bf16[1280,128]{1,0:T(8,128)(2,1)S(1)}, bf16[1280,128]{1,0:T(8,128)(2,1)S(1)}, u32[]{:S(2)}, u32[]{:S(2)}) collective-permute-start(bf16[1280,128]{1,0:T(8,128)(2,1)S(1)} %get-tuple-element.21), channel_id=1, source_target_pairs={{0,30},{1,31},{2,4},{3,5},{4,2},{5,3},{6,8},{7,9},{8,6},{9,7},{10,... | collective-permute-start | bytes 983048 | tf_op jit(solution)/shard_map/ppermute | solution.py:593
  12.4 9.7 %interior.1 = (bf16[256,2048]{1,0:T(8,128)(2,1)S(1)}, bf16[256,2048]{1,0:T(8,128)(2,1)S(1)}, bf16[9,64,2048]{2,1,0:T(8,128)(2,1)S(1)}) custom-call(s32[16,128]{1,0:T(8,128)S(1)} %get-tuple-element.22.rows, bf16[1,1,256,2048]{3,2,1,0:T(8,128)(2,1)S(1)} %get-tuple-element.23.scalars, bf16[1,1,9,64,2048]{4,3,2,1,0:T(8,128)(2,1)S(1)} %get-tuple-element.24.tensors, ...), custom_call_target="tpu_custom_call" | custom-call | flops 6979321856 | bytes 6815744 | tf_op jit(solution)/shard_map/interior/pallas_call | solution.py:614
  22.0 0.0 copy-start
  22.0 0.0 copy-start.1
  22.1 0.0 copy-start.2
  22.1 0.0 copy-start.3
  22.1 0.0 copy-start.4
  22.1 0.0 copy-start.5
  22.1 0.0 copy-start.6
  22.1 0.0 copy-start.7
  22.1 0.0 copy-start.8
  22.1 0.0 copy-start.9
  22.2 0.0 copy-start.10
  22.2 0.0 copy-start.11
  22.2 0.0 copy-start.13
  22.2 5.1 %incoming.1 = (bf16[256,2048]{1,0:T(8,128)(2,1)S(1)}, bf16[512,2048]{1,0:T(8,128)(2,1)S(1)}) custom-call(bf16[256,2048]{1,0:T(8,128)(2,1)S(1)} %get-tuple-element.25.message, bf16[256,2048]{1,0:T(8,128)(2,1)S(1)} %get-tuple-element.26.middle, s32[16,128]{1,0:T(8,128)S(1)} %get-tuple-element.22.rows, s32[1,1,2048]{2,1,0:T(1,128)} %refs_7_.5, ...), custom_call_target="tpu_custom_call" | custom-call | flops 4294967296 | bytes 4194304 | tf_op jit(solution)/shard_map/incoming/pallas_call | solution.py:643
  27.3 0.0 copy-start.12
  27.3 0.0 collective-permute-done.refs_0_
  27.3 0.0 collective-permute-done.1.refs_1_
  27.3 0.1 collective-permute-start.2
  27.4 0.5 %collective-permute-start.3 = (bf16[1280,128]{1,0:T(8,128)(2,1)S(1)}, bf16[1280,128]{1,0:T(8,128)(2,1)S(1)}, u32[]{:S(2)}, u32[]{:S(2)}) collective-permute-start(bf16[1280,128]{1,0:T(8,128)(2,1)S(1)} %collective-permute-done.1.refs_1_), channel_id=1, source_target_pairs={{0,1},{1,0},{2,3},{3,2},{4,5},{5,4},{6,7},{7,6},{8,9},{9,8},{10,11... | collective-permute-start | bytes 983048 | tf_op jit(solution)/shard_map/ppermute | solution.py:593
  27.9 0.1 collective-permute-start.4
  27.9 1.8 %collective-permute-done.4.refs_2_ = bf16[848,128]{1,0:T(8,128)(2,1)S(1)} collective-permute-done((bf16[848,128]{1,0:T(8,128)(2,1)S(1)}, bf16[848,128]{1,0:T(8,128)(2,1)S(1)}, u32[]{:S(2)}, u32[]{:S(2)}) %collective-permute-start.4) | collective-permute-done | bytes 217120 | tf_op jit(solution)/shard_map/ppermute | solution.py:593
  29.8 0.0 copy-done
  29.8 0.0 copy-done.1
  29.8 0.0 copy-done.2
  29.8 0.0 copy-done.3
  29.8 0.0 copy-done.4
  29.8 0.0 copy-done.5
  29.8 0.0 copy-done.6
  29.8 0.0 copy-done.7
  29.8 0.0 copy-done.8
  29.8 0.0 copy-done.9
  29.8 0.0 copy-done.10
  29.9 0.0 copy-done.11
  29.9 0.0 copy-done.13
  29.9 1.9 %near.1 = (bf16[256,256]{1,0:T(8,128)(2,1)S(1)}, bf16[576,256]{1,0:T(8,128)(2,1)S(1)}) custom-call(bf16[1280,128]{1,0:T(8,128)(2,1)S(1)} %collective-permute-done.refs_0_, bf16[1280,128]{1,0:T(8,128)(2,1)S(1)} %collective-permute-done.1.refs_1_, bf16[848,128]{1,0:T(8,128)(2,1)S(1)} %collective-permute-done.4.refs_2_, ...), custom_call_target="tpu_custom_call" | custom-call | flops 218103808 | bytes 851968 | tf_op jit(solution)/shard_map/near/pallas_call | solution.py:670
  31.8 0.0 collective-permute-done.2.refs_0_
  31.8 0.0 collective-permute-done.3.refs_1_
  31.8 0.0 copy-done.12
  31.8 5.0 %boundary.1 = (bf16[1,1,256,2048]{3,2,1,0:T(8,128)(2,1)}, bf16[1,1,9,64,2048]{4,3,2,1,0:T(8,128)(2,1)}) custom-call(bf16[1280,128]{1,0:T(8,128)(2,1)S(1)} %collective-permute-done.2.refs_0_, bf16[1280,128]{1,0:T(8,128)(2,1)S(1)} %collective-permute-done.3.refs_1_, bf16[256,256]{1,0:T(8,128)(2,1)S(1)} %get-tuple-element.33.refs_2_, ...), custom_call_target="tpu_custom_call" | custom-call | flops 1744830464 | bytes 13631488 | tf_op jit(solution)/shard_map/boundary/pallas_call | solution.py:690
Async XLA Ops:
  4.8 22.5 %collective-permute-start = (bf16[1280,128]{1,0:T(8,128)(2,1)S(1)}, bf16[1280,128]{1,0:T(8,128)(2,1)S(1)}, u32[]{:S(2)}, u32[]{:S(2)}) collective-permute-start(bf16[1280,128]{1,0:T(8,128)(2,1)S(1)} %get-tuple-element.20), channel_id=1, source_target_pairs={{0,2},{1,3},{2,0},{3,1},{4,6},{5,7},{6,4},{7,5},{8,10},{9,11},{10,... | collective-permute-start | bytes 983048 | tf_op jit(solution)/shard_map/ppermute | solution.py:593
  7.8 19.5 %collective-permute-start.1 = (bf16[1280,128]{1,0:T(8,128)(2,1)S(1)}, bf16[1280,128]{1,0:T(8,128)(2,1)S(1)}, u32[]{:S(2)}, u32[]{:S(2)}) collective-permute-start(bf16[1280,128]{1,0:T(8,128)(2,1)S(1)} %get-tuple-element.21), channel_id=1, source_target_pairs={{0,30},{1,31},{2,4},{3,5},{4,2},{5,3},{6,8},{7,9},{8,6},{9,7},{10,... | collective-permute-start | bytes 983048 | tf_op jit(solution)/shard_map/ppermute | solution.py:593
  22.0 7.7 %copy-start = (bf16[512,256]{1,0:T(8,128)(2,1)S(1)}, bf16[512,256]{1,0:T(8,128)(2,1)}, u32[]{:S(2)}) copy-start(bf16[512,256]{1,0:T(8,128)(2,1)} %refs_20_.1) | copy-start | bytes 786436
  22.0 7.7 %copy-start.1 = (bf16[512,256]{1,0:T(8,128)(2,1)S(1)}, bf16[512,256]{1,0:T(8,128)(2,1)}, u32[]{:S(2)}) copy-start(bf16[512,256]{1,0:T(8,128)(2,1)} %refs_21_.1) | copy-start | bytes 786436
  22.1 7.7 %copy-start.2 = (bf16[256,512]{1,0:T(8,128)(2,1)S(1)}, bf16[256,512]{1,0:T(8,128)(2,1)}, u32[]{:S(2)}) copy-start(bf16[256,512]{1,0:T(8,128)(2,1)} %refs_22_.1) | copy-start | bytes 786436
  22.1 7.7 %copy-start.3 = (bf16[256,256]{1,0:T(8,128)(2,1)S(1)}, bf16[256,256]{1,0:T(8,128)(2,1)}, u32[]{:S(2)}) copy-start(bf16[256,256]{1,0:T(8,128)(2,1)} %refs_11_.5) | copy-start | bytes 393220
  22.1 7.7 %copy-start.4 = (bf16[256,256]{1,0:T(8,128)(2,1)S(1)}, bf16[256,256]{1,0:T(8,128)(2,1)}, u32[]{:S(2)}) copy-start(bf16[256,256]{1,0:T(8,128)(2,1)} %refs_12_.3) | copy-start | bytes 393220
  22.1 7.7 %copy-start.5 = (bf16[256,256]{1,0:T(8,128)(2,1)S(1)}, bf16[256,256]{1,0:T(8,128)(2,1)}, u32[]{:S(2)}) copy-start(bf16[256,256]{1,0:T(8,128)(2,1)} %refs_13_.3) | copy-start | bytes 393220
  22.1 7.7 %copy-start.6 = (bf16[256,256]{1,0:T(8,128)(2,1)S(1)}, bf16[256,256]{1,0:T(8,128)(2,1)}, u32[]{:S(2)}) copy-start(bf16[256,256]{1,0:T(8,128)(2,1)} %refs_14_.3) | copy-start | bytes 393220
  22.1 7.7 %copy-start.7 = (bf16[256,256]{1,0:T(8,128)(2,1)S(1)}, bf16[256,256]{1,0:T(8,128)(2,1)}, u32[]{:S(2)}) copy-start(bf16[256,256]{1,0:T(8,128)(2,1)} %refs_16_.3) | copy-start | bytes 393220
  22.1 7.7 %copy-start.8 = (bf16[256,192]{0,1:T(8,128)(2,1)S(1)}, bf16[256,192]{0,1:T(8,128)(2,1)}, u32[]{:S(2)}) copy-start(bf16[256,192]{0,1:T(8,128)(2,1)} %param.32) | copy-start | bytes 294916
  22.1 7.7 %copy-start.9 = (bf16[192,256]{1,0:T(8,128)(2,1)S(1)}, bf16[192,256]{1,0:T(8,128)(2,1)}, u32[]{:S(2)}) copy-start(bf16[192,256]{1,0:T(8,128)(2,1)} %refs_17_.3) | copy-start | bytes 294916
  22.2 7.7 %copy-start.10 = (bf16[192,256]{1,0:T(8,128)(2,1)S(1)}, bf16[192,256]{1,0:T(8,128)(2,1)}, u32[]{:S(2)}) copy-start(bf16[192,256]{1,0:T(8,128)(2,1)} %refs_18_.1) | copy-start | bytes 294916
  22.2 7.7 %copy-start.11 = (bf16[64,64]{1,0:T(8,128)(2,1)S(1)}, bf16[64,64]{1,0:T(8,128)(2,1)}, u32[]{:S(2)}) copy-start(bf16[64,64]{1,0:T(8,128)(2,1)} %refs_19_.1) | copy-start | bytes 24580
  22.2 7.7 %copy-start.13 = (f32[256,4]{0,1:T(4,128)S(1)}, f32[256,4]{0,1:T(4,128)}, u32[]{:S(2)}) copy-start(f32[256,4]{0,1:T(4,128)} %param.24) | copy-start | bytes 12292
  27.3 4.5 %copy-start.12 = (s32[1,1,2048]{2,1,0:T(1,128)S(1)}, s32[1,1,2048]{2,1,0:T(1,128)}, u32[]{:S(2)}) copy-start(s32[1,1,2048]{2,1,0:T(1,128)} %refs_7_.5) | copy-start | bytes 24580
  27.3 4.5 %collective-permute-start.2 = (bf16[1280,128]{1,0:T(8,128)(2,1)S(1)}, bf16[1280,128]{1,0:T(8,128)(2,1)S(1)}, u32[]{:S(2)}, u32[]{:S(2)}) collective-permute-start(bf16[1280,128]{1,0:T(8,128)(2,1)S(1)} %collective-permute-done.refs_0_), channel_id=1, source_target_pairs={{0,1},{1,0},{2,3},{3,2},{4,5},{5,4},{6,7},{7,6},{8,9},{9,8},{10,11... | collective-permute-start | bytes 983048 | tf_op jit(solution)/shard_map/ppermute | solution.py:593
  27.4 4.4 %collective-permute-start.3 = (bf16[1280,128]{1,0:T(8,128)(2,1)S(1)}, bf16[1280,128]{1,0:T(8,128)(2,1)S(1)}, u32[]{:S(2)}, u32[]{:S(2)}) collective-permute-start(bf16[1280,128]{1,0:T(8,128)(2,1)S(1)} %collective-permute-done.1.refs_1_), channel_id=1, source_target_pairs={{0,1},{1,0},{2,3},{3,2},{4,5},{5,4},{6,7},{7,6},{8,9},{9,8},{10,11... | collective-permute-start | bytes 983048 | tf_op jit(solution)/shard_map/ppermute | solution.py:593
  27.9 1.9 %collective-permute-start.4 = (bf16[848,128]{1,0:T(8,128)(2,1)S(1)}, bf16[848,128]{1,0:T(8,128)(2,1)S(1)}, u32[]{:S(2)}, u32[]{:S(2)}) collective-permute-start(bf16[848,128]{1,0:T(8,128)(2,1)S(1)} %get-tuple-element.30), channel_id=1, source_target_pairs={{0,1},{1,0},{2,3},{3,2},{4,5},{5,4},{6,7},{7,6},{8,9},{9,8},{10,11... | collective-permute-start | bytes 651272 | tf_op jit(solution)/shard_map/ppermute | solution.py:593

commit v9 on v7

--- a/solution.py
+++ b/solution.py
@@ -192,7 +192,11 @@
         axis=1,
     )
     slots = index.shape[1]
-    onehot[...] = (lax.broadcasted_iota(jnp.int32, (edges, slots), 0) == index).astype(BF16)
+    low = lax.broadcasted_iota(jnp.int32, (256, slots), 0).astype(F32).astype(BF16)
+    for at in range(0, edges, 256):
+        inside = jnp.logical_and(index >= at, index < at + 256)
+        key = jnp.where(inside, index - at, -1).astype(F32).astype(BF16)
+        onehot[at : at + 256, :] = jnp.where(low == key, BF16(1), BF16(0))
     near = jnp.minimum(reverse[0], edges - 1) * 8
     rows[...] = jnp.concatenate(
         [near[:, j * 128 : (j + 1) * 128] for j in range(edges // 128)], axis=0
@@ -374,11 +378,12 @@
     scalars_out[:, here] = contract(middle[:, here], v, w_contract[...])
     target = reverse[0, :, here] - edges
     odd = lax.rem(lax.axis_index("gx"), 2) == 1
-    at = lax.broadcasted_iota(jnp.int32, (block, width), 0)
+    low = lax.broadcasted_iota(jnp.int32, (block, width), 0).astype(F32).astype(BF16)
     for j, (p, q) in enumerate(zip(*plan.orders)):
-        merge[j * block : (j + 1) * block, here] = (
-            at + pick(odd, (OPPOSITE[p], OPPOSITE[q])) * block == target
-        ).astype(BF16)
+        at = pick(odd, (OPPOSITE[p], OPPOSITE[q])) * block
+        inside = jnp.logical_and(target >= at, target < at + block)
+        key = jnp.where(inside, target - at, -1).astype(F32).astype(BF16)
+        merge[j * block : (j + 1) * block, here] = jnp.where(low == key, BF16(1), BF16(0))
 
 
 def settle(plan, block, positions, base, received, own, where, table, weights, far, s_new, t_new):

time: 36.6 us -> 36.5 us (level)
  no operation moved by 1% of the time
where the time goes in v9:
time: 36.5 us; the launch traced here: 36.3 us
  Pallas kernels  25.3 us (69%)
  starting transfers between devices  8.21 us (22%)
  waiting for transfers between devices  1.83 us (5%)
  between operations  0.9 us (2%)
    pallas_call x1, Pallas kernels, per_device(): pl.pallas_call(interior_kernel, grid=(steps,), in_specs=[pl.BlockSpec(mem...  9.67 us
    ppermute x5, starting transfers between devices, exchange(): return lax.ppermute(x, ('gx', 'gy'), pairs)  8.21 us
    pallas_call x1, Pallas kernels, per_device(): pl.pallas_call(functools.partial(incoming_kernel, plan, block), grid=(ste...  5.06 us
    pallas_call x1, Pallas kernels, per_device(): pl.pallas_call(functools.partial(boundary_kernel, plan, block, positions,...  4.98 us
    pallas_call x1, Pallas kernels, per_device(): pl.pallas_call(functools.partial(prepare_kernel, plan), in_specs=[hbm] *...  3.66 us
    pallas_call x1, Pallas kernels, per_device(): pl.pallas_call(functools.partial(near_kernel, plan, block, near), in_spec...  1.89 us
    ppermute x5, waiting for transfers between devices, exchange(): return lax.ppermute(x, ('gx', 'gy'), pairs)  1.83 us
  transfers between devices with their start and end apart: 5, of which 1 were waited for; matrix products, arithmetic and copies ran while one was open for 0% of the time, Pallas kernels for 46%

profile of v9, /device:TPU:0, one launch (start us, length us, event | category | flops | bytes accessed | tf_op | source)
XLA Modules:
  0.0 36.3 jit_solution(17576906898237074673)
XLA Ops:
  0.6 3.7 %prepare.1 = (bf16[848,512]{1,0:T(8,128)(2,1)S(1)}, f32[8,512]{1,0:T(8,128)S(1)}, s32[16,128]{1,0:T(8,128)S(1)}, bf16[1,1,256,2048]{3,2,1,0:T(8,128)(2,1)S(1)}, ...) custom-call(s32[1,1,8,64]{3,2,1,0:T(8,128)} %refs_0_.3, ...), custom_call_target="tpu_custom_call" | custom-call | tf_op jit(solution)/shard_map/prepare/pallas_call | solution.py:563
  4.3 3.0 %collective-permute-start = (bf16[1280,128]{1,0:T(8,128)(2,1)S(1)}, bf16[1280,128]{1,0:T(8,128)(2,1)S(1)}, u32[]{:S(2)}, u32[]{:S(2)}) collective-permute-start(bf16[1280,128]{1,0:T(8,128)(2,1)S(1)} %get-tuple-element.20), channel_id=1, source_target_pairs={{0,2},{1,3},{2,0},{3,1},{4,6},{5,7},{6,4},{7,5},{8,10},{9,11},{10,... | collective-permute-start | bytes 983048 | tf_op jit(solution)/shard_map/ppermute | solution.py:584
  7.3 4.5 %collective-permute-start.1 = (bf16[1280,128]{1,0:T(8,128)(2,1)S(1)}, bf16[1280,128]{1,0:T(8,128)(2,1)S(1)}, u32[]{:S(2)}, u32[]{:S(2)}) collective-permute-start(bf16[1280,128]{1,0:T(8,128)(2,1)S(1)} %get-tuple-element.21), channel_id=1, source_target_pairs={{0,30},{1,31},{2,4},{3,5},{4,2},{5,3},{6,8},{7,9},{8,6},{9,7},{10,... | collective-permute-start | bytes 983048 | tf_op jit(solution)/shard_map/ppermute | solution.py:584
  11.9 9.7 %interior.1 = (bf16[256,2048]{1,0:T(8,128)(2,1)S(1)}, bf16[256,2048]{1,0:T(8,128)(2,1)S(1)}, bf16[9,64,2048]{2,1,0:T(8,128)(2,1)S(1)}) custom-call(s32[16,128]{1,0:T(8,128)S(1)} %get-tuple-element.22.rows, bf16[1,1,256,2048]{3,2,1,0:T(8,128)(2,1)S(1)} %get-tuple-element.23.scalars, bf16[1,1,9,64,2048]{4,3,2,1,0:T(8,128)(2,1)S(1)} %get-tuple-element.24.tensors, ...), custom_call_target="tpu_custom_call" | custom-call | flops 6979321856 | bytes 6815744 | tf_op jit(solution)/shard_map/interior/pallas_call | solution.py:605
  21.5 0.0 copy-start
  21.5 0.0 copy-start.1
  21.6 0.0 copy-start.2
  21.6 0.0 copy-start.3
  21.6 0.0 copy-start.4
  21.6 0.0 copy-start.5
  21.6 0.0 copy-start.6
  21.6 0.0 copy-start.7
  21.6 0.0 copy-start.8
  21.6 0.0 copy-start.9
  21.7 0.0 copy-start.10
  21.7 0.0 copy-start.11
  21.7 0.0 copy-start.13
  21.7 5.1 %incoming.1 = (bf16[256,2048]{1,0:T(8,128)(2,1)S(1)}, bf16[512,2048]{1,0:T(8,128)(2,1)S(1)}) custom-call(bf16[256,2048]{1,0:T(8,128)(2,1)S(1)} %get-tuple-element.25.message, bf16[256,2048]{1,0:T(8,128)(2,1)S(1)} %get-tuple-element.26.middle, s32[16,128]{1,0:T(8,128)S(1)} %get-tuple-element.22.rows, s32[1,1,2048]{2,1,0:T(1,128)} %refs_7_.5, ...), custom_call_target="tpu_custom_call" | custom-call | flops 4294967296 | bytes 4194304 | tf_op jit(solution)/shard_map/incoming/pallas_call | solution.py:634
  26.8 0.0 copy-start.12
  26.8 0.0 collective-permute-done.refs_0_
  26.8 0.0 collective-permute-done.1.refs_1_
  26.8 0.1 collective-permute-start.2
  26.9 0.5 %collective-permute-start.3 = (bf16[1280,128]{1,0:T(8,128)(2,1)S(1)}, bf16[1280,128]{1,0:T(8,128)(2,1)S(1)}, u32[]{:S(2)}, u32[]{:S(2)}) collective-permute-start(bf16[1280,128]{1,0:T(8,128)(2,1)S(1)} %collective-permute-done.1.refs_1_), channel_id=1, source_target_pairs={{0,1},{1,0},{2,3},{3,2},{4,5},{5,4},{6,7},{7,6},{8,9},{9,8},{10,11... | collective-permute-start | bytes 983048 | tf_op jit(solution)/shard_map/ppermute | solution.py:584
  27.4 0.1 collective-permute-start.4
  27.4 1.8 %collective-permute-done.4.refs_2_ = bf16[848,128]{1,0:T(8,128)(2,1)S(1)} collective-permute-done((bf16[848,128]{1,0:T(8,128)(2,1)S(1)}, bf16[848,128]{1,0:T(8,128)(2,1)S(1)}, u32[]{:S(2)}, u32[]{:S(2)}) %collective-permute-start.4) | collective-permute-done | bytes 217120 | tf_op jit(solution)/shard_map/ppermute | solution.py:584
  29.3 0.0 copy-done
  29.3 0.0 copy-done.1
  29.3 0.0 copy-done.2
  29.3 0.0 copy-done.3
  29.3 0.0 copy-done.4
  29.3 0.0 copy-done.5
  29.3 0.0 copy-done.6
  29.3 0.0 copy-done.7
  29.3 0.0 copy-done.8
  29.3 0.0 copy-done.9
  29.3 0.0 copy-done.10
  29.4 0.0 copy-done.11
  29.4 0.0 copy-done.13
  29.4 1.9 %near.1 = (bf16[256,256]{1,0:T(8,128)(2,1)S(1)}, bf16[576,256]{1,0:T(8,128)(2,1)S(1)}) custom-call(bf16[1280,128]{1,0:T(8,128)(2,1)S(1)} %collective-permute-done.refs_0_, bf16[1280,128]{1,0:T(8,128)(2,1)S(1)} %collective-permute-done.1.refs_1_, bf16[848,128]{1,0:T(8,128)(2,1)S(1)} %collective-permute-done.4.refs_2_, ...), custom_call_target="tpu_custom_call" | custom-call | flops 218103808 | bytes 851968 | tf_op jit(solution)/shard_map/near/pallas_call | solution.py:661
  31.3 0.0 collective-permute-done.2.refs_0_
  31.3 0.0 collective-permute-done.3.refs_1_
  31.3 0.0 copy-done.12
  31.3 5.0 %boundary.1 = (bf16[1,1,256,2048]{3,2,1,0:T(8,128)(2,1)}, bf16[1,1,9,64,2048]{4,3,2,1,0:T(8,128)(2,1)}) custom-call(bf16[1280,128]{1,0:T(8,128)(2,1)S(1)} %collective-permute-done.2.refs_0_, bf16[1280,128]{1,0:T(8,128)(2,1)S(1)} %collective-permute-done.3.refs_1_, bf16[256,256]{1,0:T(8,128)(2,1)S(1)} %get-tuple-element.33.refs_2_, ...), custom_call_target="tpu_custom_call" | custom-call | flops 1744830464 | bytes 13631488 | tf_op jit(solution)/shard_map/boundary/pallas_call | solution.py:681
Async XLA Ops:
  4.3 22.5 %collective-permute-start = (bf16[1280,128]{1,0:T(8,128)(2,1)S(1)}, bf16[1280,128]{1,0:T(8,128)(2,1)S(1)}, u32[]{:S(2)}, u32[]{:S(2)}) collective-permute-start(bf16[1280,128]{1,0:T(8,128)(2,1)S(1)} %get-tuple-element.20), channel_id=1, source_target_pairs={{0,2},{1,3},{2,0},{3,1},{4,6},{5,7},{6,4},{7,5},{8,10},{9,11},{10,... | collective-permute-start | bytes 983048 | tf_op jit(solution)/shard_map/ppermute | solution.py:584
  7.3 19.5 %collective-permute-start.1 = (bf16[1280,128]{1,0:T(8,128)(2,1)S(1)}, bf16[1280,128]{1,0:T(8,128)(2,1)S(1)}, u32[]{:S(2)}, u32[]{:S(2)}) collective-permute-start(bf16[1280,128]{1,0:T(8,128)(2,1)S(1)} %get-tuple-element.21), channel_id=1, source_target_pairs={{0,30},{1,31},{2,4},{3,5},{4,2},{5,3},{6,8},{7,9},{8,6},{9,7},{10,... | collective-permute-start | bytes 983048 | tf_op jit(solution)/shard_map/ppermute | solution.py:584
  21.5 7.7 %copy-start = (bf16[512,256]{1,0:T(8,128)(2,1)S(1)}, bf16[512,256]{1,0:T(8,128)(2,1)}, u32[]{:S(2)}) copy-start(bf16[512,256]{1,0:T(8,128)(2,1)} %refs_20_.1) | copy-start | bytes 786436
  21.5 7.7 %copy-start.1 = (bf16[512,256]{1,0:T(8,128)(2,1)S(1)}, bf16[512,256]{1,0:T(8,128)(2,1)}, u32[]{:S(2)}) copy-start(bf16[512,256]{1,0:T(8,128)(2,1)} %refs_21_.1) | copy-start | bytes 786436
  21.6 7.7 %copy-start.2 = (bf16[256,512]{1,0:T(8,128)(2,1)S(1)}, bf16[256,512]{1,0:T(8,128)(2,1)}, u32[]{:S(2)}) copy-start(bf16[256,512]{1,0:T(8,128)(2,1)} %refs_22_.1) | copy-start | bytes 786436
  21.6 7.7 %copy-start.3 = (bf16[256,256]{1,0:T(8,128)(2,1)S(1)}, bf16[256,256]{1,0:T(8,128)(2,1)}, u32[]{:S(2)}) copy-start(bf16[256,256]{1,0:T(8,128)(2,1)} %refs_11_.5) | copy-start | bytes 393220
  21.6 7.7 %copy-start.4 = (bf16[256,256]{1,0:T(8,128)(2,1)S(1)}, bf16[256,256]{1,0:T(8,128)(2,1)}, u32[]{:S(2)}) copy-start(bf16[256,256]{1,0:T(8,128)(2,1)} %refs_12_.3) | copy-start | bytes 393220
  21.6 7.7 %copy-start.5 = (bf16[256,256]{1,0:T(8,128)(2,1)S(1)}, bf16[256,256]{1,0:T(8,128)(2,1)}, u32[]{:S(2)}) copy-start(bf16[256,256]{1,0:T(8,128)(2,1)} %refs_13_.3) | copy-start | bytes 393220
  21.6 7.7 %copy-start.6 = (bf16[256,256]{1,0:T(8,128)(2,1)S(1)}, bf16[256,256]{1,0:T(8,128)(2,1)}, u32[]{:S(2)}) copy-start(bf16[256,256]{1,0:T(8,128)(2,1)} %refs_14_.3) | copy-start | bytes 393220
  21.6 7.7 %copy-start.7 = (bf16[256,256]{1,0:T(8,128)(2,1)S(1)}, bf16[256,256]{1,0:T(8,128)(2,1)}, u32[]{:S(2)}) copy-start(bf16[256,256]{1,0:T(8,128)(2,1)} %refs_16_.3) | copy-start | bytes 393220
  21.6 7.7 %copy-start.8 = (bf16[256,192]{0,1:T(8,128)(2,1)S(1)}, bf16[256,192]{0,1:T(8,128)(2,1)}, u32[]{:S(2)}) copy-start(bf16[256,192]{0,1:T(8,128)(2,1)} %param.32) | copy-start | bytes 294916
  21.6 7.7 %copy-start.9 = (bf16[192,256]{1,0:T(8,128)(2,1)S(1)}, bf16[192,256]{1,0:T(8,128)(2,1)}, u32[]{:S(2)}) copy-start(bf16[192,256]{1,0:T(8,128)(2,1)} %refs_17_.3) | copy-start | bytes 294916
  21.7 7.7 %copy-start.10 = (bf16[192,256]{1,0:T(8,128)(2,1)S(1)}, bf16[192,256]{1,0:T(8,128)(2,1)}, u32[]{:S(2)}) copy-start(bf16[192,256]{1,0:T(8,128)(2,1)} %refs_18_.1) | copy-start | bytes 294916
  21.7 7.7 %copy-start.11 = (bf16[64,64]{1,0:T(8,128)(2,1)S(1)}, bf16[64,64]{1,0:T(8,128)(2,1)}, u32[]{:S(2)}) copy-start(bf16[64,64]{1,0:T(8,128)(2,1)} %refs_19_.1) | copy-start | bytes 24580
  21.7 7.7 %copy-start.13 = (f32[256,4]{0,1:T(4,128)S(1)}, f32[256,4]{0,1:T(4,128)}, u32[]{:S(2)}) copy-start(f32[256,4]{0,1:T(4,128)} %param.24) | copy-start | bytes 12292
  26.8 4.5 %copy-start.12 = (s32[1,1,2048]{2,1,0:T(1,128)S(1)}, s32[1,1,2048]{2,1,0:T(1,128)}, u32[]{:S(2)}) copy-start(s32[1,1,2048]{2,1,0:T(1,128)} %refs_7_.5) | copy-start | bytes 24580
  26.8 4.5 %collective-permute-start.2 = (bf16[1280,128]{1,0:T(8,128)(2,1)S(1)}, bf16[1280,128]{1,0:T(8,128)(2,1)S(1)}, u32[]{:S(2)}, u32[]{:S(2)}) collective-permute-start(bf16[1280,128]{1,0:T(8,128)(2,1)S(1)} %collective-permute-done.refs_0_), channel_id=1, source_target_pairs={{0,1},{1,0},{2,3},{3,2},{4,5},{5,4},{6,7},{7,6},{8,9},{9,8},{10,11... | collective-permute-start | bytes 983048 | tf_op jit(solution)/shard_map/ppermute | solution.py:584
  26.9 4.4 %collective-permute-start.3 = (bf16[1280,128]{1,0:T(8,128)(2,1)S(1)}, bf16[1280,128]{1,0:T(8,128)(2,1)S(1)}, u32[]{:S(2)}, u32[]{:S(2)}) collective-permute-start(bf16[1280,128]{1,0:T(8,128)(2,1)S(1)} %collective-permute-done.1.refs_1_), channel_id=1, source_target_pairs={{0,1},{1,0},{2,3},{3,2},{4,5},{5,4},{6,7},{7,6},{8,9},{9,8},{10,11... | collective-permute-start | bytes 983048 | tf_op jit(solution)/shard_map/ppermute | solution.py:584
  27.4 1.9 %collective-permute-start.4 = (bf16[848,128]{1,0:T(8,128)(2,1)S(1)}, bf16[848,128]{1,0:T(8,128)(2,1)S(1)}, u32[]{:S(2)}, u32[]{:S(2)}) collective-permute-start(bf16[848,128]{1,0:T(8,128)(2,1)S(1)} %get-tuple-element.30), channel_id=1, source_target_pairs={{0,1},{1,0},{2,3},{3,2},{4,5},{5,4},{6,7},{7,6},{8,9},{9,8},{10,11... | collective-permute-start | bytes 651272 | tf_op jit(solution)/shard_map/ppermute | solution.py:584
